TPU v7x, 32 devices: a whole 2x2x4 slice. The times are simulated.
32 devices in a mesh: space: 8 (over z, x), member: 4 (over y, core).
Axes of the slice: x: 2, y: 2, z: 4, core: 2. Of those that a mesh axis runs over, the one named last changes fastest.
Arguments:
- prediction_maps: bfloat16 [4, 72, 16, 1440], P('member', None, 'space'), may hold values from -6 to 6
- truth_analysis: float32 [72, 23040], P(None, ('space', 'member')), may hold values from -6 to 6
- reciprocal_spread: float32 [72], replicated, may hold values from 0.3 to 3
- deconv_inputs: bfloat16 [4, 72, 16, 1440], P('member', None, 'space'), may hold values from -6 to 6
- filter_tensor: bfloat16 [5, 5, 72, 72], replicated, may hold values from -0.125 to 0.125
Outputs:
- grad_hidden: bfloat16 [4, 72, 16, 1440], P('member', None, 'space')
- grad_kernel: float32 [5, 5, 72, 72], replicated
All inputs are finite; a program needn't handle non-finite values.
Results may differ from a plain program's by a relative error of at most 0.018.
Values may be sent and summed in bfloat16 or wider, within the bound.
No kernel may reach another device: no remote copies, remote signals or barrier semaphores. Data moves between devices by JAX's collectives and lax.ppermute only.
A program may use at most 64 MiB of HBM per device.

v0:
```python
import jax
import jax.numpy as jnp
from jax import lax
from jax.sharding import PartitionSpec as P

smoothing = 1.0


def extended(x, sides, width):
    for axis, dim in sides:
        size, length = (lax.axis_size(axis), x.shape[dim])
        up = [(i, (i + 1) % size) for i in range(size - 1)]
        down = [(j, i) for i, j in up]
        last = lax.slice_in_dim(x, length - width, length, axis=dim)
        first = lax.slice_in_dim(x, 0, width, axis=dim)
        before = lax.ppermute(last, axis, up)
        after = lax.ppermute(first, axis, down)
        x = jnp.concatenate([before, x, after], axis=dim)
    return x


def area_weights(rows_total):
    index = jnp.arange(rows_total, dtype=jnp.float32)
    latitude = (index + 0.5) * (jnp.pi / rows_total) - jnp.pi / 2
    cosine = jnp.cos(latitude)
    return cosine / jnp.mean(cosine)


def direct_term(own, target, scale):
    offset = scale * (own - target[None])
    radius = jnp.sqrt(jnp.sum(offset * offset, axis=1, keepdims=True) + smoothing)
    return scale * offset / radius


def pair_sums(scaled_own, scaled_other):
    own_sq = jnp.sum(scaled_own * scaled_own, axis=1)
    other_sq = jnp.sum(scaled_other * scaled_other, axis=1)
    inner = jnp.einsum("mcp,ncp->mnp", scaled_own, scaled_other, precision=lax.Precision.HIGHEST)
    spread_sq = own_sq[:, None, :] + other_sq[None, :, :] - 2.0 * inner + smoothing
    inverse = 1.0 / jnp.sqrt(spread_sq)
    total_weight = jnp.sum(inverse, axis=1)
    mixture = jnp.einsum("mnp,ncp->mcp", inverse, scaled_other, precision=lax.Precision.HIGHEST)
    return (total_weight, mixture)


def body(prediction_maps, truth_analysis, reciprocal_spread, deconv_inputs, filter_tensor):
    quantity_indices = prediction_maps.shape[1]
    parallel_section = prediction_maps.shape[2]
    meridian_extent = prediction_maps.shape[3]
    ksize = filter_tensor.shape[0]
    members = lax.axis_size("member")
    rows_total = parallel_section * lax.axis_size("space")
    pixel_count = parallel_section * meridian_extent
    weights = lax.dynamic_slice_in_dim(
        area_weights(rows_total), lax.axis_index("space") * parallel_section, parallel_section
    )
    scale = reciprocal_spread[None, :, None]
    prediction_vector = prediction_maps.reshape(1, quantity_indices, pixel_count)
    whole_obs = lax.all_gather(truth_analysis, "member", axis=1, tiled=True)
    own = prediction_vector.astype(jnp.float32)
    direct = direct_term(own, whole_obs, scale)
    scaled_own = scale * own
    piece = lax.all_gather(prediction_maps, "member", axis=0, tiled=True)
    other = scale * piece.astype(jnp.float32).reshape(piece.shape[0], quantity_indices, pixel_count)
    weight_part, mix_part = pair_sums(scaled_own, other)
    paired = scale * (scaled_own * weight_part[:, None, :] - mix_part)
    terms = (direct - paired / members).reshape(quantity_indices, parallel_section, meridian_extent)
    grad_out = (terms * weights[None, :, None]).astype(jnp.bfloat16)
    padded = extended(grad_out, (("space", 1),), 2)
    wrapped = jnp.concatenate([padded[:, :, -2:], padded, padded[:, :, :2]], axis=2)
    flat_hidden = deconv_inputs[0].reshape(quantity_indices, pixel_count)
    back = jnp.zeros((quantity_indices, pixel_count), jnp.float32)
    pieces = []
    for row_shift in range(ksize):
        band = wrapped[:, row_shift : row_shift + parallel_section, :]
        stacked = jnp.stack(
            [band[:, :, col_shift : col_shift + meridian_extent] for col_shift in range(ksize)]
        ).reshape(ksize * quantity_indices, pixel_count)
        row_filter = jnp.transpose(filter_tensor[row_shift], (1, 0, 2)).reshape(
            quantity_indices, ksize * quantity_indices
        )
        back = back + jnp.dot(row_filter, stacked, preferred_element_type=jnp.float32)
        product = lax.dot_general(
            flat_hidden, stacked, (((1,), (1,)), ((), ())), preferred_element_type=jnp.float32
        )
        pieces.append(
            jnp.transpose(product.reshape(quantity_indices, ksize, quantity_indices), (1, 0, 2))
        )
    partial_sum = jnp.stack(pieces)
    grad_hidden = back.astype(jnp.bfloat16).reshape(
        1, quantity_indices, parallel_section, meridian_extent
    )
    kernel_total = lax.psum(partial_sum, ("space", "member"))
    norm_factor = 1.0 / jnp.sqrt(jnp.float32(members * rows_total * meridian_extent))
    return (grad_hidden, kernel_total * norm_factor)


def solution(mesh):
    return jax.shard_map(
        body,
        mesh=mesh,
        in_specs=(
            P("member", None, "space", None),
            P(None, ("space", "member")),
            P(),
            P("member", None, "space", None),
            P(),
        ),
        out_specs=(P("member", None, "space", None), P()),
        check_vma=False,
    )
```

profile of v0, /device:TPU:0, one launch (start us, length us, event | category | flops | bytes accessed | tf_op | source)
XLA Modules:
  0.0 303.7 jit_solution(18112935933690532214)
XLA Ops:
  7.2 1.9 copy.52
  9.2 1.3 reshape.255
  10.8 10.8 %all-gather = f32[4,720,72]{1,2,0:T(8,128)S(1)} all-gather(f32[1,720,72]{1,2,0:T(8,128)S(1)} %bitcast.231), channel_id=1, replica_groups=mesh['space'=8,'member'=4] {'member'}, dimensions={0}, use_global_device_ids=true | all-gather | bytes 1036800 | tf_op jit(solution)/shard_map/all_gather | solution.py:59
  21.9 0.6 reshape.258
  22.5 0.8 fusion.35
  24.3 1.2 multiply_reduce_fusion.4
  25.4 8.2 %all-gather.3.cloned.1.call-done = bf16[4,72,2,1440]{3,1,2,0:T(8,128)(2,1)} async-done(((bf16[1,72,2,1440]{3,1,2,0:T(8,128)(2,1)}), bf16[4,72,2,1440]{3,1,2,0:T(8,128)(2,1)}) %all-gather.3.cloned.1.call-update) | async-done | bytes 1658896 | tf_op jit(solution)/shard_map/all_gather | solution.py:63
  33.6 4.6 %copy.53 = f32[4,72,2,1440]{3,2,1,0:T(2,128)} copy(bf16[4,72,2,1440]{3,1,2,0:T(8,128)(2,1)} %all-gather.3.cloned.1.call-done) | data formatting | bytes 4976640 | tf_op jit(solution)/shard_map/convert_element_type | solution.py:64
  38.2 4.7 %reshape.235 = f32[4,72,2880]{2,1,0:T(8,128)S(1)} reshape(f32[4,72,2,1440]{3,2,1,0:T(2,128)} %copy.53) | data formatting | bytes 6635520 | tf_op jit(solution)/shard_map/reshape | solution.py:64
  42.9 2.1 multiply_reduce_fusion
  45.2 1.6 multiply_reduce_fusion.2
  47.4 0.6 copy-done.5
  48.9 0.9 reshape.237
  50.3 3.4 %collective-permute-start = (bf16[72,2,1440]{2,1,0:T(2,128)(2,1)S(1)}, bf16[72,2,1440]{2,1,0:T(2,128)(2,1)S(1)}, u32[]{:S(2)}, u32[]{:S(2)}) collective-permute-start(bf16[72,2,1440]{2,1,0:T(2,128)(2,1)S(1)} %multiply_convert_fusion.1), channel_id=1, source_target_pairs={{0,4},{4,8},{8,12},{12,16},{16,20},{20,24},{24,28},{1,5},{5,9},{9,... | collective-permute-start | bytes 1244168 | tf_op jit(solution)/shard_map/ppermute | solution.py:16
  53.7 1.5 collective-permute-start.1
  55.6 0.7 copy.54
  56.3 0.8 copy.55
  57.1 0.7 copy.56
  57.8 0.7 copy.57
  58.5 0.7 copy.58
  59.3 0.9 reshape.242
  60.2 12.7 %collective-permute-done = bf16[72,2,1440]{2,1,0:T(2,128)(2,1)S(1)} collective-permute-done((bf16[72,2,1440]{2,1,0:T(2,128)(2,1)S(1)}, bf16[72,2,1440]{2,1,0:T(2,128)(2,1)S(1)}, u32[]{:S(2)}, u32[]{:S(2)}) %collective-permute-start) | collective-permute-done | bytes 414752 | tf_op jit(solution)/shard_map/ppermute | solution.py:16
  72.9 7.4 %fusion.2 = (bf16[72,6,1442]{2,1,0:T(8,128)(2,1)S(1)}, bf16[72,6,1442]{2,1,0:T(8,128)(2,1)S(1)}) fusion(bf16[72,2,1440]{2,1,0:T(2,128)(2,1)} %collective-permute-done.1, bf16[72,2,1440]{2,1,0:T(2,128)(2,1)S(1)} %multiply_convert_fusion.1, bf16[72,2,1440]{2,1,0:T(2,128)(2,1)S(1)} %collective-permute-done), kind=kLoop, calls=%fused_computation.10 | loop fusion | flops 14950656 | bytes 3735936 | tf_op jit(solution)/shard_map/concatenate | solution.py:70
  80.3 1.6 fusion.12
  82.0 5.2 %fusion.11 = (bf16[5,72,2,1440]{3,2,1,0:T(2,128)(2,1)S(1)}, bf16[5,72,2,1440]{3,2,1,0:T(2,128)(2,1)S(1)}, bf16[5,72,2,1440]{3,2,1,0:T(2,128)(2,1)S(1)}, bf16[5,7...) fusion(bf16[5,72,2,1440]{3,2,1,0:T(2,128)(2,1)S(1)} %get-tuple-element.25, ...), kind=kLoop, calls=%fused_computation.38 | loop fusion | bytes 4423680
  87.6 3.8 %bitcast_dynamic-update-slice_fusion = (bf16[5,72,2,1440]{3,2,1,0:T(2,128)(2,1)S(1)}, bf16[5,72,2,1440]{3,2,1,0:T(2,128)(2,1)S(1)}, bf16[5,72,2,1440]{3,2,1,0:T(2,128)(2,1)S(1)}, bf16[5,72,2,1440]{3,2,1,0:T(2,128)(2,1)S(1)}) fusion(bf16[5,72,2,1440]{3,2,1,0:T(2,128)(2,1)S(1)} %get-tuple-element.20, bf16[72,2,1440]{2,1,0:T(2,128)(2,1)} %collective-permute-done.1, ...), kind=kLoop, calls=%fused_computation.79 | loop fusion | flops 1658880 | bytes 3068928
  91.3 5.2 %fusion.10 = (bf16[5,72,2,1440]{3,2,1,0:T(2,128)(2,1)S(1)}, bf16[5,72,2,1440]{3,2,1,0:T(2,128)(2,1)S(1)}, bf16[5,72,2,1440]{3,2,1,0:T(2,128)(2,1)S(1)}, bf16[5,7...) fusion(bf16[5,72,2,1440]{3,2,1,0:T(2,128)(2,1)S(1)} %get-tuple-element.39, ...), kind=kLoop, calls=%fused_computation.36 | loop fusion | bytes 4423680
  96.5 5.4 %fusion.9 = (bf16[5,72,2,1440]{3,2,1,0:T(2,128)(2,1)S(1)}, bf16[5,72,2,1440]{3,2,1,0:T(2,128)(2,1)S(1)}, bf16[5,72,2,1440]{3,2,1,0:T(2,128)(2,1)S(1)}, bf16[5,72...) fusion(bf16[5,72,2,1440]{3,2,1,0:T(2,128)(2,1)S(1)} %get-tuple-element.15, ...), kind=kLoop, calls=%fused_computation.34 | loop fusion | bytes 4423680 | tf_op jit(solution)/shard_map/stack | solution.py:76
  101.9 1.4 copy-done.11
  103.2 1.4 copy-done.12
  104.6 1.4 copy-done.13
  106.0 1.4 copy-done.14
  107.5 1.4 copy-done.15
  108.8 5.4 %reshape.238 = bf16[360,2880]{1,0:T(8,128)(2,1)S(1)} reshape(bf16[5,72,2,1440]{3,2,1,0:T(2,128)(2,1)} %copy-done.15) | data formatting | bytes 4147200 | tf_op jit(solution)/shard_map/reshape | solution.py:78
  114.2 0.8 convolution_bitcast_fusion.4
  115.0 0.8 copy.59
  115.8 0.9 constant_dynamic-update-slice_fusion.4
  116.7 6.3 %reshape.240 = bf16[360,2880]{1,0:T(8,128)(2,1)} reshape(bf16[5,72,2,1440]{3,2,1,0:T(2,128)(2,1)} %copy-done.14) | data formatting | bytes 4147200 | tf_op jit(solution)/shard_map/reshape | solution.py:78
  123.0 3.0 convolution_bitcast_fusion.3
  126.0 1.7 copy.60
  127.7 6.3 %reshape.243 = bf16[360,2880]{1,0:T(8,128)(2,1)} reshape(bf16[5,72,2,1440]{3,2,1,0:T(2,128)(2,1)} %copy-done.13) | data formatting | bytes 4147200 | tf_op jit(solution)/shard_map/reshape | solution.py:78
  134.0 3.0 convolution_bitcast_fusion.2
  137.0 1.7 copy.61
  138.7 6.2 %reshape.245 = bf16[360,2880]{1,0:T(8,128)(2,1)} reshape(bf16[5,72,2,1440]{3,2,1,0:T(2,128)(2,1)} %copy-done.12) | data formatting | bytes 4147200 | tf_op jit(solution)/shard_map/reshape | solution.py:78
  144.9 3.0 convolution_bitcast_fusion.1
  148.0 1.7 copy.62
  149.7 6.2 %reshape.247 = bf16[360,2880]{1,0:T(8,128)(2,1)} reshape(bf16[5,72,2,1440]{3,2,1,0:T(2,128)(2,1)} %copy-done.11) | data formatting | bytes 4147200 | tf_op jit(solution)/shard_map/reshape | solution.py:78
  155.9 3.0 convolution_bitcast_fusion
  158.9 1.0 copy.63
  160.0 0.9 constant_dynamic-update-slice_fusion.3
  160.9 0.9 constant_dynamic-update-slice_fusion.2
  161.9 0.9 constant_dynamic-update-slice_fusion.1
  162.8 0.9 copy-done.16
  163.8 0.5 fusion.38
  164.4 1.0 copy-done
  165.4 0.5 convolution_add_fusion.3
  166.2 0.5 convolution_add_fusion.2
  166.7 0.9 copy-done.2
  167.6 0.5 convolution_add_fusion.1
  168.5 0.5 fusion.1
  169.0 1.3 reshape.249
  170.3 124.0 %all-reduce.2.cloned.1.call-done = f32[5,5,72,72]{2,3,1,0:T(8,128)} async-done(((f32[5,5,72,72]{2,3,1,0:T(8,128)}), f32[5,5,72,72]{2,3,1,0:T(8,128)}) %all-reduce.2.cloned.1.call-update) | async-done | bytes 518416 | tf_op jit(solution)/shard_map/psum | solution.py:93
  294.3 1.3 broadcast_multiply_fusion
  295.6 1.2 copy.64
  (63 shorter events, 4.3 us)
Async XLA Ops:
  7.2 3.3 %copy-start.10 = (bf16[1,72,2,1440]{3,2,1,0:T(2,128)(2,1)S(1)}, bf16[1,72,2,1440]{3,2,1,0:T(2,128)(2,1)}, u32[]{:S(2)}) copy-start(bf16[1,72,2,1440]{3,2,1,0:T(2,128)(2,1)} %param.5) | copy-start | bytes 1244164
  7.2 3.6 %copy-start.24 = (f32[72,720]{1,0:T(8,128)S(1)}, f32[72,720]{1,0:T(8,128)}, u32[]{:S(2)}) copy-start(f32[72,720]{1,0:T(8,128)} %param.6) | copy-start | bytes 622084
  7.2 26.4 %all-gather.3.cloned.1.call-start = ((), (), s32[]{:S(2)}) async-start(), calls=%async_computation | async-start | bytes 2211840 | tf_op jit(solution)/shard_map/all_gather | solution.py:63
  9.1 285.2 %all-reduce.2.cloned.1.call-start = ((), (), s32[]{:S(2)}) async-start(), calls=%async_computation.1 | async-start | bytes 1843200 | tf_op jit(solution)/shard_map/psum | solution.py:93
  10.5 13.8 %copy-start.6 = (f32[72,2880]{1,0:T(8,128)}, f32[72,2880]{1,0:T(8,128)S(1)}, u32[]{:S(2)}) copy-start(f32[72,2880]{1,0:T(8,128)S(1)} %reshape.255) | copy-start | bytes 2488324
  10.8 13.3 %copy-start.4 = (f32[1,72,2880]{2,1,0:T(8,128)}, f32[1,72,2880]{2,1,0:T(8,128)S(1)}, u32[]{:S(2)}) copy-start(f32[1,72,2880]{2,1,0:T(8,128)S(1)} %reshape.256) | copy-start | bytes 2488324
  10.8 13.3 %copy-start.25 = (f32[72]{0:T(128)S(1)}, f32[72]{0:T(128)}, u32[]{:S(2)}) copy-start(f32[72]{0:T(128)} %param.7) | copy-start | bytes 868
  22.5 11.1 %copy-start.8 = (f32[2880,72]{0,1:T(8,128)}, f32[2880,72]{0,1:T(8,128)S(1)}, u32[]{:S(2)}) copy-start(f32[2880,72]{0,1:T(8,128)S(1)} %reshape.258) | copy-start | bytes 2488324
  46.9 1.2 copy-start.5
  46.9 1.4 copy-start.7
  46.9 1.6 copy-start.9
  48.9 6.2 %copy-start.18 = (bf16[1,72,2,1440]{3,2,1,0:T(2,128)(2,1)S(1)}, bf16[1,72,2,1440]{3,2,1,0:T(2,128)(2,1)}, u32[]{:S(2)}) copy-start(bf16[1,72,2,1440]{3,2,1,0:T(2,128)(2,1)} %param.8) | copy-start | bytes 1244164
  48.9 6.6 %copy-start.17 = (bf16[5,5,72,72]{3,2,1,0:T(8,128)(2,1)S(1)}, bf16[5,5,72,72]{3,2,1,0:T(8,128)(2,1)}, u32[]{:S(2)}) copy-start(bf16[5,5,72,72]{3,2,1,0:T(8,128)(2,1)} %param.9) | copy-start | bytes 777604
  50.3 22.7 %collective-permute-start = (bf16[72,2,1440]{2,1,0:T(2,128)(2,1)S(1)}, bf16[72,2,1440]{2,1,0:T(2,128)(2,1)S(1)}, u32[]{:S(2)}, u32[]{:S(2)}) collective-permute-start(bf16[72,2,1440]{2,1,0:T(2,128)(2,1)S(1)} %multiply_convert_fusion.1), channel_id=1, source_target_pairs={{0,4},{4,8},{8,12},{12,16},{16,20},{20,24},{24,28},{1,5},{5,9},{9,... | collective-permute-start | bytes 1244168 | tf_op jit(solution)/shard_map/ppermute | solution.py:16
  53.7 19.3 %collective-permute-start.1 = (bf16[72,2,1440]{2,1,0:T(2,128)(2,1)S(1)}, bf16[72,2,1440]{2,1,0:T(2,128)(2,1)}, u32[]{:S(2)}, u32[]{:S(2)}) collective-permute-start(bf16[72,2,1440]{2,1,0:T(2,128)(2,1)S(1)} %multiply_convert_fusion.1), channel_id=1, source_target_pairs={{4,0},{8,4},{12,8},{16,12},{20,16},{24,20},{28,24},{5,1},{9,5},{13... | collective-permute-start | bytes 1244168 | tf_op jit(solution)/shard_map/ppermute | solution.py:17
  101.9 1.4 copy-start.11
  103.2 1.4 copy-start.12
  104.6 1.4 copy-start.13
  106.0 1.4 copy-start.14
  107.5 1.4 copy-start.15
  158.9 4.9 %copy-start.23 = (bf16[72,5,72]{0,2,1:T(8,128)(2,1)S(1)}, bf16[72,5,72]{0,2,1:T(8,128)(2,1)}, u32[]{:S(2)}) copy-start(bf16[72,5,72]{0,2,1:T(8,128)(2,1)} %copy.54) | copy-start | bytes 155524
  162.8 1.6 copy-start.22
  162.8 0.9 copy-start.16
  163.8 1.6 copy-start
  164.4 1.8 copy-start.1
  164.4 1.8 copy-start.21
  165.9 1.7 copy-start.2
  165.9 1.7 copy-start.20
  166.7 1.8 copy-start.3
  166.7 1.8 copy-start.19
Sparse Core Ops, SparseCore 0:
  10.1 23.4 all-gather.2
  163.9 130.3 all-reduce.1
where the time goes:
time: 305 us; the launch traced here: 304 us
  waiting for transfers between devices  145 us (48%)
  local copies, waits for them, and re-layouts  92.3 us (30%)
  other arithmetic  20 us (7%)
  matrix products  15.6 us (5%)
  between operations  15.2 us (5%)
  blocking collectives  10.8 us (4%)
  starting transfers between devices  4.95 us (2%)
    psum x1, waiting for transfers between devices, body(): kernel_total = lax.psum(partial_sum, ('space', 'member'))  124 us
    unnamed x62, local copies, waits for them, and re-layouts  30.9 us
    reshape x5, local copies, waits for them, and re-layouts, body(): stacked = jnp.stack([band[:, :, col_shift:col_shift + meridian_extent] fo...  30.4 us
    dot_general x5, matrix products, body(): lax.dot_general(flat_hidden, stacked, (((1,), (1,)), ((), ())), preferred...  12.9 us
    ppermute x1, waiting for transfers between devices, extended(): before = lax.ppermute(last, axis, up)  12.7 us
    all_gather x1, blocking collectives, body(): whole_obs = lax.all_gather(truth_analysis, 'member', axis=1, tiled=True)  10.8 us
    all_gather x1, waiting for transfers between devices, body(): piece = lax.all_gather(prediction_maps, 'member', axis=0, tiled=True)  8.17 us
    concatenate x1, other arithmetic, body(): jnp.concatenate([padded[:, :, -2:], padded, padded[:, :, :2]], axis=2)  7.37 us
  transfers between devices with their start and end apart: 4, of which 3 were waited for; matrix products, arithmetic and copies ran while one was open for 5% of the time, Pallas kernels for 0%

commit v1 on v0

v1 whole, which is shorter than its diff:
```python
import functools

import jax
import jax.numpy as jnp
from jax import lax
from jax.experimental import pallas as pl
from jax.experimental.pallas import tpu as pltpu
from jax.sharding import Mesh, PartitionSpec as P

smoothing = 1.0
LANES = 128
BF = jnp.bfloat16
F32 = jnp.float32
VM = pl.BlockSpec(memory_space=pltpu.VMEM)
SM = pl.BlockSpec(memory_space=pltpu.SMEM)


def up(n, k):
    return -(-n // k) * k


def area_weights(rows_total):
    index = jnp.arange(rows_total, dtype=F32)
    latitude = (index + 0.5) * (jnp.pi / rows_total) - jnp.pi / 2
    cosine = jnp.cos(latitude)
    return cosine / jnp.mean(cosine)


def call(kernel, outs, ins, scratch=(), flops=0):
    nbytes = sum(x.size * x.dtype.itemsize for x in (*ins, *outs))
    return pl.pallas_call(
        kernel,
        out_shape=list(outs),
        in_specs=[SM if x.dtype == jnp.int32 else VM for x in ins],
        out_specs=[VM for _ in outs],
        scratch_shapes=list(scratch),
        cost_estimate=pl.CostEstimate(
            flops=flops, bytes_accessed=nbytes, transcendentals=0
        ),
        compiler_params=pltpu.CompilerParams(vmem_limit_bytes=40 << 20),
    )(*ins)


def lane_iota(shape):
    return lax.broadcasted_iota(jnp.int32, shape, len(shape) - 1)


def rows_kernel(width, half, x_ref, o_ref):
    rows = x_ref.shape[2]
    for r in range(rows):
        x = x_ref[0, :, r, :]
        o_ref[2 * r] = x[:, :half]
        tail = x[:, half:]
        o_ref[2 * r + 1] = jnp.concatenate(
            [tail, jnp.zeros((x.shape[0], 2 * half - width), x.dtype)], axis=1
        )


def fields_kernel(width, half, x_ref, t_ref, o_ref):
    rows_kernel(width, half, x_ref, o_ref)
    rows = x_ref.shape[2]
    t = t_ref[...].astype(o_ref.dtype)
    pieces = up(t.shape[1], half) // half
    for k in range(pieces):
        part = t[:, k * half : (k + 1) * half]
        if part.shape[1] < half:
            part = jnp.concatenate(
                [part, jnp.zeros((part.shape[0], half - part.shape[1]), part.dtype)],
                axis=1,
            )
        o_ref[2 * rows + k] = part


def energy_kernel(width, half, span, members, me_ref, w_ref, s_ref, *refs):
    others = refs[:members]
    o_ref, t_scr = refs[members:]
    rows = o_ref.shape[0]
    channels = o_ref.shape[1]
    parts = members // rows
    me = me_ref[0]
    for d in range(members):
        t_scr[me ^ d] = others[d][2 * rows][:, : t_scr.shape[2]]
    s = s_ref[...]
    for r in range(rows):
        truth = None
        for k in range(parts):
            piece = t_scr[r * parts + k].astype(F32)
            piece = jnp.concatenate(
                [piece, jnp.zeros((channels, 2 * half - piece.shape[1]), F32)], axis=1
            )
            if k:
                piece = pltpu.roll(piece, k * span, 1)
            truth = piece if truth is None else truth + piece
        weight = w_ref[r : r + 1, 0:1]
        for h in range(2):
            t = truth[:, h * half : (h + 1) * half]
            own = others[0][2 * r + h].astype(F32)
            scaled = s * own
            offset = scaled - s * t
            radius_sq = jnp.sum(offset * offset, axis=0, keepdims=True) + smoothing
            direct = offset * lax.rsqrt(radius_sq)
            self_inverse = 1.0 / jnp.sqrt(smoothing)
            total = self_inverse
            mixture = scaled * self_inverse
            for d in range(1, members):
                other = s * others[d][2 * r + h].astype(F32)
                diff = scaled - other
                spread_sq = jnp.sum(diff * diff, axis=0, keepdims=True) + smoothing
                inverse = lax.rsqrt(spread_sq)
                total = total + inverse
                mixture = mixture + other * inverse
            paired = scaled * total - mixture
            g = (weight * s) * (direct - paired * (1.0 / members))
            o_ref[r, :, h * half : (h + 1) * half] = g.astype(BF)
        last = (width // LANES) * LANES
        body = o_ref[r, :, last : last + LANES].astype(F32)
        head = o_ref[r, :, 0:LANES].astype(F32)
        lane = lane_iota(body.shape)
        off = width - last
        body = jnp.where(lane < off, body, 0.0)
        wrapped = jnp.where(
            (lane >= off) & (lane < off + 2), pltpu.roll(head, off, 1), body
        )
        tail = pltpu.roll(body, LANES - off, 1)
        wrapped = jnp.where(lane >= LANES - 2, tail, wrapped)
        o_ref[r, :, last : last + LANES] = wrapped.astype(BF)


def gather_rows(parity, own, near, far, scr):
    rows = scr.shape[0] // 3
    above, below = 2 * rows * (1 - parity), 2 * rows * parity
    for r in range(rows):
        scr[rows + r] = own(r)
        scr[above + r] = near(r)
        scr[below + r] = far(r)


def whole_row(ref):
    def get(r):
        return jnp.concatenate([ref[2 * r], ref[2 * r + 1]], axis=1)

    return get


def kgrad_kernel(ksize, par_ref, g_ref, own_ref, near_ref, far_ref, o_ref, h_scr, acc):
    rows, channels, lanes = g_ref.shape
    mid = ksize // 2
    gather_rows(
        par_ref[0], whole_row(own_ref), whole_row(near_ref), whole_row(far_ref), h_scr
    )
    total = None
    for r in range(rows):
        g = g_ref[r].astype(F32)
        shifted = jnp.concatenate(
            [
                (g if b == mid else pltpu.roll(g, (mid - b) % lanes, 1)).astype(BF)
                for b in range(ksize)
            ],
            axis=0,
        )
        h = h_scr[r : r + ksize].reshape(ksize * channels, lanes)
        part = lax.dot_general(
            h, shifted, (((1,), (1,)), ((), ())), preferred_element_type=F32
        )
        total = part if total is None else total + part
    n = ksize * channels
    o_ref[...] = jnp.zeros_like(o_ref)
    o_ref[:n, :n] = total.astype(o_ref.dtype)


def conv_kernel(ksize, width, par_ref, w_ref, own_ref, near_ref, far_ref, o_ref, g_scr):
    rows, channels, lanes = own_ref.shape
    mid = ksize // 2
    gather_rows(
        par_ref[0],
        lambda r: own_ref[r],
        lambda r: near_ref[r],
        lambda r: far_ref[r],
        g_scr,
    )
    w = w_ref[...]
    for r in range(rows):
        g = g_scr[r : r + ksize].reshape(ksize * channels, lanes)
        y = jnp.dot(w, g, preferred_element_type=F32)
        out = None
        for b in range(ksize):
            part = y[b * channels : (b + 1) * channels]
            if b != mid:
                part = pltpu.roll(part, (mid - b) % lanes, 1)
            out = part if out is None else out + part
        o_ref[r] = out[:, :width].astype(o_ref.dtype)


def final_kernel(ksize, channels, norm, x_ref, o_ref):
    for a in range(ksize):
        for b in range(ksize):
            i, j = (ksize - 1 - a) * channels, b * channels
            o_ref[a, b] = (
                x_ref[i : i + channels, j : j + channels].astype(F32) * norm
            )


def flip(x, axis, bit):
    size = lax.axis_size(axis)
    return lax.ppermute(x, axis, [(i, i ^ bit) for i in range(size)])


def along(x):
    size = lax.axis_size("space")
    pairs = [(i, i + 2) for i in range(0, size - 2, 2)]
    pairs += [(i, i - 2) for i in range(3, size, 2)]
    return lax.ppermute(x, "space", pairs)


def bits(axis):
    size, out = lax.axis_size(axis), []
    while (1 << len(out)) < size:
        out.append(1 << len(out))
    return out


def add(a, b):
    return (a.astype(F32) + b.astype(F32)).astype(BF)


def halve(x, axis):
    odd = lax.axis_index(axis) & 1
    n = x.shape[0] // 2
    keep = lax.dynamic_slice_in_dim(x, odd * n, n, 0)
    give = lax.dynamic_slice_in_dim(x, (1 - odd) * n, n, 0)
    return add(keep, flip(give, axis, 1))


def join(x, axis):
    odd = lax.axis_index(axis) & 1
    other = flip(x, axis, 1)
    both = jnp.concatenate([x, other], axis=0)
    swapped = jnp.concatenate([other, x], axis=0)
    return jnp.where(odd == 0, both, swapped)


def reduce_all(x):
    x = halve(x, "core")
    x = halve(x, "chip")
    for bit in bits("chip")[1:]:
        x = add(x, flip(x, "chip", bit))
    for bit in bits("space"):
        x = add(x, flip(x, "space", bit))
    return join(join(x, "chip"), "core")


def body(prediction_maps, truth_analysis, reciprocal_spread, deconv_inputs, filter_tensor):
    channels, rows, width = prediction_maps.shape[1:]
    ksize = filter_tensor.shape[0]
    chips = lax.axis_size("chip")
    members = chips * lax.axis_size("core")
    rows_total = rows * lax.axis_size("space")
    half = up(up(width + 4, LANES), 2 * LANES) // 2
    lanes = 2 * half
    span = truth_analysis.shape[1]
    space = lax.axis_index("space")
    me = lax.axis_index("chip") * 2 + lax.axis_index("core")
    parity = (space % 2).reshape(1)
    sds = jax.ShapeDtypeStruct
    weights = lax.dynamic_slice_in_dim(area_weights(rows_total), space * rows, rows)

    fields = call(
        functools.partial(fields_kernel, width, half),
        [sds((2 * rows + 1, channels, half), BF)],
        [prediction_maps, truth_analysis],
    )[0]
    have = [fields]
    for bit in bits("chip"):
        have += [flip(x, "chip", bit) for x in have]
    pairs = []
    for x in have:
        pairs += [x, flip(x, "core", 1)]

    hidden = call(
        functools.partial(rows_kernel, width, half),
        [sds((2 * rows, channels, half), BF)],
        [deconv_inputs],
    )[0]
    hidden_near = flip(hidden, "space", 1)
    hidden_far = along(hidden_near)
    taps = jnp.transpose(filter_tensor, (1, 2, 0, 3)).reshape(
        ksize * channels, ksize * channels
    )

    grad = call(
        functools.partial(energy_kernel, width, half, span, members),
        [sds((rows, channels, lanes), BF)],
        [
            me.reshape(1),
            jnp.broadcast_to(weights[:, None], (rows, LANES)),
            reciprocal_spread[:, None],
            *pairs,
        ],
        [pltpu.VMEM((members, channels, span), BF)],
    )[0]

    grad_near = flip(grad, "space", 1)
    grad_far = along(grad_near)

    n = ksize * channels
    packed = up(n, LANES)
    partial = call(
        functools.partial(kgrad_kernel, ksize),
        [sds((packed, packed), BF)],
        [parity, grad, hidden, hidden_near, hidden_far],
        [pltpu.VMEM((3 * rows, channels, lanes), BF), pltpu.VMEM((8, LANES), F32)],
        2 * n * n * rows * lanes,
    )[0]
    total = reduce_all(partial)

    back = call(
        functools.partial(conv_kernel, ksize, width),
        [sds((rows, channels, width), BF)],
        [parity, taps, grad, grad_near, grad_far],
        [pltpu.VMEM((3 * rows, channels, lanes), BF)],
        2 * n * n * rows * lanes,
    )[0]
    grad_hidden = jnp.transpose(back, (1, 0, 2))[None]

    norm = 1.0 / float(members * rows_total * width) ** 0.5
    grad_kernel = call(
        functools.partial(final_kernel, ksize, channels, norm),
        [sds((ksize, ksize, channels, channels), F32)],
        [total],
    )[0]
    return (grad_hidden, grad_kernel)


def solution(mesh):
    space, members = mesh.devices.shape
    fine = Mesh(
        mesh.devices.reshape(space, members // 2, 2), ("space", "chip", "core")
    )
    member = ("chip", "core")
    return jax.shard_map(
        body,
        mesh=fine,
        in_specs=(
            P(member, None, "space", None),
            P(None, ("space", *member)),
            P(),
            P(member, None, "space", None),
            P(),
        ),
        out_specs=(P(member, None, "space", None), P()),
        check_vma=False,
    )
```

time: 305 us -> 71.5 us (0.23)
  waiting for transfers between devices: 145 us -> 30.3 us
  local copies, waits for them, and re-layouts: 92.3 us -> 4.51 us
  starting transfers between devices: 4.95 us -> 24.5 us
  other arithmetic: 20 us -> 0.97 us
  matrix products: 15.6 us -> 0 us
  between operations: 15.2 us -> 1.44 us
  blocking collectives: 10.8 us -> 0 us
  Pallas kernels: 0 us -> 8.91 us
    psum x1 -> x0, waiting for transfers between devices: 124 us -> none  [body(): kernel_total = lax.psum(partial_sum, ('space', 'member'))]
    reshape x9 -> x1, local copies, waits for them, and re-layouts: 38.3 us -> 0.37 us  [body(): jnp.transpose(filter_tensor, (1, 2, 0, 3))]
    unnamed x62 -> x11, local copies, waits for them, and re-layouts: 30.9 us -> 3.71 us
    ppermute x2 -> x14, starting transfers between devices: 4.87 us -> 24.5 us  [the longest x12 17.9 us: flip(): return lax.ppermute(x, axis, [(i, i ^ bit) for i in range(size)])]
    ppermute x2 -> x14, waiting for transfers between devices: 12.7 us -> 30.3 us  [the longest x12 21.9 us: flip(): return lax.ppermute(x, axis, [(i, i ^ bit) for i in range(size)])]
    dot_general x10 -> x0, matrix products: 15.6 us -> none  [the longest x5 12.9 us: body(): lax.dot_general(flat_hidden, stacked, (((1,), (1,)), ((), ())), preferred...]
    all_gather x1 -> x0, blocking collectives: 10.8 us -> none  [body(): whole_obs = lax.all_gather(truth_analysis, 'member', axis=1, tiled=True)]
    pallas_call x0 -> x6, Pallas kernels: none -> 8.91 us  [call(): pl.pallas_call(kernel, out_shape=list(outs), in_specs=[SM if x.dtype == j...]
  transfers between devices with their start and end apart: 4 -> 14, of which waited for: 3 -> 11; matrix products, arithmetic and copies ran while one was open for 5% -> 2% of each run, Pallas kernels for 0% -> 5%
where the time goes in v1:
time: 71.5 us; the launch traced here: 70.7 us
  waiting for transfers between devices  30.3 us (42%)
  starting transfers between devices  24.5 us (34%)
  Pallas kernels  8.91 us (12%)
  local copies, waits for them, and re-layouts  4.51 us (6%)
  between operations  1.44 us (2%)
  other arithmetic  0.97 us (1%)
    ppermute x12, waiting for transfers between devices, flip(): return lax.ppermute(x, axis, [(i, i ^ bit) for i in range(size)])  21.9 us
    ppermute x12, starting transfers between devices, flip(): return lax.ppermute(x, axis, [(i, i ^ bit) for i in range(size)])  17.9 us
    pallas_call x6, Pallas kernels, call(): pl.pallas_call(kernel, out_shape=list(outs), in_specs=[SM if x.dtype == j...  8.91 us
    ppermute x2, waiting for transfers between devices, along(): return lax.ppermute(x, 'space', pairs)  8.38 us
    ppermute x2, starting transfers between devices, along(): return lax.ppermute(x, 'space', pairs)  6.65 us
    unnamed x11, local copies, waits for them, and re-layouts  3.71 us
  transfers between devices with their start and end apart: 14, of which 11 were waited for; matrix products, arithmetic and copies ran while one was open for 2% of the time, Pallas kernels for 5%

profile of v1, /device:TPU:0, one launch (start us, length us, event | category | flops | bytes accessed | tf_op | source)
XLA Modules:
  0.0 70.7 jit_solution(5551299817726498929)
XLA Ops:
  0.6 0.0 copy-start
  0.6 1.0 %copy-done = bf16[1,72,2,1440]{3,2,1,0:T(2,128)(2,1)S(1)} copy-done((bf16[1,72,2,1440]{3,2,1,0:T(2,128)(2,1)S(1)}, bf16[1,72,2,1440]{3,2,1,0:T(2,128)(2,1)}, u32[]{:S(2)}) %copy-start) | copy-done | bytes 414744
  1.6 0.0 copy-start.2
  1.6 0.9 %copy-done.2 = f32[72,720]{1,0:T(8,128)S(1)} copy-done((f32[72,720]{1,0:T(8,128)S(1)}, f32[72,720]{1,0:T(8,128)}, u32[]{:S(2)}) %copy-start.2) | copy-done | bytes 207384
  2.6 0.0 copy-start.1
  2.6 1.0 %shard_map.68.refs_0_ = bf16[5,72,768]{2,1,0:T(8,128)(2,1)S(1)} custom-call(bf16[1,72,2,1440]{3,2,1,0:T(2,128)(2,1)S(1)} %copy-done, f32[72,720]{1,0:T(8,128)S(1)} %copy-done.2), custom_call_target="tpu_custom_call" | custom-call | bytes 1175040 | tf_op jit(solution)/shard_map/pallas_call | solution.py:31
  3.6 3.1 %collective-permute-start.1 = (bf16[5,72,768]{2,1,0:T(8,128)(2,1)S(1)}, bf16[5,72,768]{2,1,0:T(8,128)(2,1)S(1)}, u32[]{:S(2)}, u32[]{:S(2)}) collective-permute-start(bf16[5,72,768]{2,1,0:T(8,128)(2,1)S(1)} %shard_map.68.refs_0_), channel_id=1, source_target_pairs={{0,2},{2,0},{1,3},{3,1},{4,6},{6,4},{5,7},{7,5},{8,10},{10,8},{9,1... | collective-permute-start | bytes 1658888 | tf_op jit(solution)/shard_map/ppermute | solution.py:205
  6.7 0.0 copy-done.1
  6.7 1.0 %shard_map.71.own_ref = bf16[4,72,768]{2,1,0:T(8,128)(2,1)S(1)} custom-call(bf16[1,72,2,1440]{3,2,1,0:T(2,128)(2,1)S(1)} %copy-done.1), custom_call_target="tpu_custom_call" | custom-call | bytes 857088 | tf_op jit(solution)/shard_map/pallas_call | solution.py:31
  7.7 1.6 %collective-permute-start.5 = (bf16[4,72,768]{2,1,0:T(8,128)(2,1)S(1)}, bf16[4,72,768]{2,1,0:T(8,128)(2,1)}, u32[]{:S(2)}, u32[]{:S(2)}) collective-permute-start(bf16[4,72,768]{2,1,0:T(8,128)(2,1)S(1)} %shard_map.71.own_ref), channel_id=1, source_target_pairs={{0,4},{4,0},{8,12},{12,8},{16,20},{20,16},{24,28},{28,24},{1,5},{5... | collective-permute-start | bytes 1327112 | tf_op jit(solution)/shard_map/ppermute | solution.py:205
  9.3 0.0 collective-permute-start
  9.3 9.9 %collective-permute-done.1.refs_2_ = bf16[5,72,768]{2,1,0:T(8,128)(2,1)S(1)} collective-permute-done((bf16[5,72,768]{2,1,0:T(8,128)(2,1)S(1)}, bf16[5,72,768]{2,1,0:T(8,128)(2,1)S(1)}, u32[]{:S(2)}, u32[]{:S(2)}) %collective-permute-start.1) | collective-permute-done | bytes 552992 | tf_op jit(solution)/shard_map/ppermute | solution.py:205
  19.2 0.0 collective-permute-start.2
  19.2 0.3 collective-permute-done.5.near_ref
  19.5 4.2 %collective-permute-start.6 = (bf16[4,72,768]{2,1,0:T(8,128)(2,1)}, bf16[4,72,768]{2,1,0:T(8,128)(2,1)}, u32[]{:S(2)}, u32[]{:S(2)}) collective-permute-start(bf16[4,72,768]{2,1,0:T(8,128)(2,1)} %collective-permute-done.5.near_ref), channel_id=1, source_target_pairs={{0,8},{8,16},{16,24},{12,4},{20,12},{28,20},{1,9},{9,17},{17,25},{... | collective-permute-start | bytes 1327112 | tf_op jit(solution)/shard_map/ppermute | solution.py:212
  23.8 0.0 copy-start.4
  23.8 0.7 copy-done.4
  24.4 0.1 copy.11.s_ref
  24.5 0.7 fusion
  25.9 0.1 dynamic_slice.15
  26.0 0.0 collective-permute-done.refs_1_
  26.0 0.0 collective-permute-done.2.refs_3_
  26.0 0.1 broadcast_in_dim.12.w_ref
  26.0 1.4 %shard_map.69.own_ref.g_ref = bf16[2,72,1536]{2,1,0:T(8,128)(2,1)S(1)} custom-call(s32[1]{0:T(128)} %bitcast.2.me_ref, f32[2,128]{1,0:T(2,128)S(1)} %broadcast_in_dim.12.w_ref, f32[72,1]{1,0:T(8,128)S(1)} %copy.11.s_ref, bf16[5,72,768]{2,1,0:T(8,128)(2,1)S(1)} %shard_map.68.refs_0_, bf16[5,72,768]{2,1,0:T(8,128)(2,1)S(1)} %collective-permute-done.refs_1_, ...), custom_call_target="tpu_custom_call" | custom-call | bytes 2655524 | tf_op jit(solution)/shard_map/pallas_call | solution.py:31
  27.5 5.9 %collective-permute-done.6.far_ref = bf16[4,72,768]{2,1,0:T(8,128)(2,1)} collective-permute-done((bf16[4,72,768]{2,1,0:T(8,128)(2,1)}, bf16[4,72,768]{2,1,0:T(8,128)(2,1)}, u32[]{:S(2)}, u32[]{:S(2)}) %collective-permute-start.6) | collective-permute-done | bytes 442400 | tf_op jit(solution)/shard_map/ppermute | solution.py:212
  33.3 2.6 %shard_map.72 = bf16[384,384]{1,0:T(8,128)(2,1)S(1)} custom-call(s32[1]{0:T(128)} %bitcast.par_ref, bf16[2,72,1536]{2,1,0:T(8,128)(2,1)S(1)} %shard_map.69.own_ref.g_ref, bf16[4,72,768]{2,1,0:T(8,128)(2,1)S(1)} %shard_map.71.own_ref, bf16[4,72,768]{2,1,0:T(8,128)(2,1)} %collective-permute-done.5.near_ref, bf16[4,72,768]{2,1,0:T(8,128)(2,1)} %collective-permute-done.6.far_ref), custom_call_target="tpu_custom_call" | custom-call | flops 796262400 | bytes 2064388 | tf_op jit(solution)/shard_map/pallas_call | solution.py:31
  36.0 0.1 collective-permute-start.7
  36.0 1.3 %collective-permute-done.7 = bf16[192,384]{1,0:T(8,128)(2,1)S(1)} collective-permute-done((bf16[192,384]{1,0:T(8,128)(2,1)S(1)}, bf16[192,384]{1,0:T(8,128)(2,1)S(1)}, u32[]{:S(2)}, u32[]{:S(2)}) %collective-permute-start.7) | collective-permute-done | bytes 147488 | tf_op jit(solution)/shard_map/ppermute | solution.py:205
  37.5 1.6 %collective-permute-start.8 = (bf16[96,384]{1,0:T(8,128)(2,1)S(1)}, bf16[96,384]{1,0:T(8,128)(2,1)S(1)}, u32[]{:S(2)}, u32[]{:S(2)}) collective-permute-start(bf16[96,384]{1,0:T(8,128)(2,1)S(1)} %constant_dynamic-slice_fusion), channel_id=1, source_target_pairs={{0,2},{2,0},{1,3},{3,1},{4,6},{6,4},{5,7},{7,5},{8,10},{10,8},{9,1... | collective-permute-start | bytes 221192 | tf_op jit(solution)/shard_map/ppermute | solution.py:205
  39.1 2.8 %collective-permute-done.8 = bf16[96,384]{1,0:T(8,128)(2,1)S(1)} collective-permute-done((bf16[96,384]{1,0:T(8,128)(2,1)S(1)}, bf16[96,384]{1,0:T(8,128)(2,1)S(1)}, u32[]{:S(2)}, u32[]{:S(2)}) %collective-permute-start.8) | collective-permute-done | bytes 73760 | tf_op jit(solution)/shard_map/ppermute | solution.py:205
  41.9 0.0 copy-start.3
  41.9 2.5 %collective-permute-start.9 = (bf16[96,384]{1,0:T(8,128)(2,1)S(1)}, bf16[96,384]{1,0:T(8,128)(2,1)S(1)}, u32[]{:S(2)}, u32[]{:S(2)}) collective-permute-start(bf16[96,384]{1,0:T(8,128)(2,1)S(1)} %add_convert_fusion.4), channel_id=1, source_target_pairs={{0,4},{4,0},{8,12},{12,8},{16,20},{20,16},{24,28},{28,24},{1,5},{5... | collective-permute-start | bytes 221192 | tf_op jit(solution)/shard_map/ppermute | solution.py:205
  44.4 2.3 %collective-permute-done.9 = bf16[96,384]{1,0:T(8,128)(2,1)S(1)} collective-permute-done((bf16[96,384]{1,0:T(8,128)(2,1)S(1)}, bf16[96,384]{1,0:T(8,128)(2,1)S(1)}, u32[]{:S(2)}, u32[]{:S(2)}) %collective-permute-start.9) | collective-permute-done | bytes 73760 | tf_op jit(solution)/shard_map/ppermute | solution.py:205
  46.7 2.2 %collective-permute-start.10 = (bf16[96,384]{1,0:T(8,128)(2,1)S(1)}, bf16[96,384]{1,0:T(8,128)(2,1)S(1)}, u32[]{:S(2)}, u32[]{:S(2)}) collective-permute-start(bf16[96,384]{1,0:T(8,128)(2,1)S(1)} %add_convert_fusion.3), channel_id=1, source_target_pairs={{0,8},{4,12},{8,0},{12,4},{16,24},{20,28},{24,16},{28,20},{1,9},{5... | collective-permute-start | bytes 221192 | tf_op jit(solution)/shard_map/ppermute | solution.py:205
  48.9 1.5 %collective-permute-start.3 = (bf16[2,72,1536]{2,1,0:T(8,128)(2,1)S(1)}, bf16[2,72,1536]{2,1,0:T(8,128)(2,1)S(1)}, u32[]{:S(2)}, u32[]{:S(2)}) collective-permute-start(bf16[2,72,1536]{2,1,0:T(8,128)(2,1)S(1)} %shard_map.69.own_ref.g_ref), channel_id=1, source_target_pairs={{0,4},{4,0},{8,12},{12,8},{16,20},{20,16},{24,28},{28,24},{1,5},{5... | collective-permute-start | bytes 1327112 | tf_op jit(solution)/shard_map/ppermute | solution.py:205
  50.4 0.8 %collective-permute-done.10 = bf16[96,384]{1,0:T(8,128)(2,1)S(1)} collective-permute-done((bf16[96,384]{1,0:T(8,128)(2,1)S(1)}, bf16[96,384]{1,0:T(8,128)(2,1)S(1)}, u32[]{:S(2)}, u32[]{:S(2)}) %collective-permute-start.10) | collective-permute-done | bytes 73760 | tf_op jit(solution)/shard_map/ppermute | solution.py:205
  51.3 3.8 %collective-permute-start.11 = (bf16[96,384]{1,0:T(8,128)(2,1)S(1)}, bf16[96,384]{1,0:T(8,128)(2,1)S(1)}, u32[]{:S(2)}, u32[]{:S(2)}) collective-permute-start(bf16[96,384]{1,0:T(8,128)(2,1)S(1)} %add_convert_fusion.2), channel_id=1, source_target_pairs={{0,16},{4,20},{8,24},{12,28},{16,0},{20,4},{24,8},{28,12},{1,17},{... | collective-permute-start | bytes 221192 | tf_op jit(solution)/shard_map/ppermute | solution.py:205
  55.1 3.1 %collective-permute-done.11 = bf16[96,384]{1,0:T(8,128)(2,1)S(1)} collective-permute-done((bf16[96,384]{1,0:T(8,128)(2,1)S(1)}, bf16[96,384]{1,0:T(8,128)(2,1)S(1)}, u32[]{:S(2)}, u32[]{:S(2)}) %collective-permute-start.11) | collective-permute-done | bytes 73760 | tf_op jit(solution)/shard_map/ppermute | solution.py:205
  58.3 1.6 %collective-permute-start.12 = (bf16[96,384]{1,0:T(8,128)(2,1)S(1)}, bf16[96,384]{1,0:T(8,128)(2,1)S(1)}, u32[]{:S(2)}, u32[]{:S(2)}) collective-permute-start(bf16[96,384]{1,0:T(8,128)(2,1)S(1)} %add_convert_fusion.1), channel_id=1, source_target_pairs={{0,2},{2,0},{1,3},{3,1},{4,6},{6,4},{5,7},{7,5},{8,10},{10,8},{9,1... | collective-permute-start | bytes 221192 | tf_op jit(solution)/shard_map/ppermute | solution.py:205
  59.8 0.0 collective-permute-done.3.near_ref
  59.8 2.4 %collective-permute-start.4 = (bf16[2,72,1536]{2,1,0:T(8,128)(2,1)S(1)}, bf16[2,72,1536]{2,1,0:T(8,128)(2,1)S(1)}, u32[]{:S(2)}, u32[]{:S(2)}) collective-permute-start(bf16[2,72,1536]{2,1,0:T(8,128)(2,1)S(1)} %collective-permute-done.3.near_ref), channel_id=1, source_target_pairs={{0,8},{8,16},{16,24},{12,4},{20,12},{28,20},{1,9},{9,17},{17,25},{... | collective-permute-start | bytes 1327112 | tf_op jit(solution)/shard_map/ppermute | solution.py:212
  62.3 0.4 collective-permute-done.12
  62.7 0.1 collective-permute-start.13
  62.8 0.0 copy-done.3
  62.8 0.1 copy.10
  62.9 0.4 reshape.15.w_ref
  63.3 0.8 %collective-permute-done.13 = bf16[192,384]{1,0:T(8,128)(2,1)S(1)} collective-permute-done((bf16[192,384]{1,0:T(8,128)(2,1)S(1)}, bf16[192,384]{1,0:T(8,128)(2,1)S(1)}, u32[]{:S(2)}, u32[]{:S(2)}) %collective-permute-start.13) | collective-permute-done | bytes 147488 | tf_op jit(solution)/shard_map/ppermute | solution.py:205
  64.1 0.1 maximum_select_fusion.x_ref
  64.2 1.3 %shard_map.73 = f32[5,5,72,72]{3,2,1,0:T(8,128)} custom-call(bf16[384,384]{1,0:T(8,128)(2,1)S(1)} %maximum_select_fusion.x_ref), custom_call_target="tpu_custom_call" | custom-call | bytes 813312 | tf_op jit(solution)/shard_map/pallas_call | solution.py:31
  65.5 2.5 %collective-permute-done.4.far_ref = bf16[2,72,1536]{2,1,0:T(8,128)(2,1)S(1)} collective-permute-done((bf16[2,72,1536]{2,1,0:T(8,128)(2,1)S(1)}, bf16[2,72,1536]{2,1,0:T(8,128)(2,1)S(1)}, u32[]{:S(2)}, u32[]{:S(2)}) %collective-permute-start.4) | collective-permute-done | bytes 442400 | tf_op jit(solution)/shard_map/ppermute | solution.py:212
  68.0 1.6 %shard_map.70 = bf16[2,72,1440]{2,1,0:T(8,128)(2,1)S(1)} custom-call(s32[1]{0:T(128)} %bitcast.par_ref, bf16[360,360]{1,0:T(8,128)(2,1)S(1)} %reshape.15.w_ref, bf16[2,72,1536]{2,1,0:T(8,128)(2,1)S(1)} %shard_map.69.own_ref.g_ref, bf16[2,72,1536]{2,1,0:T(8,128)(2,1)S(1)} %collective-permute-done.3.near_ref, ...), custom_call_target="tpu_custom_call" | custom-call | flops 796262400 | bytes 2001028 | tf_op jit(solution)/shard_map/pallas_call | solution.py:31
  69.6 1.1 %copy.12 = bf16[1,72,2,1440]{3,2,1,0:T(2,128)(2,1)} copy(bf16[1,72,2,1440]{3,1,2,0:T(8,128)(2,1)S(1)} %bitcast.7) | data formatting | bytes 829440
  (9 shorter events, 0.3 us)
Async XLA Ops:
  0.6 1.0 %copy-start = (bf16[1,72,2,1440]{3,2,1,0:T(2,128)(2,1)S(1)}, bf16[1,72,2,1440]{3,2,1,0:T(2,128)(2,1)}, u32[]{:S(2)}) copy-start(bf16[1,72,2,1440]{3,2,1,0:T(2,128)(2,1)} %x_ref.2) | copy-start | bytes 1244164
  1.6 0.9 %copy-start.2 = (f32[72,720]{1,0:T(8,128)S(1)}, f32[72,720]{1,0:T(8,128)}, u32[]{:S(2)}) copy-start(f32[72,720]{1,0:T(8,128)} %t_ref.1) | copy-start | bytes 622084
  2.6 4.1 %copy-start.1 = (bf16[1,72,2,1440]{3,2,1,0:T(2,128)(2,1)S(1)}, bf16[1,72,2,1440]{3,2,1,0:T(2,128)(2,1)}, u32[]{:S(2)}) copy-start(bf16[1,72,2,1440]{3,2,1,0:T(2,128)(2,1)} %x_ref.3) | copy-start | bytes 1244164
  3.6 15.6 %collective-permute-start.1 = (bf16[5,72,768]{2,1,0:T(8,128)(2,1)S(1)}, bf16[5,72,768]{2,1,0:T(8,128)(2,1)S(1)}, u32[]{:S(2)}, u32[]{:S(2)}) collective-permute-start(bf16[5,72,768]{2,1,0:T(8,128)(2,1)S(1)} %shard_map.68.refs_0_), channel_id=1, source_target_pairs={{0,2},{2,0},{1,3},{3,1},{4,6},{6,4},{5,7},{7,5},{8,10},{10,8},{9,1... | collective-permute-start | bytes 1658888 | tf_op jit(solution)/shard_map/ppermute | solution.py:205
  7.7 11.8 %collective-permute-start.5 = (bf16[4,72,768]{2,1,0:T(8,128)(2,1)S(1)}, bf16[4,72,768]{2,1,0:T(8,128)(2,1)}, u32[]{:S(2)}, u32[]{:S(2)}) collective-permute-start(bf16[4,72,768]{2,1,0:T(8,128)(2,1)S(1)} %shard_map.71.own_ref), channel_id=1, source_target_pairs={{0,4},{4,0},{8,12},{12,8},{16,20},{20,16},{24,28},{28,24},{1,5},{5... | collective-permute-start | bytes 1327112 | tf_op jit(solution)/shard_map/ppermute | solution.py:205
  9.3 16.7 %collective-permute-start = (bf16[5,72,768]{2,1,0:T(8,128)(2,1)S(1)}, bf16[5,72,768]{2,1,0:T(8,128)(2,1)S(1)}, u32[]{:S(2)}, u32[]{:S(2)}) collective-permute-start(bf16[5,72,768]{2,1,0:T(8,128)(2,1)S(1)} %shard_map.68.refs_0_), channel_id=1, source_target_pairs={{0,1},{1,0},{2,3},{3,2},{4,5},{5,4},{6,7},{7,6},{8,9},{9,8},{10,11... | collective-permute-start | bytes 1658888 | tf_op jit(solution)/shard_map/ppermute | solution.py:205
  19.2 6.7 %collective-permute-start.2 = (bf16[5,72,768]{2,1,0:T(8,128)(2,1)S(1)}, bf16[5,72,768]{2,1,0:T(8,128)(2,1)S(1)}, u32[]{:S(2)}, u32[]{:S(2)}) collective-permute-start(bf16[5,72,768]{2,1,0:T(8,128)(2,1)S(1)} %collective-permute-done.1.refs_2_), channel_id=1, source_target_pairs={{0,1},{1,0},{2,3},{3,2},{4,5},{5,4},{6,7},{7,6},{8,9},{9,8},{10,11... | collective-permute-start | bytes 1658888 | tf_op jit(solution)/shard_map/ppermute | solution.py:205
  19.5 13.8 %collective-permute-start.6 = (bf16[4,72,768]{2,1,0:T(8,128)(2,1)}, bf16[4,72,768]{2,1,0:T(8,128)(2,1)}, u32[]{:S(2)}, u32[]{:S(2)}) collective-permute-start(bf16[4,72,768]{2,1,0:T(8,128)(2,1)} %collective-permute-done.5.near_ref), channel_id=1, source_target_pairs={{0,8},{8,16},{16,24},{12,4},{20,12},{28,20},{1,9},{9,17},{17,25},{... | collective-permute-start | bytes 1327112 | tf_op jit(solution)/shard_map/ppermute | solution.py:212
  23.8 0.7 copy-start.4
  36.0 1.4 %collective-permute-start.7 = (bf16[192,384]{1,0:T(8,128)(2,1)S(1)}, bf16[192,384]{1,0:T(8,128)(2,1)S(1)}, u32[]{:S(2)}, u32[]{:S(2)}) collective-permute-start(bf16[192,384]{1,0:T(8,128)(2,1)S(1)} %constant_dynamic-slice_fusion.1), channel_id=1, source_target_pairs={{0,1},{1,0},{2,3},{3,2},{4,5},{5,4},{6,7},{7,6},{8,9},{9,8},{10,11... | collective-permute-start | bytes 442376 | tf_op jit(solution)/shard_map/ppermute | solution.py:205
  37.5 4.4 %collective-permute-start.8 = (bf16[96,384]{1,0:T(8,128)(2,1)S(1)}, bf16[96,384]{1,0:T(8,128)(2,1)S(1)}, u32[]{:S(2)}, u32[]{:S(2)}) collective-permute-start(bf16[96,384]{1,0:T(8,128)(2,1)S(1)} %constant_dynamic-slice_fusion), channel_id=1, source_target_pairs={{0,2},{2,0},{1,3},{3,1},{4,6},{6,4},{5,7},{7,5},{8,10},{10,8},{9,1... | collective-permute-start | bytes 221192 | tf_op jit(solution)/shard_map/ppermute | solution.py:205
  41.9 20.9 %copy-start.3 = (bf16[5,5,72,72]{3,2,1,0:T(8,128)(2,1)S(1)}, bf16[5,5,72,72]{3,2,1,0:T(8,128)(2,1)}, u32[]{:S(2)}) copy-start(bf16[5,5,72,72]{3,2,1,0:T(8,128)(2,1)} %param.9) | copy-start | bytes 777604
  41.9 4.8 %collective-permute-start.9 = (bf16[96,384]{1,0:T(8,128)(2,1)S(1)}, bf16[96,384]{1,0:T(8,128)(2,1)S(1)}, u32[]{:S(2)}, u32[]{:S(2)}) collective-permute-start(bf16[96,384]{1,0:T(8,128)(2,1)S(1)} %add_convert_fusion.4), channel_id=1, source_target_pairs={{0,4},{4,0},{8,12},{12,8},{16,20},{20,16},{24,28},{28,24},{1,5},{5... | collective-permute-start | bytes 221192 | tf_op jit(solution)/shard_map/ppermute | solution.py:205
  46.7 4.5 %collective-permute-start.10 = (bf16[96,384]{1,0:T(8,128)(2,1)S(1)}, bf16[96,384]{1,0:T(8,128)(2,1)S(1)}, u32[]{:S(2)}, u32[]{:S(2)}) collective-permute-start(bf16[96,384]{1,0:T(8,128)(2,1)S(1)} %add_convert_fusion.3), channel_id=1, source_target_pairs={{0,8},{4,12},{8,0},{12,4},{16,24},{20,28},{24,16},{28,20},{1,9},{5... | collective-permute-start | bytes 221192 | tf_op jit(solution)/shard_map/ppermute | solution.py:205
  48.9 10.9 %collective-permute-start.3 = (bf16[2,72,1536]{2,1,0:T(8,128)(2,1)S(1)}, bf16[2,72,1536]{2,1,0:T(8,128)(2,1)S(1)}, u32[]{:S(2)}, u32[]{:S(2)}) collective-permute-start(bf16[2,72,1536]{2,1,0:T(8,128)(2,1)S(1)} %shard_map.69.own_ref.g_ref), channel_id=1, source_target_pairs={{0,4},{4,0},{8,12},{12,8},{16,20},{20,16},{24,28},{28,24},{1,5},{5... | collective-permute-start | bytes 1327112 | tf_op jit(solution)/shard_map/ppermute | solution.py:205
  51.3 6.9 %collective-permute-start.11 = (bf16[96,384]{1,0:T(8,128)(2,1)S(1)}, bf16[96,384]{1,0:T(8,128)(2,1)S(1)}, u32[]{:S(2)}, u32[]{:S(2)}) collective-permute-start(bf16[96,384]{1,0:T(8,128)(2,1)S(1)} %add_convert_fusion.2), channel_id=1, source_target_pairs={{0,16},{4,20},{8,24},{12,28},{16,0},{20,4},{24,8},{28,12},{1,17},{... | collective-permute-start | bytes 221192 | tf_op jit(solution)/shard_map/ppermute | solution.py:205
  58.3 4.4 %collective-permute-start.12 = (bf16[96,384]{1,0:T(8,128)(2,1)S(1)}, bf16[96,384]{1,0:T(8,128)(2,1)S(1)}, u32[]{:S(2)}, u32[]{:S(2)}) collective-permute-start(bf16[96,384]{1,0:T(8,128)(2,1)S(1)} %add_convert_fusion.1), channel_id=1, source_target_pairs={{0,2},{2,0},{1,3},{3,1},{4,6},{6,4},{5,7},{7,5},{8,10},{10,8},{9,1... | collective-permute-start | bytes 221192 | tf_op jit(solution)/shard_map/ppermute | solution.py:205
  59.8 8.2 %collective-permute-start.4 = (bf16[2,72,1536]{2,1,0:T(8,128)(2,1)S(1)}, bf16[2,72,1536]{2,1,0:T(8,128)(2,1)S(1)}, u32[]{:S(2)}, u32[]{:S(2)}) collective-permute-start(bf16[2,72,1536]{2,1,0:T(8,128)(2,1)S(1)} %collective-permute-done.3.near_ref), channel_id=1, source_target_pairs={{0,8},{8,16},{16,24},{12,4},{20,12},{28,20},{1,9},{9,17},{17,25},{... | collective-permute-start | bytes 1327112 | tf_op jit(solution)/shard_map/ppermute | solution.py:212
  62.7 1.4 %collective-permute-start.13 = (bf16[192,384]{1,0:T(8,128)(2,1)S(1)}, bf16[192,384]{1,0:T(8,128)(2,1)S(1)}, u32[]{:S(2)}, u32[]{:S(2)}) collective-permute-start(bf16[192,384]{1,0:T(8,128)(2,1)S(1)} %maximum_select_fusion.1), channel_id=1, source_target_pairs={{0,1},{1,0},{2,3},{3,2},{4,5},{5,4},{6,7},{7,6},{8,9},{9,8},{10,11... | collective-permute-start | bytes 442376 | tf_op jit(solution)/shard_map/ppermute | solution.py:205

commit v2 on v1

v2 whole, which is shorter than its diff:
```python
import functools

import jax
import jax.numpy as jnp
import numpy as np
from jax import lax
from jax.experimental import pallas as pl
from jax.experimental.pallas import tpu as pltpu
from jax.sharding import Mesh, PartitionSpec as P


smoothing = 1.0
LANES = 128
BF = jnp.bfloat16
F32 = jnp.float32
VM = pl.BlockSpec(memory_space=pltpu.VMEM)
ANY = pl.BlockSpec(memory_space=pl.ANY)


def up(n, k):
    return -(-n // k) * k


def area_weights(rows_total):
    index = np.arange(rows_total)
    latitude = (index + 0.5) * (np.pi / rows_total) - np.pi / 2
    cosine = np.cos(latitude)
    return cosine / np.mean(cosine)


def call(kernel, outs, ins, scratch=(), flops=0, anywhere=()):
    nbytes = sum(x.size * x.dtype.itemsize for x in (*ins, *outs))
    return pl.pallas_call(
        kernel,
        out_shape=list(outs),
        in_specs=[ANY if i in anywhere else VM for i in range(len(ins))],
        out_specs=[VM for _ in outs],
        scratch_shapes=list(scratch),
        cost_estimate=pl.CostEstimate(
            flops=flops, bytes_accessed=nbytes, transcendentals=0
        ),
        compiler_params=pltpu.CompilerParams(vmem_limit_bytes=16 << 20),
    )(*ins)


def lane_iota(shape):
    return lax.broadcasted_iota(jnp.int32, shape, len(shape) - 1)


def mixed(ref):
    x = ref[0]
    return x.reshape(x.shape[0] * x.shape[1], x.shape[2])


def scale_kernel(rows, s_ref, o_ref):
    n, c = o_ref.shape[0], s_ref.shape[1]
    i = lax.broadcasted_iota(jnp.int32, (n, c), 0)
    j = lax.broadcasted_iota(jnp.int32, (n, c), 1)
    s = jnp.where(i // rows == j, jnp.broadcast_to(s_ref[...], (n, c)), 0.0)
    s = jnp.sum(s, axis=1, keepdims=True)
    o_ref[...] = jnp.broadcast_to(s * s, o_ref.shape)


def pick(table, index):
    out = jnp.float32(table[0])
    for i, v in enumerate(table[1:], 1):
        out = jnp.where(index == i, jnp.float32(v), out)
    return out


def energy_kernel(span, members, weights, s_ref, *refs):
    fields, truths = refs[:members], refs[members : 2 * members]
    o_ref, part_scr, mix_scr, truth, grad, sem = refs[2 * members :]
    rows, channels, lanes = o_ref.shape
    width = fields[0].shape[3]
    mix = channels * rows
    parts = members // rows
    me = lax.axis_index("chip") * 2 + lax.axis_index("core")
    first = lax.axis_index("space") * rows
    copies = [
        pltpu.make_async_copy(truths[d], part_scr.at[me ^ d], sem.at[d])
        for d in range(members)
    ]
    for copy in copies:
        copy.start()
    for d in range(members):
        mix_scr[d] = mixed(fields[d])
    for copy in copies:
        copy.wait()
    i = lax.broadcasted_iota(jnp.int32, (mix, channels), 0)
    j = lax.broadcasted_iota(jnp.int32, (mix, channels), 1)
    place = [(i == j * rows + r).astype(BF) for r in range(rows)]
    for k in range(parts):
        truth[:, k * span : (k + 1) * span] = sum(
            jnp.dot(place[r], part_scr[r * parts + k], preferred_element_type=F32)
            for r in range(rows)
        )

    def sums(x):
        x = jnp.sum(x, axis=0)
        step = rows
        while step < 8:
            x = x + pltpu.roll(x, step, 0)
            step *= 2
        return x

    def load(d, low, high):
        x = mix_scr[d, :, low:high].astype(F32)
        return x.reshape(mix // 8, 8, high - low)

    sub = lax.broadcasted_iota(jnp.int32, (8, LANES), 0) % rows
    weight = pick(weights, first)
    pattern = jnp.full((8, LANES), weight, F32)
    for r in range(1, rows):
        pattern = jnp.where(sub == r, pick(weights, first + r), pattern)
    grad[width // LANES] = jnp.zeros((mix, LANES), F32)
    for low in range(0, width, LANES):
        high = min(low + LANES, width)
        n = high - low
        sq = s_ref[:, :n].reshape(mix // 8, 8, n)
        own = load(0, low, high)
        offset = own - truth[:, low:high].reshape(mix // 8, 8, n)
        direct = lax.rsqrt(sums(offset * offset * sq) + smoothing)
        self_inverse = 1.0 / jnp.sqrt(smoothing)
        total = jnp.full((8, n), self_inverse, F32)
        mixture = own * self_inverse
        for d in range(1, members):
            other = load(d, low, high)
            diff = own - other
            inverse = lax.rsqrt(sums(diff * diff * sq) + smoothing)
            total = total + inverse
            mixture = mixture + other * inverse[None]
        paired = own * total[None] - mixture
        g = offset * direct[None] - paired * (1.0 / members)
        g = g * (sq * pattern[None, :, :n])
        grad[low // LANES, :, :n] = g.reshape(mix, n)
    last = width // LANES
    body, head = grad[last], grad[0]
    lane = lane_iota(body.shape)
    off = width - last * LANES
    wrapped = jnp.where(
        (lane >= off) & (lane < off + 2), pltpu.roll(head, off, 1), body
    )
    tail = pltpu.roll(body, LANES - off, 1)
    grad[last] = jnp.where(lane >= LANES - 2, tail, wrapped)
    for r in range(rows):
        for tile in range(lanes // LANES):
            g = grad[tile, pl.ds(r, channels, stride=rows), :]
            o_ref[r, :, tile * LANES : (tile + 1) * LANES] = g.astype(BF)


def over_lanes(h, shifted):
    rows, n, _ = shifted.shape
    s = shifted[...].reshape(rows * n, shifted.shape[2])[:, : h.shape[1]]
    return lax.dot_general(h, s, (((1,), (1,)), ((), ())), preferred_element_type=F32)


def kgrad_own_kernel(ksize, g_ref, own_ref, shift_ref, o_ref):
    rows, channels, lanes = g_ref.shape
    mid = ksize // 2
    for r in range(rows):
        g = g_ref[r].astype(F32)
        for b in range(ksize):
            moved = g if b == mid else pltpu.roll(g, (mid - b) % lanes, 1)
            shift_ref[r, b * channels : (b + 1) * channels] = moved.astype(BF)
        rest = shift_ref.shape[1] - ksize * channels
        shift_ref[r, ksize * channels :] = jnp.zeros((rest, lanes), BF)
    o_ref[...] = over_lanes(mixed(own_ref), shift_ref)


def kgrad_kernel(ksize, shift_ref, own_ref, near_ref, far_ref, o_ref, acc):
    channels, rows = near_ref.shape[1:3]
    n = shift_ref.shape[1]
    odd = lax.axis_index("space") % 2
    mix = rows * channels
    both = over_lanes(
        jnp.concatenate([mixed(near_ref), mixed(far_ref)], axis=0), shift_ref
    )
    near, far = 2 * (1 - odd), 2 * odd
    for t in range(acc.shape[1]):
        lanes = slice(t * LANES, (t + 1) * LANES)
        acc[1, t] = own_ref[:, lanes]
        acc[near, t] = both[:mix, lanes]
        acc[far, t] = both[mix:, lanes]
    for i in range(ksize):
        for t in range(n // LANES):
            tap = None
            for r in range(rows):
                band, row = divmod(rows - ksize // 2 + r + i, rows)
                part = acc[
                    band, r * (n // LANES) + t, pl.ds(row, channels, stride=rows), :
                ]
                tap = part if tap is None else tap + part
            o_ref[
                i * channels : (i + 1) * channels, t * LANES : (t + 1) * LANES
            ] = tap.astype(o_ref.dtype)
    used = ksize * channels
    o_ref[used:] = jnp.zeros((o_ref.shape[0] - used, n), o_ref.dtype)


def gather_rows(own, near, far, scr):
    rows = scr.shape[0] // 3
    odd = lax.axis_index("space") % 2
    above, below = 2 * rows * (1 - odd), 2 * rows * odd
    for r in range(rows):
        scr[rows + r] = own(r)
        scr[above + r] = near(r)
        scr[below + r] = far(r)


def conv_kernel(ksize, w_ref, own_ref, near_ref, far_ref, o_ref, g_scr):
    rows, channels, lanes = own_ref.shape
    width = o_ref.shape[2]
    mid = ksize // 2
    gather_rows(
        lambda r: own_ref[r], lambda r: near_ref[r], lambda r: far_ref[r], g_scr
    )
    w = w_ref[...]
    for r in range(rows):
        g = g_scr[r : r + ksize].reshape(ksize * channels, lanes)
        y = jnp.dot(w, g, preferred_element_type=F32)
        out = None
        for b in range(ksize):
            part = y[b * channels : (b + 1) * channels]
            if b != mid:
                part = pltpu.roll(part, (mid - b) % lanes, 1)
            out = part if out is None else out + part
        o_ref[r] = out[:, :width].astype(o_ref.dtype)


def final_kernel(ksize, channels, norm, x_ref, o_ref):
    for a in range(ksize):
        for b in range(ksize):
            i, j = (ksize - 1 - a) * channels, b * channels
            o_ref[a, b] = (
                x_ref[i : i + channels, j : j + channels].astype(F32) * norm
            )


def flip(x, axis, bit):
    size = lax.axis_size(axis)
    return lax.ppermute(x, axis, [(i, i ^ bit) for i in range(size)])


def across(x):
    size = lax.axis_size("space")
    pairs = [(i, i + 1) for i in range(1, size - 1, 2)]
    pairs += [(i, i - 1) for i in range(2, size, 2)]
    return lax.ppermute(x, "space", pairs)


def bits(axis):
    size, out = lax.axis_size(axis), []
    while (1 << len(out)) < size:
        out.append(1 << len(out))
    return out


def add(a, b):
    return (a.astype(F32) + b.astype(F32)).astype(BF)


def halve(x, axis):
    odd = lax.axis_index(axis) & 1
    n = x.shape[0] // 2
    keep = lax.dynamic_slice_in_dim(x, odd * n, n, 0)
    give = lax.dynamic_slice_in_dim(x, (1 - odd) * n, n, 0)
    return add(keep, flip(give, axis, 1))


def join(x, axis):
    odd = lax.axis_index(axis) & 1
    other = flip(x, axis, 1)
    both = jnp.concatenate([x, other], axis=0)
    swapped = jnp.concatenate([other, x], axis=0)
    return jnp.where(odd == 0, both, swapped)


def reduce_all(x):
    x = halve(x, "core")
    x = halve(x, "chip")
    for bit in bits("chip")[1:]:
        x = add(x, flip(x, "chip", bit))
    for bit in bits("space")[1:] + [1]:
        x = add(x, flip(x, "space", bit))
    x = join(x, "chip")
    return join(x, "core")


def body(prediction_maps, truth_analysis, reciprocal_spread, deconv_inputs, filter_tensor):
    channels, rows, width = prediction_maps.shape[1:]
    ksize = filter_tensor.shape[0]
    members = lax.axis_size("chip") * lax.axis_size("core")
    rows_total = rows * lax.axis_size("space")
    lanes = up(width + 4, LANES)
    span = truth_analysis.shape[1]
    sds = jax.ShapeDtypeStruct
    slab = sds((rows, channels, lanes), BF)
    scratch = [pltpu.VMEM((3 * rows, channels, lanes), BF)]

    def core(x):
        return flip(x, "core", 1)

    def spread(x):
        have = [x]
        for bit in bits("chip"):
            have += [flip(h, "chip", bit) for h in have]
        return have

    fields = spread(prediction_maps)
    hidden_near = flip(deconv_inputs, "space", 1)
    truth = truth_analysis.astype(BF)
    truths = spread(truth)
    hidden_far = across(deconv_inputs)
    scale = call(
        functools.partial(scale_kernel, rows),
        [sds((rows * channels, LANES), F32)],
        [reciprocal_spread[None]],
    )[0]
    taps = jnp.transpose(filter_tensor, (1, 2, 0, 3)).reshape(
        ksize * channels, ksize * channels
    )
    arrived, seen = [], []
    for x, t in zip(fields, truths):
        arrived += [x, core(x)]
        seen += [t, core(t)]

    table = [float(v) for v in area_weights(rows_total)]
    grad = call(
        functools.partial(energy_kernel, span, members, table),
        [slab],
        [scale, *arrived, *seen],
        [
            pltpu.VMEM((members, channels, span), BF),
            pltpu.VMEM((members, rows * channels, width), BF),
            pltpu.VMEM((rows * channels, lanes), F32),
            pltpu.VMEM((lanes // LANES, rows * channels, LANES), F32),
            pltpu.SemaphoreType.DMA((members,)),
        ],
        anywhere=range(1 + members, 1 + 2 * members),
    )[0]

    grad_near = flip(grad, "space", 1)
    grad_far = across(grad)

    n = ksize * channels
    packed = up(n, LANES)
    flops = 2 * n * n * rows * lanes
    mix = rows * channels
    shifted, own_part = call(
        functools.partial(kgrad_own_kernel, ksize),
        [sds((rows, packed, lanes), BF), sds((mix, rows * packed), F32)],
        [grad, deconv_inputs],
        flops=flops // 3,
    )
    partial = call(
        functools.partial(kgrad_kernel, ksize),
        [sds((packed, packed), BF)],
        [shifted, own_part, hidden_near, hidden_far],
        [pltpu.VMEM((3, rows * packed // LANES, mix, LANES), F32)],
        flops * 2 // 3,
    )[0]
    total = reduce_all(partial)

    back = call(
        functools.partial(conv_kernel, ksize),
        [sds((rows, channels, width), BF)],
        [taps, grad, grad_near, grad_far],
        scratch,
        2 * n * n * rows * lanes,
    )[0]
    grad_hidden = jnp.transpose(back, (1, 0, 2))[None]

    norm = 1.0 / float(members * rows_total * width) ** 0.5
    grad_kernel = call(
        functools.partial(final_kernel, ksize, channels, norm),
        [sds((ksize, ksize, channels, channels), F32)],
        [total],
    )[0]
    return (grad_hidden, grad_kernel)


def solution(mesh):
    space, members = mesh.devices.shape
    fine = Mesh(
        mesh.devices.reshape(space, members // 2, 2), ("space", "chip", "core")
    )
    member = ("chip", "core")

    return jax.shard_map(
        body,
        mesh=fine,
        in_specs=(
            P(member, None, "space", None),
            P(None, ("space", *member)),
            P(),
            P(member, None, "space", None),
            P(),
        ),
        out_specs=(P(member, None, "space", None), P()),
        check_vma=False,
    )
```

time: 71.5 us -> 77.2 us (1.080)
  waiting for transfers between devices: 30.3 us -> 44.9 us
  starting transfers between devices: 24.5 us -> 18.9 us
  Pallas kernels: 8.91 us -> 7.14 us
  local copies, waits for them, and re-layouts: 4.51 us -> 3.34 us
    ppermute x12 -> x15, waiting for transfers between devices: 21.9 us -> 44.9 us  [flip(): return lax.ppermute(x, axis, [(i, i ^ bit) for i in range(size)])]
    ppermute x2, waiting for transfers between devices: 8.38 us -> 0.01 us  [across(): return lax.ppermute(x, 'space', pairs)]
    ppermute x2, starting transfers between devices: 6.65 us -> 1.35 us  [across(): return lax.ppermute(x, 'space', pairs)]
    pallas_call x6, Pallas kernels: 8.91 us -> 7.14 us  [call(): pl.pallas_call(kernel, out_shape=list(outs), in_specs=[ANY if i in anywhe...]
    convert_element_type x0 -> x1, other arithmetic: none -> 0.95 us  [body(): truth = truth_analysis.astype(BF)]
    unnamed x11 -> x9, local copies, waits for them, and re-layouts: 3.71 us -> 2.78 us
    ppermute x12 -> x15, starting transfers between devices: 17.9 us -> 17.6 us  [flip(): return lax.ppermute(x, axis, [(i, i ^ bit) for i in range(size)])]
  transfers between devices with their start and end apart: 14 -> 17, of which waited for: 11 -> 12; matrix products, arithmetic and copies ran while one was open for 2% -> 3% of each run, Pallas kernels for 5% -> 6%
where the time goes in v2:
time: 77.2 us; the launch traced here: 76.3 us
  waiting for transfers between devices  44.9 us (58%)
  starting transfers between devices  18.9 us (24%)
  Pallas kernels  7.14 us (9%)
  local copies, waits for them, and re-layouts  3.34 us (4%)
  other arithmetic  1.2 us (2%)
  between operations  0.82 us (1%)
    ppermute x15, waiting for transfers between devices, flip(): return lax.ppermute(x, axis, [(i, i ^ bit) for i in range(size)])  44.9 us
    ppermute x15, starting transfers between devices, flip(): return lax.ppermute(x, axis, [(i, i ^ bit) for i in range(size)])  17.6 us
    pallas_call x6, Pallas kernels, call(): pl.pallas_call(kernel, out_shape=list(outs), in_specs=[ANY if i in anywhe...  7.14 us
    unnamed x9, local copies, waits for them, and re-layouts  2.78 us
  transfers between devices with their start and end apart: 17, of which 12 were waited for; matrix products, arithmetic and copies ran while one was open for 3% of the time, Pallas kernels for 6%

profile of v2, /device:TPU:0, one launch (start us, length us, event | category | flops | bytes accessed | tf_op | source)
XLA Modules:
  0.0 76.3 jit_solution(9546772006167340835)
XLA Ops:
  0.6 3.1 %collective-permute-start.1 = (bf16[1,72,2,1440]{3,2,1,0:T(2,128)(2,1)}, bf16[1,72,2,1440]{3,2,1,0:T(2,128)(2,1)S(1)}, u32[]{:S(2)}, u32[]{:S(2)}) collective-permute-start(bf16[1,72,2,1440]{3,2,1,0:T(2,128)(2,1)} %refs_0_.1), channel_id=1, source_target_pairs={{0,2},{2,0},{1,3},{3,1},{4,6},{6,4},{5,7},{7,5},{8,10},{10,8},{9,1... | collective-permute-start | bytes 1244168 | tf_op jit(solution)/shard_map/ppermute | solution.py:242
  3.7 0.0 collective-permute-start
  3.7 10.4 %collective-permute-done.1.refs_2_ = bf16[1,72,2,1440]{3,2,1,0:T(2,128)(2,1)S(1)} collective-permute-done((bf16[1,72,2,1440]{3,2,1,0:T(2,128)(2,1)}, bf16[1,72,2,1440]{3,2,1,0:T(2,128)(2,1)S(1)}, u32[]{:S(2)}, u32[]{:S(2)}) %collective-permute-start.1) | collective-permute-done | bytes 414752 | tf_op jit(solution)/shard_map/ppermute | solution.py:242
  14.1 0.0 collective-permute-start.2
  14.1 1.7 %collective-permute-start.8 = (bf16[1,72,2,1440]{3,2,1,0:T(2,128)(2,1)}, bf16[1,72,2,1440]{3,2,1,0:T(2,128)(2,1)S(1)}, u32[]{:S(2)}, u32[]{:S(2)}) collective-permute-start(bf16[1,72,2,1440]{3,2,1,0:T(2,128)(2,1)} %own_ref.1), channel_id=1, source_target_pairs={{0,4},{4,0},{8,12},{12,8},{16,20},{20,16},{24,28},{28,24},{1,5},{5... | collective-permute-start | bytes 1244168 | tf_op jit(solution)/shard_map/ppermute | solution.py:242
  15.8 0.7 collective-permute-start.9
  16.5 0.9 %convert_element_type.48.refs_4_ = bf16[72,720]{1,0:T(8,128)(2,1)S(1)} convert(f32[72,720]{1,0:T(8,128)} %param.6) | non-fusion elementwise | flops 51840 | bytes 311040 | tf_op jit(solution)/shard_map/convert_element_type | solution.py:312
  17.4 1.6 %collective-permute-start.4 = (bf16[72,720]{1,0:T(8,128)(2,1)S(1)}, bf16[72,720]{1,0:T(8,128)(2,1)S(1)}, u32[]{:S(2)}, u32[]{:S(2)}) collective-permute-start(bf16[72,720]{1,0:T(8,128)(2,1)S(1)} %convert_element_type.48.refs_4_), channel_id=1, source_target_pairs={{0,2},{2,0},{1,3},{3,1},{4,6},{6,4},{5,7},{7,5},{8,10},{10,8},{9,1... | collective-permute-start | bytes 311048 | tf_op jit(solution)/shard_map/ppermute | solution.py:242
  19.0 3.7 %collective-permute-done.4.refs_6_ = bf16[72,720]{1,0:T(8,128)(2,1)S(1)} collective-permute-done((bf16[72,720]{1,0:T(8,128)(2,1)S(1)}, bf16[72,720]{1,0:T(8,128)(2,1)S(1)}, u32[]{:S(2)}, u32[]{:S(2)}) %collective-permute-start.4) | collective-permute-done | bytes 103712 | tf_op jit(solution)/shard_map/ppermute | solution.py:242
  22.7 0.0 collective-permute-start.3
  22.7 1.3 %collective-permute-done.3.refs_5_ = bf16[72,720]{1,0:T(8,128)(2,1)S(1)} collective-permute-done((bf16[72,720]{1,0:T(8,128)(2,1)S(1)}, bf16[72,720]{1,0:T(8,128)(2,1)S(1)}, u32[]{:S(2)}, u32[]{:S(2)}) %collective-permute-start.3) | collective-permute-done | bytes 103712 | tf_op jit(solution)/shard_map/ppermute | solution.py:242
  24.0 0.2 collective-permute-start.5
  24.1 0.0 copy-start.1
  24.2 0.7 copy-done.1
  24.8 0.1 shard_map.68.s_ref
  24.9 0.4 collective-permute-done.5.refs_7_
  25.3 0.0 collective-permute-done.refs_1_
  25.3 0.0 collective-permute-done.2.refs_3_
  25.3 0.0 copy-start
  25.3 1.0 %copy-done = bf16[1,72,2,1440]{3,2,1,0:T(2,128)(2,1)S(1)} copy-done((bf16[1,72,2,1440]{3,2,1,0:T(2,128)(2,1)S(1)}, bf16[1,72,2,1440]{3,2,1,0:T(2,128)(2,1)}, u32[]{:S(2)}) %copy-start) | copy-done | bytes 414744
  26.3 0.0 copy-start.2
  26.3 2.1 %shard_map.69.own_ref.g_ref = bf16[2,72,1536]{2,1,0:T(8,128)(2,1)S(1)} custom-call(f32[144,128]{1,0:T(8,128)S(1)} %shard_map.68.s_ref, bf16[1,72,2,1440]{3,2,1,0:T(2,128)(2,1)S(1)} %copy-done, bf16[1,72,2,1440]{3,2,1,0:T(2,128)(2,1)S(1)} %collective-permute-done.refs_1_, bf16[1,72,2,1440]{3,2,1,0:T(2,128)(2,1)S(1)} %collective-permute-done.1.refs_2_, ...), custom_call_target="tpu_custom_call" | custom-call | bytes 2589696 | tf_op jit(solution)/shard_map/pallas_call | solution.py:33
  28.5 0.0 copy-done.2
  28.5 1.1 %shard_map.71 = (bf16[2,384,1536]{2,1,0:T(8,128)(2,1)S(1)}, f32[144,768]{1,0:T(8,128)S(1)}) custom-call(bf16[2,72,1536]{2,1,0:T(8,128)(2,1)S(1)} %shard_map.69.own_ref.g_ref, bf16[1,72,2,1440]{3,2,1,0:T(2,128)(2,1)S(1)} %copy-done.2), custom_call_target="tpu_custom_call" | custom-call | flops 265420800 | bytes 3658752 | tf_op jit(solution)/shard_map/pallas_call | solution.py:33
  29.6 6.1 %collective-permute-done.8.near_ref = bf16[1,72,2,1440]{3,2,1,0:T(2,128)(2,1)S(1)} collective-permute-done((bf16[1,72,2,1440]{3,2,1,0:T(2,128)(2,1)}, bf16[1,72,2,1440]{3,2,1,0:T(2,128)(2,1)S(1)}, u32[]{:S(2)}, u32[]{:S(2)}) %collective-permute-start.8) | collective-permute-done | bytes 414752 | tf_op jit(solution)/shard_map/ppermute | solution.py:242
  35.7 0.0 collective-permute-done.9.far_ref
  35.7 0.0 copy-start.3
  35.7 1.0 %shard_map.72 = bf16[384,384]{1,0:T(8,128)(2,1)S(1)} custom-call(bf16[2,384,1536]{2,1,0:T(8,128)(2,1)S(1)} %get-tuple-element.4.shift_ref, f32[144,768]{1,0:T(8,128)S(1)} %get-tuple-element.5.own_ref, bf16[1,72,2,1440]{3,2,1,0:T(2,128)(2,1)S(1)} %collective-permute-done.8.near_ref, bf16[1,72,2,1440]{3,2,1,0:T(2,128)(2,1)S(1)} %collective-permute-done.9.far_ref), custom_call_target="tpu_custom_call" | custom-call | flops 530841600 | bytes 3926016 | tf_op jit(solution)/shard_map/pallas_call | solution.py:33
  36.7 0.1 collective-permute-start.10
  36.8 1.3 %collective-permute-done.10 = bf16[192,384]{1,0:T(8,128)(2,1)S(1)} collective-permute-done((bf16[192,384]{1,0:T(8,128)(2,1)S(1)}, bf16[192,384]{1,0:T(8,128)(2,1)S(1)}, u32[]{:S(2)}, u32[]{:S(2)}) %collective-permute-start.10) | collective-permute-done | bytes 147488 | tf_op jit(solution)/shard_map/ppermute | solution.py:242
  38.2 1.6 %collective-permute-start.11 = (bf16[96,384]{1,0:T(8,128)(2,1)S(1)}, bf16[96,384]{1,0:T(8,128)(2,1)S(1)}, u32[]{:S(2)}, u32[]{:S(2)}) collective-permute-start(bf16[96,384]{1,0:T(8,128)(2,1)S(1)} %constant_dynamic-slice_fusion), channel_id=1, source_target_pairs={{0,2},{2,0},{1,3},{3,1},{4,6},{6,4},{5,7},{7,5},{8,10},{10,8},{9,1... | collective-permute-start | bytes 221192 | tf_op jit(solution)/shard_map/ppermute | solution.py:242
  39.8 2.8 %collective-permute-done.11 = bf16[96,384]{1,0:T(8,128)(2,1)S(1)} collective-permute-done((bf16[96,384]{1,0:T(8,128)(2,1)S(1)}, bf16[96,384]{1,0:T(8,128)(2,1)S(1)}, u32[]{:S(2)}, u32[]{:S(2)}) %collective-permute-start.11) | collective-permute-done | bytes 73760 | tf_op jit(solution)/shard_map/ppermute | solution.py:242
  42.7 2.5 %collective-permute-start.12 = (bf16[96,384]{1,0:T(8,128)(2,1)S(1)}, bf16[96,384]{1,0:T(8,128)(2,1)S(1)}, u32[]{:S(2)}, u32[]{:S(2)}) collective-permute-start(bf16[96,384]{1,0:T(8,128)(2,1)S(1)} %add_convert_fusion.4), channel_id=1, source_target_pairs={{0,8},{4,12},{8,0},{12,4},{16,24},{20,28},{24,16},{28,20},{1,9},{5... | collective-permute-start | bytes 221192 | tf_op jit(solution)/shard_map/ppermute | solution.py:242
  45.2 2.3 %collective-permute-done.12 = bf16[96,384]{1,0:T(8,128)(2,1)S(1)} collective-permute-done((bf16[96,384]{1,0:T(8,128)(2,1)S(1)}, bf16[96,384]{1,0:T(8,128)(2,1)S(1)}, u32[]{:S(2)}, u32[]{:S(2)}) %collective-permute-start.12) | collective-permute-done | bytes 73760 | tf_op jit(solution)/shard_map/ppermute | solution.py:242
  47.6 3.1 %collective-permute-start.13 = (bf16[96,384]{1,0:T(8,128)(2,1)S(1)}, bf16[96,384]{1,0:T(8,128)(2,1)S(1)}, u32[]{:S(2)}, u32[]{:S(2)}) collective-permute-start(bf16[96,384]{1,0:T(8,128)(2,1)S(1)} %add_convert_fusion.3), channel_id=1, source_target_pairs={{0,16},{4,20},{8,24},{12,28},{16,0},{20,4},{24,8},{28,12},{1,17},{... | collective-permute-start | bytes 221192 | tf_op jit(solution)/shard_map/ppermute | solution.py:242
  50.7 2.3 %collective-permute-done.13 = bf16[96,384]{1,0:T(8,128)(2,1)S(1)} collective-permute-done((bf16[96,384]{1,0:T(8,128)(2,1)S(1)}, bf16[96,384]{1,0:T(8,128)(2,1)S(1)}, u32[]{:S(2)}, u32[]{:S(2)}) %collective-permute-start.13) | collective-permute-done | bytes 73760 | tf_op jit(solution)/shard_map/ppermute | solution.py:242
  53.0 1.9 %collective-permute-start.14 = (bf16[96,384]{1,0:T(8,128)(2,1)S(1)}, bf16[96,384]{1,0:T(8,128)(2,1)S(1)}, u32[]{:S(2)}, u32[]{:S(2)}) collective-permute-start(bf16[96,384]{1,0:T(8,128)(2,1)S(1)} %add_convert_fusion.2), channel_id=1, source_target_pairs={{0,4},{4,0},{8,12},{12,8},{16,20},{20,16},{24,28},{28,24},{1,5},{5... | collective-permute-start | bytes 221192 | tf_op jit(solution)/shard_map/ppermute | solution.py:242
  54.9 0.2 collective-permute-start.6
  55.1 0.7 collective-permute-start.7
  55.8 11.2 %collective-permute-done.14 = bf16[96,384]{1,0:T(8,128)(2,1)S(1)} collective-permute-done((bf16[96,384]{1,0:T(8,128)(2,1)S(1)}, bf16[96,384]{1,0:T(8,128)(2,1)S(1)}, u32[]{:S(2)}, u32[]{:S(2)}) %collective-permute-start.14) | collective-permute-done | bytes 73760 | tf_op jit(solution)/shard_map/ppermute | solution.py:242
  67.1 1.6 %collective-permute-start.15 = (bf16[96,384]{1,0:T(8,128)(2,1)S(1)}, bf16[96,384]{1,0:T(8,128)(2,1)S(1)}, u32[]{:S(2)}, u32[]{:S(2)}) collective-permute-start(bf16[96,384]{1,0:T(8,128)(2,1)S(1)} %add_convert_fusion.1), channel_id=1, source_target_pairs={{0,2},{2,0},{1,3},{3,1},{4,6},{6,4},{5,7},{7,5},{8,10},{10,8},{9,1... | collective-permute-start | bytes 221192 | tf_op jit(solution)/shard_map/ppermute | solution.py:242
  68.6 2.8 %collective-permute-done.15 = bf16[96,384]{1,0:T(8,128)(2,1)S(1)} collective-permute-done((bf16[96,384]{1,0:T(8,128)(2,1)S(1)}, bf16[96,384]{1,0:T(8,128)(2,1)S(1)}, u32[]{:S(2)}, u32[]{:S(2)}) %collective-permute-start.15) | collective-permute-done | bytes 73760 | tf_op jit(solution)/shard_map/ppermute | solution.py:242
  71.5 0.1 collective-permute-start.16
  71.6 0.0 copy-done.3
  71.6 0.1 copy.9
  71.8 0.4 reshape.7.w_ref
  72.1 0.1 collective-permute-done.6.near_ref
  72.3 0.0 collective-permute-done.7.far_ref
  72.3 1.5 %shard_map.70 = bf16[2,72,1440]{2,1,0:T(8,128)(2,1)S(1)} custom-call(bf16[360,360]{1,0:T(8,128)(2,1)S(1)} %reshape.7.w_ref, bf16[2,72,1536]{2,1,0:T(8,128)(2,1)S(1)} %shard_map.69.own_ref.g_ref, bf16[2,72,1536]{2,1,0:T(8,128)(2,1)S(1)} %collective-permute-done.6.near_ref, bf16[2,72,1536]{2,1,0:T(8,128)(2,1)S(1)} %collective-permute-done.7.far_ref), custom_call_target="tpu_custom_call" | custom-call | flops 796262400 | bytes 2001024 | tf_op jit(solution)/shard_map/pallas_call | solution.py:33
  73.8 1.1 %copy.10 = bf16[1,72,2,1440]{3,2,1,0:T(2,128)(2,1)} copy(bf16[1,72,2,1440]{3,1,2,0:T(8,128)(2,1)S(1)} %bitcast.5) | data formatting | bytes 829440
  74.9 0.0 collective-permute-done.16
  74.9 0.1 maximum_select_fusion.x_ref
  75.0 1.3 %shard_map.73 = f32[5,5,72,72]{3,2,1,0:T(8,128)} custom-call(bf16[384,384]{1,0:T(8,128)(2,1)S(1)} %maximum_select_fusion.x_ref), custom_call_target="tpu_custom_call" | custom-call | bytes 813312 | tf_op jit(solution)/shard_map/pallas_call | solution.py:33
  (8 shorter events, 0.2 us)
Async XLA Ops:
  0.6 13.4 %collective-permute-start.1 = (bf16[1,72,2,1440]{3,2,1,0:T(2,128)(2,1)}, bf16[1,72,2,1440]{3,2,1,0:T(2,128)(2,1)S(1)}, u32[]{:S(2)}, u32[]{:S(2)}) collective-permute-start(bf16[1,72,2,1440]{3,2,1,0:T(2,128)(2,1)} %refs_0_.1), channel_id=1, source_target_pairs={{0,2},{2,0},{1,3},{3,1},{4,6},{6,4},{5,7},{7,5},{8,10},{10,8},{9,1... | collective-permute-start | bytes 1244168 | tf_op jit(solution)/shard_map/ppermute | solution.py:242
  3.7 21.6 %collective-permute-start = (bf16[1,72,2,1440]{3,2,1,0:T(2,128)(2,1)}, bf16[1,72,2,1440]{3,2,1,0:T(2,128)(2,1)S(1)}, u32[]{:S(2)}, u32[]{:S(2)}) collective-permute-start(bf16[1,72,2,1440]{3,2,1,0:T(2,128)(2,1)} %refs_0_.1), channel_id=1, source_target_pairs={{0,1},{1,0},{2,3},{3,2},{4,5},{5,4},{6,7},{7,6},{8,9},{9,8},{10,11... | collective-permute-start | bytes 1244168 | tf_op jit(solution)/shard_map/ppermute | solution.py:242
  14.1 11.3 %collective-permute-start.2 = (bf16[1,72,2,1440]{3,2,1,0:T(2,128)(2,1)S(1)}, bf16[1,72,2,1440]{3,2,1,0:T(2,128)(2,1)S(1)}, u32[]{:S(2)}, u32[]{:S(2)}) collective-permute-start(bf16[1,72,2,1440]{3,2,1,0:T(2,128)(2,1)S(1)} %collective-permute-done.1.refs_2_), channel_id=1, source_target_pairs={{0,1},{1,0},{2,3},{3,2},{4,5},{5,4},{6,7},{7,6},{8,9},{9,8},{10,11... | collective-permute-start | bytes 1244168 | tf_op jit(solution)/shard_map/ppermute | solution.py:242
  14.1 21.6 %collective-permute-start.8 = (bf16[1,72,2,1440]{3,2,1,0:T(2,128)(2,1)}, bf16[1,72,2,1440]{3,2,1,0:T(2,128)(2,1)S(1)}, u32[]{:S(2)}, u32[]{:S(2)}) collective-permute-start(bf16[1,72,2,1440]{3,2,1,0:T(2,128)(2,1)} %own_ref.1), channel_id=1, source_target_pairs={{0,4},{4,0},{8,12},{12,8},{16,20},{20,16},{24,28},{28,24},{1,5},{5... | collective-permute-start | bytes 1244168 | tf_op jit(solution)/shard_map/ppermute | solution.py:242
  15.8 19.9 %collective-permute-start.9 = (bf16[1,72,2,1440]{3,2,1,0:T(2,128)(2,1)}, bf16[1,72,2,1440]{3,2,1,0:T(2,128)(2,1)S(1)}, u32[]{:S(2)}, u32[]{:S(2)}) collective-permute-start(bf16[1,72,2,1440]{3,2,1,0:T(2,128)(2,1)} %own_ref.1), channel_id=1, source_target_pairs={{4,8},{12,16},{20,24},{8,4},{16,12},{24,20},{5,9},{13,17},{21,25},... | collective-permute-start | bytes 1244168 | tf_op jit(solution)/shard_map/ppermute | solution.py:249
  17.4 5.3 %collective-permute-start.4 = (bf16[72,720]{1,0:T(8,128)(2,1)S(1)}, bf16[72,720]{1,0:T(8,128)(2,1)S(1)}, u32[]{:S(2)}, u32[]{:S(2)}) collective-permute-start(bf16[72,720]{1,0:T(8,128)(2,1)S(1)} %convert_element_type.48.refs_4_), channel_id=1, source_target_pairs={{0,2},{2,0},{1,3},{3,1},{4,6},{6,4},{5,7},{7,5},{8,10},{10,8},{9,1... | collective-permute-start | bytes 311048 | tf_op jit(solution)/shard_map/ppermute | solution.py:242
  22.7 1.3 %collective-permute-start.3 = (bf16[72,720]{1,0:T(8,128)(2,1)S(1)}, bf16[72,720]{1,0:T(8,128)(2,1)S(1)}, u32[]{:S(2)}, u32[]{:S(2)}) collective-permute-start(bf16[72,720]{1,0:T(8,128)(2,1)S(1)} %convert_element_type.48.refs_4_), channel_id=1, source_target_pairs={{0,1},{1,0},{2,3},{3,2},{4,5},{5,4},{6,7},{7,6},{8,9},{9,8},{10,11... | collective-permute-start | bytes 311048 | tf_op jit(solution)/shard_map/ppermute | solution.py:242
  24.0 1.3 %collective-permute-start.5 = (bf16[72,720]{1,0:T(8,128)(2,1)S(1)}, bf16[72,720]{1,0:T(8,128)(2,1)S(1)}, u32[]{:S(2)}, u32[]{:S(2)}) collective-permute-start(bf16[72,720]{1,0:T(8,128)(2,1)S(1)} %collective-permute-done.4.refs_6_), channel_id=1, source_target_pairs={{0,1},{1,0},{2,3},{3,2},{4,5},{5,4},{6,7},{7,6},{8,9},{9,8},{10,11... | collective-permute-start | bytes 311048 | tf_op jit(solution)/shard_map/ppermute | solution.py:242
  24.1 0.7 copy-start.1
  25.3 1.0 %copy-start = (bf16[1,72,2,1440]{3,2,1,0:T(2,128)(2,1)S(1)}, bf16[1,72,2,1440]{3,2,1,0:T(2,128)(2,1)}, u32[]{:S(2)}) copy-start(bf16[1,72,2,1440]{3,2,1,0:T(2,128)(2,1)} %refs_0_.1) | copy-start | bytes 1244164
  26.3 2.1 %copy-start.2 = (bf16[1,72,2,1440]{3,2,1,0:T(2,128)(2,1)S(1)}, bf16[1,72,2,1440]{3,2,1,0:T(2,128)(2,1)}, u32[]{:S(2)}) copy-start(bf16[1,72,2,1440]{3,2,1,0:T(2,128)(2,1)} %own_ref.1) | copy-start | bytes 1244164
  35.7 35.9 %copy-start.3 = (bf16[5,5,72,72]{3,2,1,0:T(8,128)(2,1)S(1)}, bf16[5,5,72,72]{3,2,1,0:T(8,128)(2,1)}, u32[]{:S(2)}) copy-start(bf16[5,5,72,72]{3,2,1,0:T(8,128)(2,1)} %param.9) | copy-start | bytes 777604
  36.7 1.4 %collective-permute-start.10 = (bf16[192,384]{1,0:T(8,128)(2,1)S(1)}, bf16[192,384]{1,0:T(8,128)(2,1)S(1)}, u32[]{:S(2)}, u32[]{:S(2)}) collective-permute-start(bf16[192,384]{1,0:T(8,128)(2,1)S(1)} %constant_dynamic-slice_fusion.1), channel_id=1, source_target_pairs={{0,1},{1,0},{2,3},{3,2},{4,5},{5,4},{6,7},{7,6},{8,9},{9,8},{10,11... | collective-permute-start | bytes 442376 | tf_op jit(solution)/shard_map/ppermute | solution.py:242
  38.2 4.4 %collective-permute-start.11 = (bf16[96,384]{1,0:T(8,128)(2,1)S(1)}, bf16[96,384]{1,0:T(8,128)(2,1)S(1)}, u32[]{:S(2)}, u32[]{:S(2)}) collective-permute-start(bf16[96,384]{1,0:T(8,128)(2,1)S(1)} %constant_dynamic-slice_fusion), channel_id=1, source_target_pairs={{0,2},{2,0},{1,3},{3,1},{4,6},{6,4},{5,7},{7,5},{8,10},{10,8},{9,1... | collective-permute-start | bytes 221192 | tf_op jit(solution)/shard_map/ppermute | solution.py:242
  42.7 4.9 %collective-permute-start.12 = (bf16[96,384]{1,0:T(8,128)(2,1)S(1)}, bf16[96,384]{1,0:T(8,128)(2,1)S(1)}, u32[]{:S(2)}, u32[]{:S(2)}) collective-permute-start(bf16[96,384]{1,0:T(8,128)(2,1)S(1)} %add_convert_fusion.4), channel_id=1, source_target_pairs={{0,8},{4,12},{8,0},{12,4},{16,24},{20,28},{24,16},{28,20},{1,9},{5... | collective-permute-start | bytes 221192 | tf_op jit(solution)/shard_map/ppermute | solution.py:242
  47.6 5.4 %collective-permute-start.13 = (bf16[96,384]{1,0:T(8,128)(2,1)S(1)}, bf16[96,384]{1,0:T(8,128)(2,1)S(1)}, u32[]{:S(2)}, u32[]{:S(2)}) collective-permute-start(bf16[96,384]{1,0:T(8,128)(2,1)S(1)} %add_convert_fusion.3), channel_id=1, source_target_pairs={{0,16},{4,20},{8,24},{12,28},{16,0},{20,4},{24,8},{28,12},{1,17},{... | collective-permute-start | bytes 221192 | tf_op jit(solution)/shard_map/ppermute | solution.py:242
  53.0 14.0 %collective-permute-start.14 = (bf16[96,384]{1,0:T(8,128)(2,1)S(1)}, bf16[96,384]{1,0:T(8,128)(2,1)S(1)}, u32[]{:S(2)}, u32[]{:S(2)}) collective-permute-start(bf16[96,384]{1,0:T(8,128)(2,1)S(1)} %add_convert_fusion.2), channel_id=1, source_target_pairs={{0,4},{4,0},{8,12},{12,8},{16,20},{20,16},{24,28},{28,24},{1,5},{5... | collective-permute-start | bytes 221192 | tf_op jit(solution)/shard_map/ppermute | solution.py:242
  54.9 17.3 %collective-permute-start.6 = (bf16[2,72,1536]{2,1,0:T(8,128)(2,1)S(1)}, bf16[2,72,1536]{2,1,0:T(8,128)(2,1)S(1)}, u32[]{:S(2)}, u32[]{:S(2)}) collective-permute-start(bf16[2,72,1536]{2,1,0:T(8,128)(2,1)S(1)} %shard_map.69.own_ref.g_ref), channel_id=1, source_target_pairs={{0,4},{4,0},{8,12},{12,8},{16,20},{20,16},{24,28},{28,24},{1,5},{5... | collective-permute-start | bytes 1327112 | tf_op jit(solution)/shard_map/ppermute | solution.py:242
  55.1 17.1 %collective-permute-start.7 = (bf16[2,72,1536]{2,1,0:T(8,128)(2,1)S(1)}, bf16[2,72,1536]{2,1,0:T(8,128)(2,1)S(1)}, u32[]{:S(2)}, u32[]{:S(2)}) collective-permute-start(bf16[2,72,1536]{2,1,0:T(8,128)(2,1)S(1)} %shard_map.69.own_ref.g_ref), channel_id=1, source_target_pairs={{4,8},{12,16},{20,24},{8,4},{16,12},{24,20},{5,9},{13,17},{21,25},... | collective-permute-start | bytes 1327112 | tf_op jit(solution)/shard_map/ppermute | solution.py:249
  67.1 4.4 %collective-permute-start.15 = (bf16[96,384]{1,0:T(8,128)(2,1)S(1)}, bf16[96,384]{1,0:T(8,128)(2,1)S(1)}, u32[]{:S(2)}, u32[]{:S(2)}) collective-permute-start(bf16[96,384]{1,0:T(8,128)(2,1)S(1)} %add_convert_fusion.1), channel_id=1, source_target_pairs={{0,2},{2,0},{1,3},{3,1},{4,6},{6,4},{5,7},{7,5},{8,10},{10,8},{9,1... | collective-permute-start | bytes 221192 | tf_op jit(solution)/shard_map/ppermute | solution.py:242
  71.5 3.4 %collective-permute-start.16 = (bf16[192,384]{1,0:T(8,128)(2,1)S(1)}, bf16[192,384]{1,0:T(8,128)(2,1)S(1)}, u32[]{:S(2)}, u32[]{:S(2)}) collective-permute-start(bf16[192,384]{1,0:T(8,128)(2,1)S(1)} %maximum_select_fusion.1), channel_id=1, source_target_pairs={{0,1},{1,0},{2,3},{3,2},{4,5},{5,4},{6,7},{7,6},{8,9},{9,8},{10,11... | collective-permute-start | bytes 442376 | tf_op jit(solution)/shard_map/ppermute | solution.py:242

commit v3 on v2

--- a/solution.py
+++ b/solution.py
@@ -1,4 +1,5 @@
 import functools
+import math
 
 import jax
 import jax.numpy as jnp
@@ -14,7 +15,7 @@
 BF = jnp.bfloat16
 F32 = jnp.float32
 VM = pl.BlockSpec(memory_space=pltpu.VMEM)
-ANY = pl.BlockSpec(memory_space=pl.ANY)
+ANY = pl.BlockSpec(memory_space=pltpu.HBM)
 
 
 def up(n, k):
@@ -28,18 +29,23 @@
     return cosine / np.mean(cosine)
 
 
-def call(kernel, outs, ins, scratch=(), flops=0, anywhere=()):
+def call(kernel, outs, ins, scratch=(), flops=0, anywhere=(), outside=False, spare=3 << 20):
     nbytes = sum(x.size * x.dtype.itemsize for x in (*ins, *outs))
+    held = sum(
+        up(s.shape[-1], LANES) * math.prod(s.shape[:-1]) * s.dtype.itemsize
+        for s in scratch
+        if s.memory_space == pltpu.VMEM
+    )
     return pl.pallas_call(
         kernel,
         out_shape=list(outs),
         in_specs=[ANY if i in anywhere else VM for i in range(len(ins))],
-        out_specs=[VM for _ in outs],
+        out_specs=[ANY if outside else VM for _ in outs],
         scratch_shapes=list(scratch),
         cost_estimate=pl.CostEstimate(
             flops=flops, bytes_accessed=nbytes, transcendentals=0
         ),
-        compiler_params=pltpu.CompilerParams(vmem_limit_bytes=16 << 20),
+        compiler_params=pltpu.CompilerParams(vmem_limit_bytes=held + spare),
     )(*ins)
 
 
@@ -228,18 +234,29 @@
         o_ref[r] = out[:, :width].astype(o_ref.dtype)
 
 
-def final_kernel(ksize, channels, norm, x_ref, o_ref):
+def final_kernel(ksize, channels, norm, x_ref, o_ref, scr, sem):
+    copies = []
     for a in range(ksize):
+        i = (ksize - 1 - a) * channels
         for b in range(ksize):
-            i, j = (ksize - 1 - a) * channels, b * channels
-            o_ref[a, b] = (
-                x_ref[i : i + channels, j : j + channels].astype(F32) * norm
-            )
+            j = b * channels
+            scr[a, b] = x_ref[i : i + channels, j : j + channels].astype(F32) * norm
+        copies.append(pltpu.make_async_copy(scr.at[a], o_ref.at[a], sem.at[a]))
+        copies[-1].start()
+    for copy in copies:
+        copy.wait()
 
 
 def flip(x, axis, bit):
     size = lax.axis_size(axis)
     return lax.ppermute(x, axis, [(i, i ^ bit) for i in range(size)])
+
+
+def along(x):
+    size = lax.axis_size("space")
+    pairs = [(i, i + 2) for i in range(0, size - 2, 2)]
+    pairs += [(i, i - 2) for i in range(3, size, 2)]
+    return lax.ppermute(x, "space", pairs)
 
 
 def across(x):
@@ -260,31 +277,35 @@
     return (a.astype(F32) + b.astype(F32)).astype(BF)
 
 
-def halve(x, axis):
-    odd = lax.axis_index(axis) & 1
+def own_bit(axis, bit):
+    return (lax.axis_index(axis) // bit) & 1
+
+
+def halve(x, axis, bit):
+    high = own_bit(axis, bit)
     n = x.shape[0] // 2
-    keep = lax.dynamic_slice_in_dim(x, odd * n, n, 0)
-    give = lax.dynamic_slice_in_dim(x, (1 - odd) * n, n, 0)
-    return add(keep, flip(give, axis, 1))
-
-
-def join(x, axis):
-    odd = lax.axis_index(axis) & 1
-    other = flip(x, axis, 1)
+    keep = lax.dynamic_slice_in_dim(x, high * n, n, 0)
+    give = lax.dynamic_slice_in_dim(x, (1 - high) * n, n, 0)
+    return add(keep, flip(give, axis, bit))
+
+
+def join(x, axis, bit):
+    other = flip(x, axis, bit)
     both = jnp.concatenate([x, other], axis=0)
     swapped = jnp.concatenate([other, x], axis=0)
-    return jnp.where(odd == 0, both, swapped)
+    return jnp.where(own_bit(axis, bit) == 0, both, swapped)
 
 
 def reduce_all(x):
-    x = halve(x, "core")
-    x = halve(x, "chip")
-    for bit in bits("chip")[1:]:
-        x = add(x, flip(x, "chip", bit))
-    for bit in bits("space")[1:] + [1]:
-        x = add(x, flip(x, "space", bit))
-    x = join(x, "chip")
-    return join(x, "core")
+    core, first = ("core", 1), ("space", 2)
+    x = halve(x, *core)
+    x = halve(x, *first)
+    rest = [("space", b) for b in bits("space")[2:]]
+    rest += [("chip", b) for b in bits("chip")] + [("space", 1)]
+    for axis in rest:
+        x = add(x, flip(x, *axis))
+    x = join(x, *first)
+    return join(x, *core)
 
 
 def body(prediction_maps, truth_analysis, reciprocal_spread, deconv_inputs, filter_tensor):
@@ -338,10 +359,11 @@
             pltpu.SemaphoreType.DMA((members,)),
         ],
         anywhere=range(1 + members, 1 + 2 * members),
+        spare=max(3, members) << 20,
     )[0]
 
     grad_near = flip(grad, "space", 1)
-    grad_far = across(grad)
+    grad_far = along(grad_near)
 
     n = ksize * channels
     packed = up(n, LANES)
@@ -376,6 +398,11 @@
         functools.partial(final_kernel, ksize, channels, norm),
         [sds((ksize, ksize, channels, channels), F32)],
         [total],
+        [
+            pltpu.VMEM((ksize, ksize, channels, channels), F32),
+            pltpu.SemaphoreType.DMA((ksize,)),
+        ],
+        outside=True,
     )[0]
     return (grad_hidden, grad_kernel)
 

time: 77.2 us -> 77.8 us (level)
  starting transfers between devices: 18.9 us -> 21.5 us
  waiting for transfers between devices: 44.9 us -> 43.8 us
    ppermute x15, waiting for transfers between devices: 44.9 us -> 39.2 us  [flip(): return lax.ppermute(x, axis, [(i, i ^ bit) for i in range(size)])]
    ppermute x0 -> x1, waiting for transfers between devices: none -> 4.59 us  [along(): return lax.ppermute(x, 'space', pairs)]
    ppermute x0 -> x1, starting transfers between devices: none -> 3.7 us  [along(): return lax.ppermute(x, 'space', pairs)]
  transfers between devices with their start and end apart: 17 -> 17, of which waited for: 12 -> 13; matrix products, arithmetic and copies ran while one was open for 3% -> 2% of each run, Pallas kernels for 6% -> 6%
where the time goes in v3:
time: 77.8 us; the launch traced here: 77.5 us
  waiting for transfers between devices  43.8 us (56%)
  starting transfers between devices  21.5 us (28%)
  Pallas kernels  6.94 us (9%)
  local copies, waits for them, and re-layouts  3.34 us (4%)
  other arithmetic  1.2 us (2%)
  between operations  0.83 us (1%)
    ppermute x15, waiting for transfers between devices, flip(): return lax.ppermute(x, axis, [(i, i ^ bit) for i in range(size)])  39.2 us
    ppermute x15, starting transfers between devices, flip(): return lax.ppermute(x, axis, [(i, i ^ bit) for i in range(size)])  17.1 us
    pallas_call x6, Pallas kernels, call(): pl.pallas_call(kernel, out_shape=list(outs), in_specs=[ANY if i in anywhe...  6.94 us
    ppermute x1, waiting for transfers between devices, along(): return lax.ppermute(x, 'space', pairs)  4.59 us
    ppermute x1, starting transfers between devices, along(): return lax.ppermute(x, 'space', pairs)  3.7 us
    unnamed x9, local copies, waits for them, and re-layouts  2.78 us
  transfers between devices with their start and end apart: 17, of which 13 were waited for; matrix products, arithmetic and copies ran while one was open for 2% of the time, Pallas kernels for 6%

profile of v3, /device:TPU:0, one launch (start us, length us, event | category | flops | bytes accessed | tf_op | source)
XLA Modules:
  0.0 77.5 jit_solution(5865057060032043547)
XLA Ops:
  0.6 3.1 %collective-permute-start.1 = (bf16[1,72,2,1440]{3,2,1,0:T(2,128)(2,1)}, bf16[1,72,2,1440]{3,2,1,0:T(2,128)(2,1)S(1)}, u32[]{:S(2)}, u32[]{:S(2)}) collective-permute-start(bf16[1,72,2,1440]{3,2,1,0:T(2,128)(2,1)} %refs_0_.1), channel_id=1, source_target_pairs={{0,2},{2,0},{1,3},{3,1},{4,6},{6,4},{5,7},{7,5},{8,10},{10,8},{9,1... | collective-permute-start | bytes 1244168 | tf_op jit(solution)/shard_map/ppermute | solution.py:252
  3.7 0.0 collective-permute-start
  3.7 10.4 %collective-permute-done.1.refs_2_ = bf16[1,72,2,1440]{3,2,1,0:T(2,128)(2,1)S(1)} collective-permute-done((bf16[1,72,2,1440]{3,2,1,0:T(2,128)(2,1)}, bf16[1,72,2,1440]{3,2,1,0:T(2,128)(2,1)S(1)}, u32[]{:S(2)}, u32[]{:S(2)}) %collective-permute-start.1) | collective-permute-done | bytes 414752 | tf_op jit(solution)/shard_map/ppermute | solution.py:252
  14.1 0.0 collective-permute-start.2
  14.1 1.7 %collective-permute-start.8 = (bf16[1,72,2,1440]{3,2,1,0:T(2,128)(2,1)}, bf16[1,72,2,1440]{3,2,1,0:T(2,128)(2,1)S(1)}, u32[]{:S(2)}, u32[]{:S(2)}) collective-permute-start(bf16[1,72,2,1440]{3,2,1,0:T(2,128)(2,1)} %own_ref.1), channel_id=1, source_target_pairs={{0,4},{4,0},{8,12},{12,8},{16,20},{20,16},{24,28},{28,24},{1,5},{5... | collective-permute-start | bytes 1244168 | tf_op jit(solution)/shard_map/ppermute | solution.py:252
  15.8 0.7 collective-permute-start.9
  16.5 0.9 %convert_element_type.48.refs_4_ = bf16[72,720]{1,0:T(8,128)(2,1)S(1)} convert(f32[72,720]{1,0:T(8,128)} %param.6) | non-fusion elementwise | flops 51840 | bytes 311040 | tf_op jit(solution)/shard_map/convert_element_type | solution.py:333
  17.4 0.3 collective-permute-start.3
  17.7 1.1 %collective-permute-done.3.refs_5_ = bf16[72,720]{1,0:T(8,128)(2,1)S(1)} collective-permute-done((bf16[72,720]{1,0:T(8,128)(2,1)S(1)}, bf16[72,720]{1,0:T(8,128)(2,1)S(1)}, u32[]{:S(2)}, u32[]{:S(2)}) %collective-permute-start.3) | collective-permute-done | bytes 103712 | tf_op jit(solution)/shard_map/ppermute | solution.py:252
  18.8 1.5 %collective-permute-start.4 = (bf16[72,720]{1,0:T(8,128)(2,1)S(1)}, bf16[72,720]{1,0:T(8,128)(2,1)S(1)}, u32[]{:S(2)}, u32[]{:S(2)}) collective-permute-start(bf16[72,720]{1,0:T(8,128)(2,1)S(1)} %convert_element_type.48.refs_4_), channel_id=1, source_target_pairs={{0,2},{2,0},{1,3},{3,1},{4,6},{6,4},{5,7},{7,5},{8,10},{10,8},{9,1... | collective-permute-start | bytes 311048 | tf_op jit(solution)/shard_map/ppermute | solution.py:252
  20.3 3.7 %collective-permute-done.4.refs_6_ = bf16[72,720]{1,0:T(8,128)(2,1)S(1)} collective-permute-done((bf16[72,720]{1,0:T(8,128)(2,1)S(1)}, bf16[72,720]{1,0:T(8,128)(2,1)S(1)}, u32[]{:S(2)}, u32[]{:S(2)}) %collective-permute-start.4) | collective-permute-done | bytes 103712 | tf_op jit(solution)/shard_map/ppermute | solution.py:252
  24.0 0.0 collective-permute-start.5
  24.0 0.0 copy-start.1
  24.0 0.7 copy-done.1
  24.7 0.1 shard_map.68.s_ref
  24.8 0.6 collective-permute-done.5.refs_7_
  25.3 0.0 collective-permute-done.refs_1_
  25.3 0.0 collective-permute-done.2.refs_3_
  25.3 0.0 copy-start
  25.3 1.0 %copy-done = bf16[1,72,2,1440]{3,2,1,0:T(2,128)(2,1)S(1)} copy-done((bf16[1,72,2,1440]{3,2,1,0:T(2,128)(2,1)S(1)}, bf16[1,72,2,1440]{3,2,1,0:T(2,128)(2,1)}, u32[]{:S(2)}) %copy-start) | copy-done | bytes 414744
  26.3 0.0 copy-start.2
  26.3 2.1 %shard_map.69.own_ref.g_ref = bf16[2,72,1536]{2,1,0:T(8,128)(2,1)S(1)} custom-call(f32[144,128]{1,0:T(8,128)S(1)} %shard_map.68.s_ref, bf16[1,72,2,1440]{3,2,1,0:T(2,128)(2,1)S(1)} %copy-done, bf16[1,72,2,1440]{3,2,1,0:T(2,128)(2,1)S(1)} %collective-permute-done.refs_1_, bf16[1,72,2,1440]{3,2,1,0:T(2,128)(2,1)S(1)} %collective-permute-done.1.refs_2_, ...), custom_call_target="tpu_custom_call" | custom-call | bytes 2589696 | tf_op jit(solution)/shard_map/pallas_call | solution.py:39
  28.5 0.0 copy-done.2
  28.5 1.1 %shard_map.71 = (bf16[2,384,1536]{2,1,0:T(8,128)(2,1)S(1)}, f32[144,768]{1,0:T(8,128)S(1)}) custom-call(bf16[2,72,1536]{2,1,0:T(8,128)(2,1)S(1)} %shard_map.69.own_ref.g_ref, bf16[1,72,2,1440]{3,2,1,0:T(2,128)(2,1)S(1)} %copy-done.2), custom_call_target="tpu_custom_call" | custom-call | flops 265420800 | bytes 3658752 | tf_op jit(solution)/shard_map/pallas_call | solution.py:39
  29.6 6.1 %collective-permute-done.8.near_ref = bf16[1,72,2,1440]{3,2,1,0:T(2,128)(2,1)S(1)} collective-permute-done((bf16[1,72,2,1440]{3,2,1,0:T(2,128)(2,1)}, bf16[1,72,2,1440]{3,2,1,0:T(2,128)(2,1)S(1)}, u32[]{:S(2)}, u32[]{:S(2)}) %collective-permute-start.8) | collective-permute-done | bytes 414752 | tf_op jit(solution)/shard_map/ppermute | solution.py:252
  35.7 0.0 collective-permute-done.9.far_ref
  35.7 0.0 copy-start.3
  35.7 1.0 %shard_map.72 = bf16[384,384]{1,0:T(8,128)(2,1)S(1)} custom-call(bf16[2,384,1536]{2,1,0:T(8,128)(2,1)S(1)} %get-tuple-element.4.shift_ref, f32[144,768]{1,0:T(8,128)S(1)} %get-tuple-element.5.own_ref, bf16[1,72,2,1440]{3,2,1,0:T(2,128)(2,1)S(1)} %collective-permute-done.8.near_ref, bf16[1,72,2,1440]{3,2,1,0:T(2,128)(2,1)S(1)} %collective-permute-done.9.far_ref), custom_call_target="tpu_custom_call" | custom-call | flops 530841600 | bytes 3926016 | tf_op jit(solution)/shard_map/pallas_call | solution.py:39
  36.7 0.1 collective-permute-start.10
  36.8 1.3 %collective-permute-done.10 = bf16[192,384]{1,0:T(8,128)(2,1)S(1)} collective-permute-done((bf16[192,384]{1,0:T(8,128)(2,1)S(1)}, bf16[192,384]{1,0:T(8,128)(2,1)S(1)}, u32[]{:S(2)}, u32[]{:S(2)}) %collective-permute-start.10) | collective-permute-done | bytes 147488 | tf_op jit(solution)/shard_map/ppermute | solution.py:252
  38.2 2.5 %collective-permute-start.11 = (bf16[96,384]{1,0:T(8,128)(2,1)S(1)}, bf16[96,384]{1,0:T(8,128)(2,1)S(1)}, u32[]{:S(2)}, u32[]{:S(2)}) collective-permute-start(bf16[96,384]{1,0:T(8,128)(2,1)S(1)} %constant_dynamic-slice_fusion), channel_id=1, source_target_pairs={{0,8},{4,12},{8,0},{12,4},{16,24},{20,28},{24,16},{28,20},{1,9},{5... | collective-permute-start | bytes 221192 | tf_op jit(solution)/shard_map/ppermute | solution.py:252
  40.8 2.6 %collective-permute-done.11 = bf16[96,384]{1,0:T(8,128)(2,1)S(1)} collective-permute-done((bf16[96,384]{1,0:T(8,128)(2,1)S(1)}, bf16[96,384]{1,0:T(8,128)(2,1)S(1)}, u32[]{:S(2)}, u32[]{:S(2)}) %collective-permute-start.11) | collective-permute-done | bytes 73760 | tf_op jit(solution)/shard_map/ppermute | solution.py:252
  43.4 2.9 %collective-permute-start.12 = (bf16[96,384]{1,0:T(8,128)(2,1)S(1)}, bf16[96,384]{1,0:T(8,128)(2,1)S(1)}, u32[]{:S(2)}, u32[]{:S(2)}) collective-permute-start(bf16[96,384]{1,0:T(8,128)(2,1)S(1)} %add_convert_fusion.4), channel_id=1, source_target_pairs={{0,16},{4,20},{8,24},{12,28},{16,0},{20,4},{24,8},{28,12},{1,17},{... | collective-permute-start | bytes 221192 | tf_op jit(solution)/shard_map/ppermute | solution.py:252
  46.2 2.6 %collective-permute-done.12 = bf16[96,384]{1,0:T(8,128)(2,1)S(1)} collective-permute-done((bf16[96,384]{1,0:T(8,128)(2,1)S(1)}, bf16[96,384]{1,0:T(8,128)(2,1)S(1)}, u32[]{:S(2)}, u32[]{:S(2)}) %collective-permute-start.12) | collective-permute-done | bytes 73760 | tf_op jit(solution)/shard_map/ppermute | solution.py:252
  48.9 1.6 %collective-permute-start.13 = (bf16[96,384]{1,0:T(8,128)(2,1)S(1)}, bf16[96,384]{1,0:T(8,128)(2,1)S(1)}, u32[]{:S(2)}, u32[]{:S(2)}) collective-permute-start(bf16[96,384]{1,0:T(8,128)(2,1)S(1)} %add_convert_fusion.3), channel_id=1, source_target_pairs={{0,2},{2,0},{1,3},{3,1},{4,6},{6,4},{5,7},{7,5},{8,10},{10,8},{9,1... | collective-permute-start | bytes 221192 | tf_op jit(solution)/shard_map/ppermute | solution.py:252
  50.5 1.5 %collective-permute-start.6 = (bf16[2,72,1536]{2,1,0:T(8,128)(2,1)S(1)}, bf16[2,72,1536]{2,1,0:T(8,128)(2,1)S(1)}, u32[]{:S(2)}, u32[]{:S(2)}) collective-permute-start(bf16[2,72,1536]{2,1,0:T(8,128)(2,1)S(1)} %shard_map.69.own_ref.g_ref), channel_id=1, source_target_pairs={{0,4},{4,0},{8,12},{12,8},{16,20},{20,16},{24,28},{28,24},{1,5},{5... | collective-permute-start | bytes 1327112 | tf_op jit(solution)/shard_map/ppermute | solution.py:252
  52.0 1.3 %collective-permute-done.13 = bf16[96,384]{1,0:T(8,128)(2,1)S(1)} collective-permute-done((bf16[96,384]{1,0:T(8,128)(2,1)S(1)}, bf16[96,384]{1,0:T(8,128)(2,1)S(1)}, u32[]{:S(2)}, u32[]{:S(2)}) %collective-permute-start.13) | collective-permute-done | bytes 73760 | tf_op jit(solution)/shard_map/ppermute | solution.py:252
  53.3 1.6 %collective-permute-start.14 = (bf16[96,384]{1,0:T(8,128)(2,1)S(1)}, bf16[96,384]{1,0:T(8,128)(2,1)S(1)}, u32[]{:S(2)}, u32[]{:S(2)}) collective-permute-start(bf16[96,384]{1,0:T(8,128)(2,1)S(1)} %add_convert_fusion.2), channel_id=1, source_target_pairs={{0,4},{4,0},{8,12},{12,8},{16,20},{20,16},{24,28},{28,24},{1,5},{5... | collective-permute-start | bytes 221192 | tf_op jit(solution)/shard_map/ppermute | solution.py:252
  54.9 8.3 %collective-permute-done.14 = bf16[96,384]{1,0:T(8,128)(2,1)S(1)} collective-permute-done((bf16[96,384]{1,0:T(8,128)(2,1)S(1)}, bf16[96,384]{1,0:T(8,128)(2,1)S(1)}, u32[]{:S(2)}, u32[]{:S(2)}) %collective-permute-start.14) | collective-permute-done | bytes 73760 | tf_op jit(solution)/shard_map/ppermute | solution.py:252
  63.3 0.3 collective-permute-start.15
  63.6 0.0 collective-permute-done.6.near_ref
  63.6 3.7 %collective-permute-start.7 = (bf16[2,72,1536]{2,1,0:T(8,128)(2,1)S(1)}, bf16[2,72,1536]{2,1,0:T(8,128)(2,1)S(1)}, u32[]{:S(2)}, u32[]{:S(2)}) collective-permute-start(bf16[2,72,1536]{2,1,0:T(8,128)(2,1)S(1)} %collective-permute-done.6.near_ref), channel_id=1, source_target_pairs={{0,8},{8,16},{16,24},{12,4},{20,12},{28,20},{1,9},{9,17},{17,25},{... | collective-permute-start | bytes 1327112 | tf_op jit(solution)/shard_map/ppermute | solution.py:259
  67.3 0.4 collective-permute-done.15
  67.7 0.1 collective-permute-start.16
  67.8 0.0 copy-done.3
  67.8 0.1 copy.9
  68.0 0.4 reshape.7.w_ref
  68.3 0.8 %collective-permute-done.16 = bf16[192,384]{1,0:T(8,128)(2,1)S(1)} collective-permute-done((bf16[192,384]{1,0:T(8,128)(2,1)S(1)}, bf16[192,384]{1,0:T(8,128)(2,1)S(1)}, u32[]{:S(2)}, u32[]{:S(2)}) %collective-permute-start.16) | collective-permute-done | bytes 147488 | tf_op jit(solution)/shard_map/ppermute | solution.py:252
  69.1 0.1 maximum_select_fusion.x_ref
  69.2 1.1 %shard_map.73 = f32[5,5,72,72]{3,2,1,0:T(8,128)} custom-call(bf16[384,384]{1,0:T(8,128)(2,1)S(1)} %maximum_select_fusion.x_ref), custom_call_target="tpu_custom_call" | custom-call | bytes 813312 | tf_op jit(solution)/shard_map/pallas_call | solution.py:39
  70.3 4.6 %collective-permute-done.7.far_ref = bf16[2,72,1536]{2,1,0:T(8,128)(2,1)S(1)} collective-permute-done((bf16[2,72,1536]{2,1,0:T(8,128)(2,1)S(1)}, bf16[2,72,1536]{2,1,0:T(8,128)(2,1)S(1)}, u32[]{:S(2)}, u32[]{:S(2)}) %collective-permute-start.7) | collective-permute-done | bytes 442400 | tf_op jit(solution)/shard_map/ppermute | solution.py:259
  74.9 1.5 %shard_map.70 = bf16[2,72,1440]{2,1,0:T(8,128)(2,1)S(1)} custom-call(bf16[360,360]{1,0:T(8,128)(2,1)S(1)} %reshape.7.w_ref, bf16[2,72,1536]{2,1,0:T(8,128)(2,1)S(1)} %shard_map.69.own_ref.g_ref, bf16[2,72,1536]{2,1,0:T(8,128)(2,1)S(1)} %collective-permute-done.6.near_ref, bf16[2,72,1536]{2,1,0:T(8,128)(2,1)S(1)} %collective-permute-done.7.far_ref), custom_call_target="tpu_custom_call" | custom-call | flops 796262400 | bytes 2001024 | tf_op jit(solution)/shard_map/pallas_call | solution.py:39
  76.4 1.1 %copy.10 = bf16[1,72,2,1440]{3,2,1,0:T(2,128)(2,1)} copy(bf16[1,72,2,1440]{3,1,2,0:T(8,128)(2,1)S(1)} %bitcast.5) | data formatting | bytes 829440
  (8 shorter events, 0.2 us)
Async XLA Ops:
  0.6 13.4 %collective-permute-start.1 = (bf16[1,72,2,1440]{3,2,1,0:T(2,128)(2,1)}, bf16[1,72,2,1440]{3,2,1,0:T(2,128)(2,1)S(1)}, u32[]{:S(2)}, u32[]{:S(2)}) collective-permute-start(bf16[1,72,2,1440]{3,2,1,0:T(2,128)(2,1)} %refs_0_.1), channel_id=1, source_target_pairs={{0,2},{2,0},{1,3},{3,1},{4,6},{6,4},{5,7},{7,5},{8,10},{10,8},{9,1... | collective-permute-start | bytes 1244168 | tf_op jit(solution)/shard_map/ppermute | solution.py:252
  3.7 21.6 %collective-permute-start = (bf16[1,72,2,1440]{3,2,1,0:T(2,128)(2,1)}, bf16[1,72,2,1440]{3,2,1,0:T(2,128)(2,1)S(1)}, u32[]{:S(2)}, u32[]{:S(2)}) collective-permute-start(bf16[1,72,2,1440]{3,2,1,0:T(2,128)(2,1)} %refs_0_.1), channel_id=1, source_target_pairs={{0,1},{1,0},{2,3},{3,2},{4,5},{5,4},{6,7},{7,6},{8,9},{9,8},{10,11... | collective-permute-start | bytes 1244168 | tf_op jit(solution)/shard_map/ppermute | solution.py:252
  14.1 11.3 %collective-permute-start.2 = (bf16[1,72,2,1440]{3,2,1,0:T(2,128)(2,1)S(1)}, bf16[1,72,2,1440]{3,2,1,0:T(2,128)(2,1)S(1)}, u32[]{:S(2)}, u32[]{:S(2)}) collective-permute-start(bf16[1,72,2,1440]{3,2,1,0:T(2,128)(2,1)S(1)} %collective-permute-done.1.refs_2_), channel_id=1, source_target_pairs={{0,1},{1,0},{2,3},{3,2},{4,5},{5,4},{6,7},{7,6},{8,9},{9,8},{10,11... | collective-permute-start | bytes 1244168 | tf_op jit(solution)/shard_map/ppermute | solution.py:252
  14.1 21.6 %collective-permute-start.8 = (bf16[1,72,2,1440]{3,2,1,0:T(2,128)(2,1)}, bf16[1,72,2,1440]{3,2,1,0:T(2,128)(2,1)S(1)}, u32[]{:S(2)}, u32[]{:S(2)}) collective-permute-start(bf16[1,72,2,1440]{3,2,1,0:T(2,128)(2,1)} %own_ref.1), channel_id=1, source_target_pairs={{0,4},{4,0},{8,12},{12,8},{16,20},{20,16},{24,28},{28,24},{1,5},{5... | collective-permute-start | bytes 1244168 | tf_op jit(solution)/shard_map/ppermute | solution.py:252
  15.8 19.9 %collective-permute-start.9 = (bf16[1,72,2,1440]{3,2,1,0:T(2,128)(2,1)}, bf16[1,72,2,1440]{3,2,1,0:T(2,128)(2,1)S(1)}, u32[]{:S(2)}, u32[]{:S(2)}) collective-permute-start(bf16[1,72,2,1440]{3,2,1,0:T(2,128)(2,1)} %own_ref.1), channel_id=1, source_target_pairs={{4,8},{12,16},{20,24},{8,4},{16,12},{24,20},{5,9},{13,17},{21,25},... | collective-permute-start | bytes 1244168 | tf_op jit(solution)/shard_map/ppermute | solution.py:266
  17.4 1.4 %collective-permute-start.3 = (bf16[72,720]{1,0:T(8,128)(2,1)S(1)}, bf16[72,720]{1,0:T(8,128)(2,1)S(1)}, u32[]{:S(2)}, u32[]{:S(2)}) collective-permute-start(bf16[72,720]{1,0:T(8,128)(2,1)S(1)} %convert_element_type.48.refs_4_), channel_id=1, source_target_pairs={{0,1},{1,0},{2,3},{3,2},{4,5},{5,4},{6,7},{7,6},{8,9},{9,8},{10,11... | collective-permute-start | bytes 311048 | tf_op jit(solution)/shard_map/ppermute | solution.py:252
  18.8 5.2 %collective-permute-start.4 = (bf16[72,720]{1,0:T(8,128)(2,1)S(1)}, bf16[72,720]{1,0:T(8,128)(2,1)S(1)}, u32[]{:S(2)}, u32[]{:S(2)}) collective-permute-start(bf16[72,720]{1,0:T(8,128)(2,1)S(1)} %convert_element_type.48.refs_4_), channel_id=1, source_target_pairs={{0,2},{2,0},{1,3},{3,1},{4,6},{6,4},{5,7},{7,5},{8,10},{10,8},{9,1... | collective-permute-start | bytes 311048 | tf_op jit(solution)/shard_map/ppermute | solution.py:252
  24.0 1.3 %collective-permute-start.5 = (bf16[72,720]{1,0:T(8,128)(2,1)S(1)}, bf16[72,720]{1,0:T(8,128)(2,1)S(1)}, u32[]{:S(2)}, u32[]{:S(2)}) collective-permute-start(bf16[72,720]{1,0:T(8,128)(2,1)S(1)} %collective-permute-done.4.refs_6_), channel_id=1, source_target_pairs={{0,1},{1,0},{2,3},{3,2},{4,5},{5,4},{6,7},{7,6},{8,9},{9,8},{10,11... | collective-permute-start | bytes 311048 | tf_op jit(solution)/shard_map/ppermute | solution.py:252
  24.0 0.7 copy-start.1
  25.3 1.0 %copy-start = (bf16[1,72,2,1440]{3,2,1,0:T(2,128)(2,1)S(1)}, bf16[1,72,2,1440]{3,2,1,0:T(2,128)(2,1)}, u32[]{:S(2)}) copy-start(bf16[1,72,2,1440]{3,2,1,0:T(2,128)(2,1)} %refs_0_.1) | copy-start | bytes 1244164
  26.3 2.1 %copy-start.2 = (bf16[1,72,2,1440]{3,2,1,0:T(2,128)(2,1)S(1)}, bf16[1,72,2,1440]{3,2,1,0:T(2,128)(2,1)}, u32[]{:S(2)}) copy-start(bf16[1,72,2,1440]{3,2,1,0:T(2,128)(2,1)} %own_ref.1) | copy-start | bytes 1244164
  35.7 32.1 %copy-start.3 = (bf16[5,5,72,72]{3,2,1,0:T(8,128)(2,1)S(1)}, bf16[5,5,72,72]{3,2,1,0:T(8,128)(2,1)}, u32[]{:S(2)}) copy-start(bf16[5,5,72,72]{3,2,1,0:T(8,128)(2,1)} %param.9) | copy-start | bytes 777604
  36.7 1.4 %collective-permute-start.10 = (bf16[192,384]{1,0:T(8,128)(2,1)S(1)}, bf16[192,384]{1,0:T(8,128)(2,1)S(1)}, u32[]{:S(2)}, u32[]{:S(2)}) collective-permute-start(bf16[192,384]{1,0:T(8,128)(2,1)S(1)} %constant_dynamic-slice_fusion.1), channel_id=1, source_target_pairs={{0,1},{1,0},{2,3},{3,2},{4,5},{5,4},{6,7},{7,6},{8,9},{9,8},{10,11... | collective-permute-start | bytes 442376 | tf_op jit(solution)/shard_map/ppermute | solution.py:252
  38.2 5.1 %collective-permute-start.11 = (bf16[96,384]{1,0:T(8,128)(2,1)S(1)}, bf16[96,384]{1,0:T(8,128)(2,1)S(1)}, u32[]{:S(2)}, u32[]{:S(2)}) collective-permute-start(bf16[96,384]{1,0:T(8,128)(2,1)S(1)} %constant_dynamic-slice_fusion), channel_id=1, source_target_pairs={{0,8},{4,12},{8,0},{12,4},{16,24},{20,28},{24,16},{28,20},{1,9},{5... | collective-permute-start | bytes 221192 | tf_op jit(solution)/shard_map/ppermute | solution.py:252
  43.4 5.5 %collective-permute-start.12 = (bf16[96,384]{1,0:T(8,128)(2,1)S(1)}, bf16[96,384]{1,0:T(8,128)(2,1)S(1)}, u32[]{:S(2)}, u32[]{:S(2)}) collective-permute-start(bf16[96,384]{1,0:T(8,128)(2,1)S(1)} %add_convert_fusion.4), channel_id=1, source_target_pairs={{0,16},{4,20},{8,24},{12,28},{16,0},{20,4},{24,8},{28,12},{1,17},{... | collective-permute-start | bytes 221192 | tf_op jit(solution)/shard_map/ppermute | solution.py:252
  48.9 4.4 %collective-permute-start.13 = (bf16[96,384]{1,0:T(8,128)(2,1)S(1)}, bf16[96,384]{1,0:T(8,128)(2,1)S(1)}, u32[]{:S(2)}, u32[]{:S(2)}) collective-permute-start(bf16[96,384]{1,0:T(8,128)(2,1)S(1)} %add_convert_fusion.3), channel_id=1, source_target_pairs={{0,2},{2,0},{1,3},{3,1},{4,6},{6,4},{5,7},{7,5},{8,10},{10,8},{9,1... | collective-permute-start | bytes 221192 | tf_op jit(solution)/shard_map/ppermute | solution.py:252
  50.5 13.1 %collective-permute-start.6 = (bf16[2,72,1536]{2,1,0:T(8,128)(2,1)S(1)}, bf16[2,72,1536]{2,1,0:T(8,128)(2,1)S(1)}, u32[]{:S(2)}, u32[]{:S(2)}) collective-permute-start(bf16[2,72,1536]{2,1,0:T(8,128)(2,1)S(1)} %shard_map.69.own_ref.g_ref), channel_id=1, source_target_pairs={{0,4},{4,0},{8,12},{12,8},{16,20},{20,16},{24,28},{28,24},{1,5},{5... | collective-permute-start | bytes 1327112 | tf_op jit(solution)/shard_map/ppermute | solution.py:252
  53.3 9.9 %collective-permute-start.14 = (bf16[96,384]{1,0:T(8,128)(2,1)S(1)}, bf16[96,384]{1,0:T(8,128)(2,1)S(1)}, u32[]{:S(2)}, u32[]{:S(2)}) collective-permute-start(bf16[96,384]{1,0:T(8,128)(2,1)S(1)} %add_convert_fusion.2), channel_id=1, source_target_pairs={{0,4},{4,0},{8,12},{12,8},{16,20},{20,16},{24,28},{28,24},{1,5},{5... | collective-permute-start | bytes 221192 | tf_op jit(solution)/shard_map/ppermute | solution.py:252
  63.3 4.4 %collective-permute-start.15 = (bf16[96,384]{1,0:T(8,128)(2,1)S(1)}, bf16[96,384]{1,0:T(8,128)(2,1)S(1)}, u32[]{:S(2)}, u32[]{:S(2)}) collective-permute-start(bf16[96,384]{1,0:T(8,128)(2,1)S(1)} %add_convert_fusion.1), channel_id=1, source_target_pairs={{0,8},{4,12},{8,0},{12,4},{16,24},{20,28},{24,16},{28,20},{1,9},{5... | collective-permute-start | bytes 221192 | tf_op jit(solution)/shard_map/ppermute | solution.py:252
  63.6 11.3 %collective-permute-start.7 = (bf16[2,72,1536]{2,1,0:T(8,128)(2,1)S(1)}, bf16[2,72,1536]{2,1,0:T(8,128)(2,1)S(1)}, u32[]{:S(2)}, u32[]{:S(2)}) collective-permute-start(bf16[2,72,1536]{2,1,0:T(8,128)(2,1)S(1)} %collective-permute-done.6.near_ref), channel_id=1, source_target_pairs={{0,8},{8,16},{16,24},{12,4},{20,12},{28,20},{1,9},{9,17},{17,25},{... | collective-permute-start | bytes 1327112 | tf_op jit(solution)/shard_map/ppermute | solution.py:259
  67.7 1.4 %collective-permute-start.16 = (bf16[192,384]{1,0:T(8,128)(2,1)S(1)}, bf16[192,384]{1,0:T(8,128)(2,1)S(1)}, u32[]{:S(2)}, u32[]{:S(2)}) collective-permute-start(bf16[192,384]{1,0:T(8,128)(2,1)S(1)} %maximum_select_fusion.1), channel_id=1, source_target_pairs={{0,1},{1,0},{2,3},{3,2},{4,5},{5,4},{6,7},{7,6},{8,9},{9,8},{10,11... | collective-permute-start | bytes 442376 | tf_op jit(solution)/shard_map/ppermute | solution.py:252

commit v4 on v3

--- a/solution.py
+++ b/solution.py
@@ -58,13 +58,22 @@
     return x.reshape(x.shape[0] * x.shape[1], x.shape[2])
 
 
-def scale_kernel(rows, s_ref, o_ref):
-    n, c = o_ref.shape[0], s_ref.shape[1]
+def own_kernel(s_ref, x_ref, scale_ref, own_ref, s_scr, x_scr, sem):
+    copies = [
+        pltpu.make_async_copy(s_ref, s_scr, sem.at[0]),
+        pltpu.make_async_copy(x_ref, x_scr, sem.at[1]),
+    ]
+    for copy in copies:
+        copy.start()
+    copies[0].wait()
+    n, c = scale_ref.shape[0], s_ref.shape[1]
     i = lax.broadcasted_iota(jnp.int32, (n, c), 0)
     j = lax.broadcasted_iota(jnp.int32, (n, c), 1)
-    s = jnp.where(i // rows == j, jnp.broadcast_to(s_ref[...], (n, c)), 0.0)
-    s = jnp.sum(s, axis=1, keepdims=True)
-    o_ref[...] = jnp.broadcast_to(s * s, o_ref.shape)
+    s = jnp.broadcast_to(s_scr[...], (n, c))
+    s = jnp.sum(jnp.where(i // (n // c) == j, s, 0.0), axis=1, keepdims=True)
+    scale_ref[...] = jnp.broadcast_to(s * s, scale_ref.shape)
+    copies[1].wait()
+    own_ref[...] = mixed(x_scr)
 
 
 def pick(table, index):
@@ -74,11 +83,47 @@
     return out
 
 
-def energy_kernel(span, members, weights, s_ref, *refs):
-    fields, truths = refs[:members], refs[members : 2 * members]
-    o_ref, part_scr, mix_scr, truth, grad, sem = refs[2 * members :]
+def sums(x, rows):
+    x = jnp.sum(x, axis=0)
+    step = rows
+    while step < 8:
+        x = x + pltpu.roll(x, step, 0)
+        step *= 2
+    return x
+
+
+def tiles(width):
+    return [(low, min(low + LANES, width)) for low in range(0, width, LANES)]
+
+
+def blocks(x):
+    return x.reshape(x.shape[0] // 8, 8, x.shape[1])
+
+
+def pair_kernel(rows, s_ref, own_ref, *refs):
+    *others, o_ref, mix_scr = refs
+    for d, other in enumerate(others):
+        mix_scr[d] = mixed(other)
+    for low, high in tiles(mix_scr.shape[2]):
+        sq = blocks(s_ref[:, : high - low])
+        own = blocks(own_ref[:, low:high].astype(F32))
+        self_inverse = 1.0 / jnp.sqrt(smoothing)
+        total = jnp.full(own.shape[1:], self_inverse, F32)
+        mixture = own * self_inverse
+        for d in range(len(others)):
+            other = blocks(mix_scr[d, :, low:high].astype(F32))
+            diff = own - other
+            inverse = lax.rsqrt(sums(diff * diff * sq, rows) + smoothing)
+            total = total + inverse
+            mixture = mixture + other * inverse[None]
+        o_ref[:, low:high] = (own * total[None] - mixture).reshape(-1, high - low)
+
+
+def energy_kernel(span, members, weights, s_ref, own_ref, pair_ref, *refs):
+    truths = refs[:members]
+    o_ref, part_scr, truth, grad, sem = refs[members:]
     rows, channels, lanes = o_ref.shape
-    width = fields[0].shape[3]
+    width = own_ref.shape[1]
     mix = channels * rows
     parts = members // rows
     me = lax.axis_index("chip") * 2 + lax.axis_index("core")
@@ -89,55 +134,28 @@
     ]
     for copy in copies:
         copy.start()
-    for d in range(members):
-        mix_scr[d] = mixed(fields[d])
-    for copy in copies:
-        copy.wait()
     i = lax.broadcasted_iota(jnp.int32, (mix, channels), 0)
     j = lax.broadcasted_iota(jnp.int32, (mix, channels), 1)
     place = [(i == j * rows + r).astype(BF) for r in range(rows)]
+    for copy in copies:
+        copy.wait()
     for k in range(parts):
         truth[:, k * span : (k + 1) * span] = sum(
             jnp.dot(place[r], part_scr[r * parts + k], preferred_element_type=F32)
             for r in range(rows)
         )
-
-    def sums(x):
-        x = jnp.sum(x, axis=0)
-        step = rows
-        while step < 8:
-            x = x + pltpu.roll(x, step, 0)
-            step *= 2
-        return x
-
-    def load(d, low, high):
-        x = mix_scr[d, :, low:high].astype(F32)
-        return x.reshape(mix // 8, 8, high - low)
-
     sub = lax.broadcasted_iota(jnp.int32, (8, LANES), 0) % rows
-    weight = pick(weights, first)
-    pattern = jnp.full((8, LANES), weight, F32)
+    pattern = jnp.full((8, LANES), pick(weights, first), F32)
     for r in range(1, rows):
         pattern = jnp.where(sub == r, pick(weights, first + r), pattern)
     grad[width // LANES] = jnp.zeros((mix, LANES), F32)
-    for low in range(0, width, LANES):
-        high = min(low + LANES, width)
+    for low, high in tiles(width):
         n = high - low
-        sq = s_ref[:, :n].reshape(mix // 8, 8, n)
-        own = load(0, low, high)
-        offset = own - truth[:, low:high].reshape(mix // 8, 8, n)
-        direct = lax.rsqrt(sums(offset * offset * sq) + smoothing)
-        self_inverse = 1.0 / jnp.sqrt(smoothing)
-        total = jnp.full((8, n), self_inverse, F32)
-        mixture = own * self_inverse
-        for d in range(1, members):
-            other = load(d, low, high)
-            diff = own - other
-            inverse = lax.rsqrt(sums(diff * diff * sq) + smoothing)
-            total = total + inverse
-            mixture = mixture + other * inverse[None]
-        paired = own * total[None] - mixture
-        g = offset * direct[None] - paired * (1.0 / members)
+        sq = blocks(s_ref[:, :n])
+        own = blocks(own_ref[:, low:high].astype(F32))
+        offset = own - blocks(truth[:, low:high])
+        direct = lax.rsqrt(sums(offset * offset * sq, rows) + smoothing)
+        g = offset * direct[None] - blocks(pair_ref[:, low:high]) * (1.0 / members)
         g = g * (sq * pattern[None, :, :n])
         grad[low // LANES, :, :n] = g.reshape(mix, n)
     last = width // LANES
@@ -329,37 +347,49 @@
         return have
 
     fields = spread(prediction_maps)
-    hidden_near = flip(deconv_inputs, "space", 1)
+    near = flip(deconv_inputs, "space", 1)
+    far = across(deconv_inputs)
     truth = truth_analysis.astype(BF)
     truths = spread(truth)
-    hidden_far = across(deconv_inputs)
-    scale = call(
-        functools.partial(scale_kernel, rows),
-        [sds((rows * channels, LANES), F32)],
-        [reciprocal_spread[None]],
-    )[0]
+    mix = rows * channels
+    scale, own = call(
+        own_kernel,
+        [sds((mix, LANES), F32), sds((mix, width), BF)],
+        [reciprocal_spread[None], prediction_maps],
+        [
+            pltpu.VMEM((1, channels), F32),
+            pltpu.VMEM((1, channels, rows, width), BF),
+            pltpu.SemaphoreType.DMA((2,)),
+        ],
+        anywhere=[0, 1],
+    )
     taps = jnp.transpose(filter_tensor, (1, 2, 0, 3)).reshape(
         ksize * channels, ksize * channels
     )
     arrived, seen = [], []
-    for x, t in zip(fields, truths):
-        arrived += [x, core(x)]
+    for i, (x, t) in enumerate(zip(fields, truths)):
+        arrived += [x, core(x)] if i else [core(x)]
         seen += [t, core(t)]
 
     table = [float(v) for v in area_weights(rows_total)]
+    paired = call(
+        functools.partial(pair_kernel, rows),
+        [sds((mix, width), F32)],
+        [scale, own, *arrived],
+        [pltpu.VMEM((members - 1, mix, width), BF)],
+        spare=max(3, members) << 20,
+    )[0]
     grad = call(
         functools.partial(energy_kernel, span, members, table),
         [slab],
-        [scale, *arrived, *seen],
+        [scale, own, paired, *seen],
         [
             pltpu.VMEM((members, channels, span), BF),
-            pltpu.VMEM((members, rows * channels, width), BF),
-            pltpu.VMEM((rows * channels, lanes), F32),
-            pltpu.VMEM((lanes // LANES, rows * channels, LANES), F32),
+            pltpu.VMEM((mix, lanes), F32),
+            pltpu.VMEM((lanes // LANES, mix, LANES), F32),
             pltpu.SemaphoreType.DMA((members,)),
         ],
-        anywhere=range(1 + members, 1 + 2 * members),
-        spare=max(3, members) << 20,
+        anywhere=range(3, 3 + members),
     )[0]
 
     grad_near = flip(grad, "space", 1)
@@ -368,7 +398,6 @@
     n = ksize * channels
     packed = up(n, LANES)
     flops = 2 * n * n * rows * lanes
-    mix = rows * channels
     shifted, own_part = call(
         functools.partial(kgrad_own_kernel, ksize),
         [sds((rows, packed, lanes), BF), sds((mix, rows * packed), F32)],
@@ -378,7 +407,7 @@
     partial = call(
         functools.partial(kgrad_kernel, ksize),
         [sds((packed, packed), BF)],
-        [shifted, own_part, hidden_near, hidden_far],
+        [shifted, own_part, near, far],
         [pltpu.VMEM((3, rows * packed // LANES, mix, LANES), F32)],
         flops * 2 // 3,
     )[0]

time: 77.8 us -> 77.8 us (level)
  waiting for transfers between devices: 43.8 us -> 42.9 us
    ppermute x15, waiting for transfers between devices: 39.2 us -> 38.3 us  [flip(): return lax.ppermute(x, axis, [(i, i ^ bit) for i in range(size)])]
    pallas_call x6 -> x7, Pallas kernels: 6.94 us -> 7.53 us  [call(): pl.pallas_call(kernel, out_shape=list(outs), in_specs=[ANY if i in anywhe...]
  transfers between devices with their start and end apart: 17 -> 17, of which waited for: 13 -> 11; matrix products, arithmetic and copies ran while one was open for 2% -> 2% of each run, Pallas kernels for 6% -> 6%
where the time goes in v4:
time: 77.8 us; the launch traced here: 77.6 us
  waiting for transfers between devices  42.9 us (55%)
  starting transfers between devices  21.7 us (28%)
  Pallas kernels  7.53 us (10%)
  local copies, waits for them, and re-layouts  3.34 us (4%)
  other arithmetic  1.2 us (2%)
  between operations  0.88 us (1%)
    ppermute x15, waiting for transfers between devices, flip(): return lax.ppermute(x, axis, [(i, i ^ bit) for i in range(size)])  38.3 us
    ppermute x15, starting transfers between devices, flip(): return lax.ppermute(x, axis, [(i, i ^ bit) for i in range(size)])  17.4 us
    pallas_call x7, Pallas kernels, call(): pl.pallas_call(kernel, out_shape=list(outs), in_specs=[ANY if i in anywhe...  7.53 us
    ppermute x1, waiting for transfers between devices, along(): return lax.ppermute(x, 'space', pairs)  4.6 us
    ppermute x1, starting transfers between devices, along(): return lax.ppermute(x, 'space', pairs)  3.69 us
    unnamed x9, local copies, waits for them, and re-layouts  2.78 us
  transfers between devices with their start and end apart: 17, of which 11 were waited for; matrix products, arithmetic and copies ran while one was open for 2% of the time, Pallas kernels for 6%

profile of v4, /device:TPU:0, one launch (start us, length us, event | category | flops | bytes accessed | tf_op | source)
XLA Modules:
  0.0 77.6 jit_solution(12856129260448529991)
XLA Ops:
  0.6 3.1 %collective-permute-start.1 = (bf16[1,72,2,1440]{3,2,1,0:T(2,128)(2,1)}, bf16[1,72,2,1440]{3,2,1,0:T(2,128)(2,1)S(1)}, u32[]{:S(2)}, u32[]{:S(2)}) collective-permute-start(bf16[1,72,2,1440]{3,2,1,0:T(2,128)(2,1)} %x_ref.1), channel_id=1, source_target_pairs={{0,2},{2,0},{1,3},{3,1},{4,6},{6,4},{5,7},{7,5},{8,10},{10,8},{9,1... | collective-permute-start | bytes 1244168 | tf_op jit(solution)/shard_map/ppermute | solution.py:270
  3.7 0.0 collective-permute-start
  3.7 10.4 %collective-permute-done.1.refs_1_ = bf16[1,72,2,1440]{3,2,1,0:T(2,128)(2,1)S(1)} collective-permute-done((bf16[1,72,2,1440]{3,2,1,0:T(2,128)(2,1)}, bf16[1,72,2,1440]{3,2,1,0:T(2,128)(2,1)S(1)}, u32[]{:S(2)}, u32[]{:S(2)}) %collective-permute-start.1) | collective-permute-done | bytes 414752 | tf_op jit(solution)/shard_map/ppermute | solution.py:270
  14.1 0.0 collective-permute-start.2
  14.1 1.7 %collective-permute-start.8 = (bf16[1,72,2,1440]{3,2,1,0:T(2,128)(2,1)}, bf16[1,72,2,1440]{3,2,1,0:T(2,128)(2,1)S(1)}, u32[]{:S(2)}, u32[]{:S(2)}) collective-permute-start(bf16[1,72,2,1440]{3,2,1,0:T(2,128)(2,1)} %own_ref.1), channel_id=1, source_target_pairs={{0,4},{4,0},{8,12},{12,8},{16,20},{20,16},{24,28},{28,24},{1,5},{5... | collective-permute-start | bytes 1244168 | tf_op jit(solution)/shard_map/ppermute | solution.py:270
  15.8 0.7 collective-permute-start.9
  16.5 0.9 %convert_element_type.48.refs_0_ = bf16[72,720]{1,0:T(8,128)(2,1)S(1)} convert(f32[72,720]{1,0:T(8,128)} %param.6) | non-fusion elementwise | flops 51840 | bytes 311040 | tf_op jit(solution)/shard_map/convert_element_type | solution.py:352
  17.4 1.6 %collective-permute-start.4 = (bf16[72,720]{1,0:T(8,128)(2,1)S(1)}, bf16[72,720]{1,0:T(8,128)(2,1)S(1)}, u32[]{:S(2)}, u32[]{:S(2)}) collective-permute-start(bf16[72,720]{1,0:T(8,128)(2,1)S(1)} %convert_element_type.48.refs_0_), channel_id=1, source_target_pairs={{0,2},{2,0},{1,3},{3,1},{4,6},{6,4},{5,7},{7,5},{8,10},{10,8},{9,1... | collective-permute-start | bytes 311048 | tf_op jit(solution)/shard_map/ppermute | solution.py:270
  19.0 3.7 %collective-permute-done.4.refs_2_ = bf16[72,720]{1,0:T(8,128)(2,1)S(1)} collective-permute-done((bf16[72,720]{1,0:T(8,128)(2,1)S(1)}, bf16[72,720]{1,0:T(8,128)(2,1)S(1)}, u32[]{:S(2)}, u32[]{:S(2)}) %collective-permute-start.4) | collective-permute-done | bytes 103712 | tf_op jit(solution)/shard_map/ppermute | solution.py:270
  22.7 0.0 collective-permute-start.3
  22.7 0.0 collective-permute-done.refs_0_
  22.7 0.5 collective-permute-start.5
  23.2 0.0 copy-start
  23.2 1.0 %copy-done = bf16[1,72,2,1440]{3,2,1,0:T(2,128)(2,1)S(1)} copy-done((bf16[1,72,2,1440]{3,2,1,0:T(2,128)(2,1)S(1)}, bf16[1,72,2,1440]{3,2,1,0:T(2,128)(2,1)}, u32[]{:S(2)}) %copy-start) | copy-done | bytes 414744
  24.2 0.0 copy-start.1
  24.2 0.7 copy-done.1
  24.9 0.4 shard_map.68
  25.3 0.0 collective-permute-done.2.refs_2_
  25.3 0.0 copy-start.2
  25.3 1.0 %shard_map.69.pair_ref = f32[144,1440]{1,0:T(8,128)S(1)} custom-call(f32[144,128]{1,0:T(8,128)S(1)} %get-tuple-element.6.s_ref, bf16[144,1440]{1,0:T(8,128)(2,1)S(1)} %get-tuple-element.7.own_ref, bf16[1,72,2,1440]{3,2,1,0:T(2,128)(2,1)S(1)} %collective-permute-done.refs_0_, bf16[1,72,2,1440]{3,2,1,0:T(2,128)(2,1)S(1)} %collective-permute-done.1.refs_1_, ...), custom_call_target="tpu_custom_call" | custom-call | bytes 2562048 | tf_op jit(solution)/shard_map/pallas_call | solution.py:39
  26.3 0.0 collective-permute-done.3.refs_1_
  26.3 0.0 collective-permute-done.5.refs_3_
  26.3 1.4 %shard_map.70.own_ref.g_ref = bf16[2,72,1536]{2,1,0:T(8,128)(2,1)S(1)} custom-call(f32[144,128]{1,0:T(8,128)S(1)} %get-tuple-element.6.s_ref, bf16[144,1440]{1,0:T(8,128)(2,1)S(1)} %get-tuple-element.7.own_ref, f32[144,1440]{1,0:T(8,128)S(1)} %shard_map.69.pair_ref, bf16[72,720]{1,0:T(8,128)(2,1)S(1)} %convert_element_type.48.refs_0_, ...), custom_call_target="tpu_custom_call" | custom-call | bytes 2174976 | tf_op jit(solution)/shard_map/pallas_call | solution.py:39
  27.7 0.0 copy-done.2
  27.7 1.1 %shard_map.72 = (bf16[2,384,1536]{2,1,0:T(8,128)(2,1)S(1)}, f32[144,768]{1,0:T(8,128)S(1)}) custom-call(bf16[2,72,1536]{2,1,0:T(8,128)(2,1)S(1)} %shard_map.70.own_ref.g_ref, bf16[1,72,2,1440]{3,2,1,0:T(2,128)(2,1)S(1)} %copy-done.2), custom_call_target="tpu_custom_call" | custom-call | flops 265420800 | bytes 3658752 | tf_op jit(solution)/shard_map/pallas_call | solution.py:39
  28.9 6.8 %collective-permute-done.8.near_ref = bf16[1,72,2,1440]{3,2,1,0:T(2,128)(2,1)S(1)} collective-permute-done((bf16[1,72,2,1440]{3,2,1,0:T(2,128)(2,1)}, bf16[1,72,2,1440]{3,2,1,0:T(2,128)(2,1)S(1)}, u32[]{:S(2)}, u32[]{:S(2)}) %collective-permute-start.8) | collective-permute-done | bytes 414752 | tf_op jit(solution)/shard_map/ppermute | solution.py:270
  35.7 0.0 collective-permute-done.9.far_ref
  35.7 0.0 copy-start.3
  35.7 1.0 %shard_map.73 = bf16[384,384]{1,0:T(8,128)(2,1)S(1)} custom-call(bf16[2,384,1536]{2,1,0:T(8,128)(2,1)S(1)} %get-tuple-element.8.shift_ref, f32[144,768]{1,0:T(8,128)S(1)} %get-tuple-element.9.own_ref, bf16[1,72,2,1440]{3,2,1,0:T(2,128)(2,1)S(1)} %collective-permute-done.8.near_ref, bf16[1,72,2,1440]{3,2,1,0:T(2,128)(2,1)S(1)} %collective-permute-done.9.far_ref), custom_call_target="tpu_custom_call" | custom-call | flops 530841600 | bytes 3926016 | tf_op jit(solution)/shard_map/pallas_call | solution.py:39
  36.7 0.1 collective-permute-start.10
  36.8 1.3 %collective-permute-done.10 = bf16[192,384]{1,0:T(8,128)(2,1)S(1)} collective-permute-done((bf16[192,384]{1,0:T(8,128)(2,1)S(1)}, bf16[192,384]{1,0:T(8,128)(2,1)S(1)}, u32[]{:S(2)}, u32[]{:S(2)}) %collective-permute-start.10) | collective-permute-done | bytes 147488 | tf_op jit(solution)/shard_map/ppermute | solution.py:270
  38.2 0.1 add_convert_fusion
  38.3 2.5 %collective-permute-start.11 = (bf16[96,384]{1,0:T(8,128)(2,1)S(1)}, bf16[96,384]{1,0:T(8,128)(2,1)S(1)}, u32[]{:S(2)}, u32[]{:S(2)}) collective-permute-start(bf16[96,384]{1,0:T(8,128)(2,1)S(1)} %constant_dynamic-slice_fusion), channel_id=1, source_target_pairs={{0,8},{4,12},{8,0},{12,4},{16,24},{20,28},{24,16},{28,20},{1,9},{5... | collective-permute-start | bytes 221192 | tf_op jit(solution)/shard_map/ppermute | solution.py:270
  40.8 2.6 %collective-permute-done.11 = bf16[96,384]{1,0:T(8,128)(2,1)S(1)} collective-permute-done((bf16[96,384]{1,0:T(8,128)(2,1)S(1)}, bf16[96,384]{1,0:T(8,128)(2,1)S(1)}, u32[]{:S(2)}, u32[]{:S(2)}) %collective-permute-start.11) | collective-permute-done | bytes 73760 | tf_op jit(solution)/shard_map/ppermute | solution.py:270
  43.4 2.9 %collective-permute-start.12 = (bf16[96,384]{1,0:T(8,128)(2,1)S(1)}, bf16[96,384]{1,0:T(8,128)(2,1)S(1)}, u32[]{:S(2)}, u32[]{:S(2)}) collective-permute-start(bf16[96,384]{1,0:T(8,128)(2,1)S(1)} %add_convert_fusion.4), channel_id=1, source_target_pairs={{0,16},{4,20},{8,24},{12,28},{16,0},{20,4},{24,8},{28,12},{1,17},{... | collective-permute-start | bytes 221192 | tf_op jit(solution)/shard_map/ppermute | solution.py:270
  46.3 2.6 %collective-permute-done.12 = bf16[96,384]{1,0:T(8,128)(2,1)S(1)} collective-permute-done((bf16[96,384]{1,0:T(8,128)(2,1)S(1)}, bf16[96,384]{1,0:T(8,128)(2,1)S(1)}, u32[]{:S(2)}, u32[]{:S(2)}) %collective-permute-start.12) | collective-permute-done | bytes 73760 | tf_op jit(solution)/shard_map/ppermute | solution.py:270
  48.9 1.6 %collective-permute-start.13 = (bf16[96,384]{1,0:T(8,128)(2,1)S(1)}, bf16[96,384]{1,0:T(8,128)(2,1)S(1)}, u32[]{:S(2)}, u32[]{:S(2)}) collective-permute-start(bf16[96,384]{1,0:T(8,128)(2,1)S(1)} %add_convert_fusion.3), channel_id=1, source_target_pairs={{0,2},{2,0},{1,3},{3,1},{4,6},{6,4},{5,7},{7,5},{8,10},{10,8},{9,1... | collective-permute-start | bytes 221192 | tf_op jit(solution)/shard_map/ppermute | solution.py:270
  50.5 1.5 %collective-permute-start.6 = (bf16[2,72,1536]{2,1,0:T(8,128)(2,1)S(1)}, bf16[2,72,1536]{2,1,0:T(8,128)(2,1)S(1)}, u32[]{:S(2)}, u32[]{:S(2)}) collective-permute-start(bf16[2,72,1536]{2,1,0:T(8,128)(2,1)S(1)} %shard_map.70.own_ref.g_ref), channel_id=1, source_target_pairs={{0,4},{4,0},{8,12},{12,8},{16,20},{20,16},{24,28},{28,24},{1,5},{5... | collective-permute-start | bytes 1327112 | tf_op jit(solution)/shard_map/ppermute | solution.py:270
  52.0 1.3 %collective-permute-done.13 = bf16[96,384]{1,0:T(8,128)(2,1)S(1)} collective-permute-done((bf16[96,384]{1,0:T(8,128)(2,1)S(1)}, bf16[96,384]{1,0:T(8,128)(2,1)S(1)}, u32[]{:S(2)}, u32[]{:S(2)}) %collective-permute-start.13) | collective-permute-done | bytes 73760 | tf_op jit(solution)/shard_map/ppermute | solution.py:270
  53.4 1.6 %collective-permute-start.14 = (bf16[96,384]{1,0:T(8,128)(2,1)S(1)}, bf16[96,384]{1,0:T(8,128)(2,1)S(1)}, u32[]{:S(2)}, u32[]{:S(2)}) collective-permute-start(bf16[96,384]{1,0:T(8,128)(2,1)S(1)} %add_convert_fusion.2), channel_id=1, source_target_pairs={{0,4},{4,0},{8,12},{12,8},{16,20},{20,16},{24,28},{28,24},{1,5},{5... | collective-permute-start | bytes 221192 | tf_op jit(solution)/shard_map/ppermute | solution.py:270
  54.9 8.3 %collective-permute-done.14 = bf16[96,384]{1,0:T(8,128)(2,1)S(1)} collective-permute-done((bf16[96,384]{1,0:T(8,128)(2,1)S(1)}, bf16[96,384]{1,0:T(8,128)(2,1)S(1)}, u32[]{:S(2)}, u32[]{:S(2)}) %collective-permute-start.14) | collective-permute-done | bytes 73760 | tf_op jit(solution)/shard_map/ppermute | solution.py:270
  63.3 0.3 collective-permute-start.15
  63.6 0.0 collective-permute-done.6.near_ref
  63.6 3.7 %collective-permute-start.7 = (bf16[2,72,1536]{2,1,0:T(8,128)(2,1)S(1)}, bf16[2,72,1536]{2,1,0:T(8,128)(2,1)S(1)}, u32[]{:S(2)}, u32[]{:S(2)}) collective-permute-start(bf16[2,72,1536]{2,1,0:T(8,128)(2,1)S(1)} %collective-permute-done.6.near_ref), channel_id=1, source_target_pairs={{0,8},{8,16},{16,24},{12,4},{20,12},{28,20},{1,9},{9,17},{17,25},{... | collective-permute-start | bytes 1327112 | tf_op jit(solution)/shard_map/ppermute | solution.py:277
  67.3 0.4 collective-permute-done.15
  67.7 0.1 collective-permute-start.16
  67.8 0.0 copy-done.3
  67.8 0.1 copy.9
  68.0 0.4 reshape.7.w_ref
  68.3 0.8 %collective-permute-done.16 = bf16[192,384]{1,0:T(8,128)(2,1)S(1)} collective-permute-done((bf16[192,384]{1,0:T(8,128)(2,1)S(1)}, bf16[192,384]{1,0:T(8,128)(2,1)S(1)}, u32[]{:S(2)}, u32[]{:S(2)}) %collective-permute-start.16) | collective-permute-done | bytes 147488 | tf_op jit(solution)/shard_map/ppermute | solution.py:270
  69.2 0.1 maximum_select_fusion.x_ref
  69.2 1.1 %shard_map.74 = f32[5,5,72,72]{3,2,1,0:T(8,128)} custom-call(bf16[384,384]{1,0:T(8,128)(2,1)S(1)} %maximum_select_fusion.x_ref), custom_call_target="tpu_custom_call" | custom-call | bytes 813312 | tf_op jit(solution)/shard_map/pallas_call | solution.py:39
  70.3 4.6 %collective-permute-done.7.far_ref = bf16[2,72,1536]{2,1,0:T(8,128)(2,1)S(1)} collective-permute-done((bf16[2,72,1536]{2,1,0:T(8,128)(2,1)S(1)}, bf16[2,72,1536]{2,1,0:T(8,128)(2,1)S(1)}, u32[]{:S(2)}, u32[]{:S(2)}) %collective-permute-start.7) | collective-permute-done | bytes 442400 | tf_op jit(solution)/shard_map/ppermute | solution.py:277
  74.9 1.5 %shard_map.71 = bf16[2,72,1440]{2,1,0:T(8,128)(2,1)S(1)} custom-call(bf16[360,360]{1,0:T(8,128)(2,1)S(1)} %reshape.7.w_ref, bf16[2,72,1536]{2,1,0:T(8,128)(2,1)S(1)} %shard_map.70.own_ref.g_ref, bf16[2,72,1536]{2,1,0:T(8,128)(2,1)S(1)} %collective-permute-done.6.near_ref, bf16[2,72,1536]{2,1,0:T(8,128)(2,1)S(1)} %collective-permute-done.7.far_ref), custom_call_target="tpu_custom_call" | custom-call | flops 796262400 | bytes 2001024 | tf_op jit(solution)/shard_map/pallas_call | solution.py:39
  76.5 1.1 %copy.10 = bf16[1,72,2,1440]{3,2,1,0:T(2,128)(2,1)} copy(bf16[1,72,2,1440]{3,1,2,0:T(8,128)(2,1)S(1)} %bitcast.5) | data formatting | bytes 829440
  (7 shorter events, 0.2 us)
Async XLA Ops:
  0.6 13.4 %collective-permute-start.1 = (bf16[1,72,2,1440]{3,2,1,0:T(2,128)(2,1)}, bf16[1,72,2,1440]{3,2,1,0:T(2,128)(2,1)S(1)}, u32[]{:S(2)}, u32[]{:S(2)}) collective-permute-start(bf16[1,72,2,1440]{3,2,1,0:T(2,128)(2,1)} %x_ref.1), channel_id=1, source_target_pairs={{0,2},{2,0},{1,3},{3,1},{4,6},{6,4},{5,7},{7,5},{8,10},{10,8},{9,1... | collective-permute-start | bytes 1244168 | tf_op jit(solution)/shard_map/ppermute | solution.py:270
  3.7 19.0 %collective-permute-start = (bf16[1,72,2,1440]{3,2,1,0:T(2,128)(2,1)}, bf16[1,72,2,1440]{3,2,1,0:T(2,128)(2,1)S(1)}, u32[]{:S(2)}, u32[]{:S(2)}) collective-permute-start(bf16[1,72,2,1440]{3,2,1,0:T(2,128)(2,1)} %x_ref.1), channel_id=1, source_target_pairs={{0,1},{1,0},{2,3},{3,2},{4,5},{5,4},{6,7},{7,6},{8,9},{9,8},{10,11... | collective-permute-start | bytes 1244168 | tf_op jit(solution)/shard_map/ppermute | solution.py:270
  14.1 11.2 %collective-permute-start.2 = (bf16[1,72,2,1440]{3,2,1,0:T(2,128)(2,1)S(1)}, bf16[1,72,2,1440]{3,2,1,0:T(2,128)(2,1)S(1)}, u32[]{:S(2)}, u32[]{:S(2)}) collective-permute-start(bf16[1,72,2,1440]{3,2,1,0:T(2,128)(2,1)S(1)} %collective-permute-done.1.refs_1_), channel_id=1, source_target_pairs={{0,1},{1,0},{2,3},{3,2},{4,5},{5,4},{6,7},{7,6},{8,9},{9,8},{10,11... | collective-permute-start | bytes 1244168 | tf_op jit(solution)/shard_map/ppermute | solution.py:270
  14.1 21.6 %collective-permute-start.8 = (bf16[1,72,2,1440]{3,2,1,0:T(2,128)(2,1)}, bf16[1,72,2,1440]{3,2,1,0:T(2,128)(2,1)S(1)}, u32[]{:S(2)}, u32[]{:S(2)}) collective-permute-start(bf16[1,72,2,1440]{3,2,1,0:T(2,128)(2,1)} %own_ref.1), channel_id=1, source_target_pairs={{0,4},{4,0},{8,12},{12,8},{16,20},{20,16},{24,28},{28,24},{1,5},{5... | collective-permute-start | bytes 1244168 | tf_op jit(solution)/shard_map/ppermute | solution.py:270
  15.8 19.9 %collective-permute-start.9 = (bf16[1,72,2,1440]{3,2,1,0:T(2,128)(2,1)}, bf16[1,72,2,1440]{3,2,1,0:T(2,128)(2,1)S(1)}, u32[]{:S(2)}, u32[]{:S(2)}) collective-permute-start(bf16[1,72,2,1440]{3,2,1,0:T(2,128)(2,1)} %own_ref.1), channel_id=1, source_target_pairs={{4,8},{12,16},{20,24},{8,4},{16,12},{24,20},{5,9},{13,17},{21,25},... | collective-permute-start | bytes 1244168 | tf_op jit(solution)/shard_map/ppermute | solution.py:284
  17.4 5.3 %collective-permute-start.4 = (bf16[72,720]{1,0:T(8,128)(2,1)S(1)}, bf16[72,720]{1,0:T(8,128)(2,1)S(1)}, u32[]{:S(2)}, u32[]{:S(2)}) collective-permute-start(bf16[72,720]{1,0:T(8,128)(2,1)S(1)} %convert_element_type.48.refs_0_), channel_id=1, source_target_pairs={{0,2},{2,0},{1,3},{3,1},{4,6},{6,4},{5,7},{7,5},{8,10},{10,8},{9,1... | collective-permute-start | bytes 311048 | tf_op jit(solution)/shard_map/ppermute | solution.py:270
  22.7 3.6 %collective-permute-start.3 = (bf16[72,720]{1,0:T(8,128)(2,1)S(1)}, bf16[72,720]{1,0:T(8,128)(2,1)S(1)}, u32[]{:S(2)}, u32[]{:S(2)}) collective-permute-start(bf16[72,720]{1,0:T(8,128)(2,1)S(1)} %convert_element_type.48.refs_0_), channel_id=1, source_target_pairs={{0,1},{1,0},{2,3},{3,2},{4,5},{5,4},{6,7},{7,6},{8,9},{9,8},{10,11... | collective-permute-start | bytes 311048 | tf_op jit(solution)/shard_map/ppermute | solution.py:270
  22.7 3.6 %collective-permute-start.5 = (bf16[72,720]{1,0:T(8,128)(2,1)S(1)}, bf16[72,720]{1,0:T(8,128)(2,1)S(1)}, u32[]{:S(2)}, u32[]{:S(2)}) collective-permute-start(bf16[72,720]{1,0:T(8,128)(2,1)S(1)} %collective-permute-done.4.refs_2_), channel_id=1, source_target_pairs={{0,1},{1,0},{2,3},{3,2},{4,5},{5,4},{6,7},{7,6},{8,9},{9,8},{10,11... | collective-permute-start | bytes 311048 | tf_op jit(solution)/shard_map/ppermute | solution.py:270
  23.2 1.0 %copy-start = (bf16[1,72,2,1440]{3,2,1,0:T(2,128)(2,1)S(1)}, bf16[1,72,2,1440]{3,2,1,0:T(2,128)(2,1)}, u32[]{:S(2)}) copy-start(bf16[1,72,2,1440]{3,2,1,0:T(2,128)(2,1)} %x_ref.1) | copy-start | bytes 1244164
  24.2 0.7 copy-start.1
  25.3 2.4 %copy-start.2 = (bf16[1,72,2,1440]{3,2,1,0:T(2,128)(2,1)S(1)}, bf16[1,72,2,1440]{3,2,1,0:T(2,128)(2,1)}, u32[]{:S(2)}) copy-start(bf16[1,72,2,1440]{3,2,1,0:T(2,128)(2,1)} %own_ref.1) | copy-start | bytes 1244164
  35.7 32.1 %copy-start.3 = (bf16[5,5,72,72]{3,2,1,0:T(8,128)(2,1)S(1)}, bf16[5,5,72,72]{3,2,1,0:T(8,128)(2,1)}, u32[]{:S(2)}) copy-start(bf16[5,5,72,72]{3,2,1,0:T(8,128)(2,1)} %param.9) | copy-start | bytes 777604
  36.7 1.4 %collective-permute-start.10 = (bf16[192,384]{1,0:T(8,128)(2,1)S(1)}, bf16[192,384]{1,0:T(8,128)(2,1)S(1)}, u32[]{:S(2)}, u32[]{:S(2)}) collective-permute-start(bf16[192,384]{1,0:T(8,128)(2,1)S(1)} %constant_dynamic-slice_fusion.1), channel_id=1, source_target_pairs={{0,1},{1,0},{2,3},{3,2},{4,5},{5,4},{6,7},{7,6},{8,9},{9,8},{10,11... | collective-permute-start | bytes 442376 | tf_op jit(solution)/shard_map/ppermute | solution.py:270
  38.3 5.1 %collective-permute-start.11 = (bf16[96,384]{1,0:T(8,128)(2,1)S(1)}, bf16[96,384]{1,0:T(8,128)(2,1)S(1)}, u32[]{:S(2)}, u32[]{:S(2)}) collective-permute-start(bf16[96,384]{1,0:T(8,128)(2,1)S(1)} %constant_dynamic-slice_fusion), channel_id=1, source_target_pairs={{0,8},{4,12},{8,0},{12,4},{16,24},{20,28},{24,16},{28,20},{1,9},{5... | collective-permute-start | bytes 221192 | tf_op jit(solution)/shard_map/ppermute | solution.py:270
  43.4 5.5 %collective-permute-start.12 = (bf16[96,384]{1,0:T(8,128)(2,1)S(1)}, bf16[96,384]{1,0:T(8,128)(2,1)S(1)}, u32[]{:S(2)}, u32[]{:S(2)}) collective-permute-start(bf16[96,384]{1,0:T(8,128)(2,1)S(1)} %add_convert_fusion.4), channel_id=1, source_target_pairs={{0,16},{4,20},{8,24},{12,28},{16,0},{20,4},{24,8},{28,12},{1,17},{... | collective-permute-start | bytes 221192 | tf_op jit(solution)/shard_map/ppermute | solution.py:270
  48.9 4.4 %collective-permute-start.13 = (bf16[96,384]{1,0:T(8,128)(2,1)S(1)}, bf16[96,384]{1,0:T(8,128)(2,1)S(1)}, u32[]{:S(2)}, u32[]{:S(2)}) collective-permute-start(bf16[96,384]{1,0:T(8,128)(2,1)S(1)} %add_convert_fusion.3), channel_id=1, source_target_pairs={{0,2},{2,0},{1,3},{3,1},{4,6},{6,4},{5,7},{7,5},{8,10},{10,8},{9,1... | collective-permute-start | bytes 221192 | tf_op jit(solution)/shard_map/ppermute | solution.py:270
  50.5 13.1 %collective-permute-start.6 = (bf16[2,72,1536]{2,1,0:T(8,128)(2,1)S(1)}, bf16[2,72,1536]{2,1,0:T(8,128)(2,1)S(1)}, u32[]{:S(2)}, u32[]{:S(2)}) collective-permute-start(bf16[2,72,1536]{2,1,0:T(8,128)(2,1)S(1)} %shard_map.70.own_ref.g_ref), channel_id=1, source_target_pairs={{0,4},{4,0},{8,12},{12,8},{16,20},{20,16},{24,28},{28,24},{1,5},{5... | collective-permute-start | bytes 1327112 | tf_op jit(solution)/shard_map/ppermute | solution.py:270
  53.4 9.9 %collective-permute-start.14 = (bf16[96,384]{1,0:T(8,128)(2,1)S(1)}, bf16[96,384]{1,0:T(8,128)(2,1)S(1)}, u32[]{:S(2)}, u32[]{:S(2)}) collective-permute-start(bf16[96,384]{1,0:T(8,128)(2,1)S(1)} %add_convert_fusion.2), channel_id=1, source_target_pairs={{0,4},{4,0},{8,12},{12,8},{16,20},{20,16},{24,28},{28,24},{1,5},{5... | collective-permute-start | bytes 221192 | tf_op jit(solution)/shard_map/ppermute | solution.py:270
  63.3 4.4 %collective-permute-start.15 = (bf16[96,384]{1,0:T(8,128)(2,1)S(1)}, bf16[96,384]{1,0:T(8,128)(2,1)S(1)}, u32[]{:S(2)}, u32[]{:S(2)}) collective-permute-start(bf16[96,384]{1,0:T(8,128)(2,1)S(1)} %add_convert_fusion.1), channel_id=1, source_target_pairs={{0,8},{4,12},{8,0},{12,4},{16,24},{20,28},{24,16},{28,20},{1,9},{5... | collective-permute-start | bytes 221192 | tf_op jit(solution)/shard_map/ppermute | solution.py:270
  63.6 11.3 %collective-permute-start.7 = (bf16[2,72,1536]{2,1,0:T(8,128)(2,1)S(1)}, bf16[2,72,1536]{2,1,0:T(8,128)(2,1)S(1)}, u32[]{:S(2)}, u32[]{:S(2)}) collective-permute-start(bf16[2,72,1536]{2,1,0:T(8,128)(2,1)S(1)} %collective-permute-done.6.near_ref), channel_id=1, source_target_pairs={{0,8},{8,16},{16,24},{12,4},{20,12},{28,20},{1,9},{9,17},{17,25},{... | collective-permute-start | bytes 1327112 | tf_op jit(solution)/shard_map/ppermute | solution.py:277
  67.7 1.4 %collective-permute-start.16 = (bf16[192,384]{1,0:T(8,128)(2,1)S(1)}, bf16[192,384]{1,0:T(8,128)(2,1)S(1)}, u32[]{:S(2)}, u32[]{:S(2)}) collective-permute-start(bf16[192,384]{1,0:T(8,128)(2,1)S(1)} %maximum_select_fusion.1), channel_id=1, source_target_pairs={{0,1},{1,0},{2,3},{3,2},{4,5},{5,4},{6,7},{7,6},{8,9},{9,8},{10,11... | collective-permute-start | bytes 442376 | tf_op jit(solution)/shard_map/ppermute | solution.py:270

commit v5 on v4

--- a/solution.py
+++ b/solution.py
@@ -29,7 +29,7 @@
     return cosine / np.mean(cosine)
 
 
-def call(kernel, outs, ins, scratch=(), flops=0, anywhere=(), outside=False, spare=3 << 20):
+def call(kernel, outs, ins, scratch=(), flops=0, anywhere=(), outside=False, aliases={}, spare=3 << 20):
     nbytes = sum(x.size * x.dtype.itemsize for x in (*ins, *outs))
     held = sum(
         up(s.shape[-1], LANES) * math.prod(s.shape[:-1]) * s.dtype.itemsize
@@ -42,6 +42,7 @@
         in_specs=[ANY if i in anywhere else VM for i in range(len(ins))],
         out_specs=[ANY if outside else VM for _ in outs],
         scratch_shapes=list(scratch),
+        input_output_aliases=aliases,
         cost_estimate=pl.CostEstimate(
             flops=flops, bytes_accessed=nbytes, transcendentals=0
         ),
@@ -232,9 +233,9 @@
         scr[below + r] = far(r)
 
 
-def conv_kernel(ksize, w_ref, own_ref, near_ref, far_ref, o_ref, g_scr):
+def conv_kernel(ksize, w_ref, own_ref, near_ref, far_ref, o_ref, g_scr, tile_scr, mix_scr):
     rows, channels, lanes = own_ref.shape
-    width = o_ref.shape[2]
+    width = o_ref.shape[3]
     mid = ksize // 2
     gather_rows(
         lambda r: own_ref[r], lambda r: near_ref[r], lambda r: far_ref[r], g_scr
@@ -249,20 +250,40 @@
             if b != mid:
                 part = pltpu.roll(part, (mid - b) % lanes, 1)
             out = part if out is None else out + part
-        o_ref[r] = out[:, :width].astype(o_ref.dtype)
-
-
-def final_kernel(ksize, channels, norm, x_ref, o_ref, scr, sem):
-    copies = []
-    for a in range(ksize):
-        i = (ksize - 1 - a) * channels
-        for b in range(ksize):
-            j = b * channels
-            scr[a, b] = x_ref[i : i + channels, j : j + channels].astype(F32) * norm
-        copies.append(pltpu.make_async_copy(scr.at[a], o_ref.at[a], sem.at[a]))
-        copies[-1].start()
-    for copy in copies:
-        copy.wait()
+        for t in range(tile_scr.shape[0]):
+            row = pl.ds(r, channels, stride=rows)
+            tile_scr[t, row, :] = out[:, t * LANES : (t + 1) * LANES]
+    for low, high in tiles(width):
+        mix_scr[:, low:high] = tile_scr[low // LANES][:, : high - low].astype(BF)
+    o_ref[0] = mix_scr[...].reshape(channels, rows, width)
+
+
+def final_kernel(ksize, channels, norm, own, x_ref, *refs):
+    o_ref, scr, sem = refs[-3:]
+    n = x_ref.shape[0]
+    half = lax.axis_index("core") % 2
+    half = half if own else 1 - half
+    for h in range(2):
+
+        @pl.when(half == h)
+        def _():
+            copies = []
+            for i in range(ksize):
+                low = max(i * channels, h * n)
+                high = min((i + 1) * channels, (h + 1) * n)
+                if low >= high:
+                    continue
+                a, rows = ksize - 1 - i, slice(low - i * channels, high - i * channels)
+                for b in range(ksize):
+                    x = x_ref[low - h * n : high - h * n, b * channels : (b + 1) * channels]
+                    scr[a, b, rows] = x.astype(F32) * norm
+                at = (a, slice(None), pl.ds(rows.start, high - low))
+                copies.append(
+                    pltpu.make_async_copy(scr.at[at], o_ref.at[at], sem.at[a])
+                )
+                copies[-1].start()
+            for copy in copies:
+                copy.wait()
 
 
 def flip(x, axis, bit):
@@ -323,7 +344,7 @@
     for axis in rest:
         x = add(x, flip(x, *axis))
     x = join(x, *first)
-    return join(x, *core)
+    return x, flip(x, *core)
 
 
 def body(prediction_maps, truth_analysis, reciprocal_spread, deconv_inputs, filter_tensor):
@@ -335,7 +356,6 @@
     span = truth_analysis.shape[1]
     sds = jax.ShapeDtypeStruct
     slab = sds((rows, channels, lanes), BF)
-    scratch = [pltpu.VMEM((3 * rows, channels, lanes), BF)]
 
     def core(x):
         return flip(x, "core", 1)
@@ -363,9 +383,7 @@
         ],
         anywhere=[0, 1],
     )
-    taps = jnp.transpose(filter_tensor, (1, 2, 0, 3)).reshape(
-        ksize * channels, ksize * channels
-    )
+    taps = jnp.transpose(filter_tensor, (1, 2, 0, 3)).reshape(ksize * channels, ksize * channels)
     arrived, seen = [], []
     for i, (x, t) in enumerate(zip(fields, truths)):
         arrived += [x, core(x)] if i else [core(x)]
@@ -411,28 +429,36 @@
         [pltpu.VMEM((3, rows * packed // LANES, mix, LANES), F32)],
         flops * 2 // 3,
     )[0]
-    total = reduce_all(partial)
-
-    back = call(
+    own_half, other_half = reduce_all(partial)
+
+    grad_hidden = call(
         functools.partial(conv_kernel, ksize),
-        [sds((rows, channels, width), BF)],
+        [sds(prediction_maps.shape, BF)],
         [taps, grad, grad_near, grad_far],
-        scratch,
+        [
+            pltpu.VMEM((3 * rows, channels, lanes), BF),
+            pltpu.VMEM((lanes // LANES, mix, LANES), F32),
+            pltpu.VMEM((mix, width), BF),
+        ],
         2 * n * n * rows * lanes,
     )[0]
-    grad_hidden = jnp.transpose(back, (1, 0, 2))[None]
 
     norm = 1.0 / float(members * rows_total * width) ** 0.5
-    grad_kernel = call(
-        functools.partial(final_kernel, ksize, channels, norm),
-        [sds((ksize, ksize, channels, channels), F32)],
-        [total],
-        [
-            pltpu.VMEM((ksize, ksize, channels, channels), F32),
-            pltpu.SemaphoreType.DMA((ksize,)),
-        ],
-        outside=True,
-    )[0]
+    shape = (ksize, ksize, channels, channels)
+
+    def finish(own, *xs):
+        return call(
+            functools.partial(final_kernel, ksize, channels, norm, own),
+            [sds(shape, F32)],
+            xs,
+            [pltpu.VMEM(shape, F32), pltpu.SemaphoreType.DMA((ksize,))],
+            anywhere=[1],
+            outside=True,
+            aliases={} if own else {1: 0},
+        )[0]
+
+    grad_kernel = finish(True, own_half)
+    grad_kernel = finish(False, other_half, grad_kernel)
     return (grad_hidden, grad_kernel)
 
 

time: 77.8 us -> 74.8 us (0.961)
  waiting for transfers between devices: 42.9 us -> 39.8 us
  Pallas kernels: 7.53 us -> 9.21 us
  local copies, waits for them, and re-layouts: 3.34 us -> 2.23 us
    ppermute x1, waiting for transfers between devices: 4.6 us -> 0.01 us  [along(): return lax.ppermute(x, 'space', pairs)]
    pallas_call x7 -> x8, Pallas kernels: 7.53 us -> 9.21 us  [call(): pl.pallas_call(kernel, out_shape=list(outs), in_specs=[ANY if i in anywhe...]
    ppermute x15, waiting for transfers between devices: 38.3 us -> 39.8 us  [flip(): return lax.ppermute(x, axis, [(i, i ^ bit) for i in range(size)])]
    unnamed x9 -> x8, local copies, waits for them, and re-layouts: 2.78 us -> 1.68 us
  transfers between devices with their start and end apart: 17 -> 17, of which waited for: 11 -> 9; matrix products, arithmetic and copies ran while one was open for 2% -> 2% of each run, Pallas kernels for 6% -> 8%
where the time goes in v5:
time: 74.8 us; the launch traced here: 74.5 us
  waiting for transfers between devices  39.8 us (53%)
  starting transfers between devices  21.3 us (28%)
  Pallas kernels  9.21 us (12%)
  local copies, waits for them, and re-layouts  2.23 us (3%)
  other arithmetic  1.12 us (1%)
  between operations  0.9 us (1%)
    ppermute x15, waiting for transfers between devices, flip(): return lax.ppermute(x, axis, [(i, i ^ bit) for i in range(size)])  39.8 us
    ppermute x15, starting transfers between devices, flip(): return lax.ppermute(x, axis, [(i, i ^ bit) for i in range(size)])  17.1 us
    pallas_call x8, Pallas kernels, call(): pl.pallas_call(kernel, out_shape=list(outs), in_specs=[ANY if i in anywhe...  9.21 us
    ppermute x1, starting transfers between devices, along(): return lax.ppermute(x, 'space', pairs)  3.5 us
    unnamed x8, local copies, waits for them, and re-layouts  1.68 us
  transfers between devices with their start and end apart: 17, of which 9 were waited for; matrix products, arithmetic and copies ran while one was open for 2% of the time, Pallas kernels for 8%

profile of v5, /device:TPU:0, one launch (start us, length us, event | category | flops | bytes accessed | tf_op | source)
XLA Modules:
  0.0 74.5 jit_solution(5937528914930199793)
XLA Ops:
  0.6 3.1 %collective-permute-start.1 = (bf16[1,72,2,1440]{3,2,1,0:T(2,128)(2,1)}, bf16[1,72,2,1440]{3,2,1,0:T(2,128)(2,1)S(1)}, u32[]{:S(2)}, u32[]{:S(2)}) collective-permute-start(bf16[1,72,2,1440]{3,2,1,0:T(2,128)(2,1)} %x_ref.1), channel_id=1, source_target_pairs={{0,2},{2,0},{1,3},{3,1},{4,6},{6,4},{5,7},{7,5},{8,10},{10,8},{9,1... | collective-permute-start | bytes 1244168 | tf_op jit(solution)/shard_map/ppermute | solution.py:291
  3.7 0.0 collective-permute-start
  3.7 10.4 %collective-permute-done.1.refs_1_ = bf16[1,72,2,1440]{3,2,1,0:T(2,128)(2,1)S(1)} collective-permute-done((bf16[1,72,2,1440]{3,2,1,0:T(2,128)(2,1)}, bf16[1,72,2,1440]{3,2,1,0:T(2,128)(2,1)S(1)}, u32[]{:S(2)}, u32[]{:S(2)}) %collective-permute-start.1) | collective-permute-done | bytes 414752 | tf_op jit(solution)/shard_map/ppermute | solution.py:291
  14.1 0.0 collective-permute-start.2
  14.1 1.7 %collective-permute-start.8 = (bf16[1,72,2,1440]{3,2,1,0:T(2,128)(2,1)}, bf16[1,72,2,1440]{3,2,1,0:T(2,128)(2,1)S(1)}, u32[]{:S(2)}, u32[]{:S(2)}) collective-permute-start(bf16[1,72,2,1440]{3,2,1,0:T(2,128)(2,1)} %own_ref.1), channel_id=1, source_target_pairs={{0,4},{4,0},{8,12},{12,8},{16,20},{20,16},{24,28},{28,24},{1,5},{5... | collective-permute-start | bytes 1244168 | tf_op jit(solution)/shard_map/ppermute | solution.py:291
  15.8 0.7 collective-permute-start.9
  16.5 0.9 %convert_element_type.48.refs_0_ = bf16[72,720]{1,0:T(8,128)(2,1)S(1)} convert(f32[72,720]{1,0:T(8,128)} %param.6) | non-fusion elementwise | flops 51840 | bytes 311040 | tf_op jit(solution)/shard_map/convert_element_type | solution.py:372
  17.4 1.6 %collective-permute-start.4 = (bf16[72,720]{1,0:T(8,128)(2,1)S(1)}, bf16[72,720]{1,0:T(8,128)(2,1)S(1)}, u32[]{:S(2)}, u32[]{:S(2)}) collective-permute-start(bf16[72,720]{1,0:T(8,128)(2,1)S(1)} %convert_element_type.48.refs_0_), channel_id=1, source_target_pairs={{0,2},{2,0},{1,3},{3,1},{4,6},{6,4},{5,7},{7,5},{8,10},{10,8},{9,1... | collective-permute-start | bytes 311048 | tf_op jit(solution)/shard_map/ppermute | solution.py:291
  19.0 3.7 %collective-permute-done.4.refs_2_ = bf16[72,720]{1,0:T(8,128)(2,1)S(1)} collective-permute-done((bf16[72,720]{1,0:T(8,128)(2,1)S(1)}, bf16[72,720]{1,0:T(8,128)(2,1)S(1)}, u32[]{:S(2)}, u32[]{:S(2)}) %collective-permute-start.4) | collective-permute-done | bytes 103712 | tf_op jit(solution)/shard_map/ppermute | solution.py:291
  22.7 0.0 collective-permute-start.3
  22.7 0.0 collective-permute-done.refs_0_
  22.7 0.5 collective-permute-start.5
  23.2 0.0 copy-start
  23.2 1.0 %copy-done = bf16[1,72,2,1440]{3,2,1,0:T(2,128)(2,1)S(1)} copy-done((bf16[1,72,2,1440]{3,2,1,0:T(2,128)(2,1)S(1)}, bf16[1,72,2,1440]{3,2,1,0:T(2,128)(2,1)}, u32[]{:S(2)}) %copy-start) | copy-done | bytes 414744
  24.2 0.0 copy-start.1
  24.2 0.7 copy-done.1
  24.9 0.4 shard_map.68
  25.3 0.0 collective-permute-done.2.refs_2_
  25.3 0.0 copy-start.2
  25.3 1.0 %shard_map.69.pair_ref = f32[144,1440]{1,0:T(8,128)S(1)} custom-call(f32[144,128]{1,0:T(8,128)S(1)} %get-tuple-element.6.s_ref, bf16[144,1440]{1,0:T(8,128)(2,1)S(1)} %get-tuple-element.7.own_ref, bf16[1,72,2,1440]{3,2,1,0:T(2,128)(2,1)S(1)} %collective-permute-done.refs_0_, bf16[1,72,2,1440]{3,2,1,0:T(2,128)(2,1)S(1)} %collective-permute-done.1.refs_1_, ...), custom_call_target="tpu_custom_call" | custom-call | bytes 2562048 | tf_op jit(solution)/shard_map/pallas_call | solution.py:39
  26.3 0.0 collective-permute-done.3.refs_1_
  26.3 0.0 collective-permute-done.5.refs_3_
  26.3 1.4 %shard_map.70.own_ref.g_ref = bf16[2,72,1536]{2,1,0:T(8,128)(2,1)S(1)} custom-call(f32[144,128]{1,0:T(8,128)S(1)} %get-tuple-element.6.s_ref, bf16[144,1440]{1,0:T(8,128)(2,1)S(1)} %get-tuple-element.7.own_ref, f32[144,1440]{1,0:T(8,128)S(1)} %shard_map.69.pair_ref, bf16[72,720]{1,0:T(8,128)(2,1)S(1)} %convert_element_type.48.refs_0_, ...), custom_call_target="tpu_custom_call" | custom-call | bytes 2174976 | tf_op jit(solution)/shard_map/pallas_call | solution.py:39
  27.7 0.0 copy-done.2
  27.7 1.1 %shard_map.72 = (bf16[2,384,1536]{2,1,0:T(8,128)(2,1)S(1)}, f32[144,768]{1,0:T(8,128)S(1)}) custom-call(bf16[2,72,1536]{2,1,0:T(8,128)(2,1)S(1)} %shard_map.70.own_ref.g_ref, bf16[1,72,2,1440]{3,2,1,0:T(2,128)(2,1)S(1)} %copy-done.2), custom_call_target="tpu_custom_call" | custom-call | flops 265420800 | bytes 3658752 | tf_op jit(solution)/shard_map/pallas_call | solution.py:39
  28.8 6.8 %collective-permute-done.8.near_ref = bf16[1,72,2,1440]{3,2,1,0:T(2,128)(2,1)S(1)} collective-permute-done((bf16[1,72,2,1440]{3,2,1,0:T(2,128)(2,1)}, bf16[1,72,2,1440]{3,2,1,0:T(2,128)(2,1)S(1)}, u32[]{:S(2)}, u32[]{:S(2)}) %collective-permute-start.8) | collective-permute-done | bytes 414752 | tf_op jit(solution)/shard_map/ppermute | solution.py:291
  35.7 0.0 collective-permute-done.9.far_ref
  35.7 0.0 copy-start.3
  35.7 1.0 %shard_map.73 = bf16[384,384]{1,0:T(8,128)(2,1)S(1)} custom-call(bf16[2,384,1536]{2,1,0:T(8,128)(2,1)S(1)} %get-tuple-element.8.shift_ref, f32[144,768]{1,0:T(8,128)S(1)} %get-tuple-element.9.own_ref, bf16[1,72,2,1440]{3,2,1,0:T(2,128)(2,1)S(1)} %collective-permute-done.8.near_ref, bf16[1,72,2,1440]{3,2,1,0:T(2,128)(2,1)S(1)} %collective-permute-done.9.far_ref), custom_call_target="tpu_custom_call" | custom-call | flops 530841600 | bytes 3926016 | tf_op jit(solution)/shard_map/pallas_call | solution.py:39
  36.7 0.1 collective-permute-start.10
  36.8 1.3 %collective-permute-done.10 = bf16[192,384]{1,0:T(8,128)(2,1)S(1)} collective-permute-done((bf16[192,384]{1,0:T(8,128)(2,1)S(1)}, bf16[192,384]{1,0:T(8,128)(2,1)S(1)}, u32[]{:S(2)}, u32[]{:S(2)}) %collective-permute-start.10) | collective-permute-done | bytes 147488 | tf_op jit(solution)/shard_map/ppermute | solution.py:291
  38.2 0.1 add_convert_fusion
  38.3 2.5 %collective-permute-start.11 = (bf16[96,384]{1,0:T(8,128)(2,1)S(1)}, bf16[96,384]{1,0:T(8,128)(2,1)S(1)}, u32[]{:S(2)}, u32[]{:S(2)}) collective-permute-start(bf16[96,384]{1,0:T(8,128)(2,1)S(1)} %constant_dynamic-slice_fusion), channel_id=1, source_target_pairs={{0,8},{4,12},{8,0},{12,4},{16,24},{20,28},{24,16},{28,20},{1,9},{5... | collective-permute-start | bytes 221192 | tf_op jit(solution)/shard_map/ppermute | solution.py:291
  40.8 2.6 %collective-permute-done.11 = bf16[96,384]{1,0:T(8,128)(2,1)S(1)} collective-permute-done((bf16[96,384]{1,0:T(8,128)(2,1)S(1)}, bf16[96,384]{1,0:T(8,128)(2,1)S(1)}, u32[]{:S(2)}, u32[]{:S(2)}) %collective-permute-start.11) | collective-permute-done | bytes 73760 | tf_op jit(solution)/shard_map/ppermute | solution.py:291
  43.4 2.9 %collective-permute-start.12 = (bf16[96,384]{1,0:T(8,128)(2,1)S(1)}, bf16[96,384]{1,0:T(8,128)(2,1)S(1)}, u32[]{:S(2)}, u32[]{:S(2)}) collective-permute-start(bf16[96,384]{1,0:T(8,128)(2,1)S(1)} %add_convert_fusion.4), channel_id=1, source_target_pairs={{0,16},{4,20},{8,24},{12,28},{16,0},{20,4},{24,8},{28,12},{1,17},{... | collective-permute-start | bytes 221192 | tf_op jit(solution)/shard_map/ppermute | solution.py:291
  46.3 1.5 %collective-permute-start.6 = (bf16[2,72,1536]{2,1,0:T(8,128)(2,1)S(1)}, bf16[2,72,1536]{2,1,0:T(8,128)(2,1)S(1)}, u32[]{:S(2)}, u32[]{:S(2)}) collective-permute-start(bf16[2,72,1536]{2,1,0:T(8,128)(2,1)S(1)} %shard_map.70.own_ref.g_ref), channel_id=1, source_target_pairs={{0,4},{4,0},{8,12},{12,8},{16,20},{20,16},{24,28},{28,24},{1,5},{5... | collective-permute-start | bytes 1327112 | tf_op jit(solution)/shard_map/ppermute | solution.py:291
  47.7 1.2 %collective-permute-done.12 = bf16[96,384]{1,0:T(8,128)(2,1)S(1)} collective-permute-done((bf16[96,384]{1,0:T(8,128)(2,1)S(1)}, bf16[96,384]{1,0:T(8,128)(2,1)S(1)}, u32[]{:S(2)}, u32[]{:S(2)}) %collective-permute-start.12) | collective-permute-done | bytes 73760 | tf_op jit(solution)/shard_map/ppermute | solution.py:291
  48.9 1.6 %collective-permute-start.13 = (bf16[96,384]{1,0:T(8,128)(2,1)S(1)}, bf16[96,384]{1,0:T(8,128)(2,1)S(1)}, u32[]{:S(2)}, u32[]{:S(2)}) collective-permute-start(bf16[96,384]{1,0:T(8,128)(2,1)S(1)} %add_convert_fusion.3), channel_id=1, source_target_pairs={{0,2},{2,0},{1,3},{3,1},{4,6},{6,4},{5,7},{7,5},{8,10},{10,8},{9,1... | collective-permute-start | bytes 221192 | tf_op jit(solution)/shard_map/ppermute | solution.py:291
  50.5 2.8 %collective-permute-done.13 = bf16[96,384]{1,0:T(8,128)(2,1)S(1)} collective-permute-done((bf16[96,384]{1,0:T(8,128)(2,1)S(1)}, bf16[96,384]{1,0:T(8,128)(2,1)S(1)}, u32[]{:S(2)}, u32[]{:S(2)}) %collective-permute-start.13) | collective-permute-done | bytes 73760 | tf_op jit(solution)/shard_map/ppermute | solution.py:291
  53.4 1.6 %collective-permute-start.14 = (bf16[96,384]{1,0:T(8,128)(2,1)S(1)}, bf16[96,384]{1,0:T(8,128)(2,1)S(1)}, u32[]{:S(2)}, u32[]{:S(2)}) collective-permute-start(bf16[96,384]{1,0:T(8,128)(2,1)S(1)} %add_convert_fusion.2), channel_id=1, source_target_pairs={{0,4},{4,0},{8,12},{12,8},{16,20},{20,16},{24,28},{28,24},{1,5},{5... | collective-permute-start | bytes 221192 | tf_op jit(solution)/shard_map/ppermute | solution.py:291
  54.9 2.9 %collective-permute-done.6.near_ref = bf16[2,72,1536]{2,1,0:T(8,128)(2,1)S(1)} collective-permute-done((bf16[2,72,1536]{2,1,0:T(8,128)(2,1)S(1)}, bf16[2,72,1536]{2,1,0:T(8,128)(2,1)S(1)}, u32[]{:S(2)}, u32[]{:S(2)}) %collective-permute-start.6) | collective-permute-done | bytes 442400 | tf_op jit(solution)/shard_map/ppermute | solution.py:291
  57.8 3.5 %collective-permute-start.7 = (bf16[2,72,1536]{2,1,0:T(8,128)(2,1)S(1)}, bf16[2,72,1536]{2,1,0:T(8,128)(2,1)S(1)}, u32[]{:S(2)}, u32[]{:S(2)}) collective-permute-start(bf16[2,72,1536]{2,1,0:T(8,128)(2,1)S(1)} %collective-permute-done.6.near_ref), channel_id=1, source_target_pairs={{0,8},{8,16},{16,24},{12,4},{20,12},{28,20},{1,9},{9,17},{17,25},{... | collective-permute-start | bytes 1327112 | tf_op jit(solution)/shard_map/ppermute | solution.py:298
  61.3 0.0 collective-permute-done.14
  61.4 0.1 collective-permute-start.15
  61.5 8.1 %collective-permute-done.15 = bf16[96,384]{1,0:T(8,128)(2,1)S(1)} collective-permute-done((bf16[96,384]{1,0:T(8,128)(2,1)S(1)}, bf16[96,384]{1,0:T(8,128)(2,1)S(1)}, u32[]{:S(2)}, u32[]{:S(2)}) %collective-permute-start.15) | collective-permute-done | bytes 73760 | tf_op jit(solution)/shard_map/ppermute | solution.py:291
  69.6 0.1 collective-permute-start.16
  69.6 0.0 copy-done.3
  69.7 0.1 copy.9
  69.8 0.4 reshape.7.w_ref
  70.2 1.0 %shard_map.74.refs_0_ = f32[5,5,72,72]{3,2,1,0:T(8,128)} custom-call(bf16[192,384]{1,0:T(8,128)(2,1)S(1)} %maximum_select_fusion.x_ref), custom_call_target="tpu_custom_call" | custom-call | bytes 665856 | tf_op jit(solution)/shard_map/pallas_call | solution.py:39
  71.1 0.0 collective-permute-done.16.x_ref
  71.2 0.9 %shard_map.75 = f32[5,5,72,72]{3,2,1,0:T(8,128)} custom-call(bf16[192,384]{1,0:T(8,128)(2,1)S(1)} %collective-permute-done.16.x_ref, f32[5,5,72,72]{3,2,1,0:T(8,128)} %shard_map.74.refs_0_), custom_call_target="tpu_custom_call", output_to_operand_aliasing={{}: (1, {})} | custom-call | bytes 1184256 | tf_op jit(solution)/shard_map/pallas_call | solution.py:39
  72.1 0.0 collective-permute-done.7.far_ref
  72.1 2.4 %shard_map.71 = bf16[1,72,2,1440]{3,2,1,0:T(2,128)(2,1)} custom-call(bf16[360,360]{1,0:T(8,128)(2,1)S(1)} %reshape.7.w_ref, bf16[2,72,1536]{2,1,0:T(8,128)(2,1)S(1)} %shard_map.70.own_ref.g_ref, bf16[2,72,1536]{2,1,0:T(8,128)(2,1)S(1)} %collective-permute-done.6.near_ref, bf16[2,72,1536]{2,1,0:T(8,128)(2,1)S(1)} %collective-permute-done.7.far_ref), custom_call_target="tpu_custom_call" | custom-call | flops 796262400 | bytes 2001024 | tf_op jit(solution)/shard_map/pallas_call | solution.py:39
  (7 shorter events, 0.2 us)
Async XLA Ops:
  0.6 13.4 %collective-permute-start.1 = (bf16[1,72,2,1440]{3,2,1,0:T(2,128)(2,1)}, bf16[1,72,2,1440]{3,2,1,0:T(2,128)(2,1)S(1)}, u32[]{:S(2)}, u32[]{:S(2)}) collective-permute-start(bf16[1,72,2,1440]{3,2,1,0:T(2,128)(2,1)} %x_ref.1), channel_id=1, source_target_pairs={{0,2},{2,0},{1,3},{3,1},{4,6},{6,4},{5,7},{7,5},{8,10},{10,8},{9,1... | collective-permute-start | bytes 1244168 | tf_op jit(solution)/shard_map/ppermute | solution.py:291
  3.7 19.0 %collective-permute-start = (bf16[1,72,2,1440]{3,2,1,0:T(2,128)(2,1)}, bf16[1,72,2,1440]{3,2,1,0:T(2,128)(2,1)S(1)}, u32[]{:S(2)}, u32[]{:S(2)}) collective-permute-start(bf16[1,72,2,1440]{3,2,1,0:T(2,128)(2,1)} %x_ref.1), channel_id=1, source_target_pairs={{0,1},{1,0},{2,3},{3,2},{4,5},{5,4},{6,7},{7,6},{8,9},{9,8},{10,11... | collective-permute-start | bytes 1244168 | tf_op jit(solution)/shard_map/ppermute | solution.py:291
  14.1 11.2 %collective-permute-start.2 = (bf16[1,72,2,1440]{3,2,1,0:T(2,128)(2,1)S(1)}, bf16[1,72,2,1440]{3,2,1,0:T(2,128)(2,1)S(1)}, u32[]{:S(2)}, u32[]{:S(2)}) collective-permute-start(bf16[1,72,2,1440]{3,2,1,0:T(2,128)(2,1)S(1)} %collective-permute-done.1.refs_1_), channel_id=1, source_target_pairs={{0,1},{1,0},{2,3},{3,2},{4,5},{5,4},{6,7},{7,6},{8,9},{9,8},{10,11... | collective-permute-start | bytes 1244168 | tf_op jit(solution)/shard_map/ppermute | solution.py:291
  14.1 21.6 %collective-permute-start.8 = (bf16[1,72,2,1440]{3,2,1,0:T(2,128)(2,1)}, bf16[1,72,2,1440]{3,2,1,0:T(2,128)(2,1)S(1)}, u32[]{:S(2)}, u32[]{:S(2)}) collective-permute-start(bf16[1,72,2,1440]{3,2,1,0:T(2,128)(2,1)} %own_ref.1), channel_id=1, source_target_pairs={{0,4},{4,0},{8,12},{12,8},{16,20},{20,16},{24,28},{28,24},{1,5},{5... | collective-permute-start | bytes 1244168 | tf_op jit(solution)/shard_map/ppermute | solution.py:291
  15.8 19.9 %collective-permute-start.9 = (bf16[1,72,2,1440]{3,2,1,0:T(2,128)(2,1)}, bf16[1,72,2,1440]{3,2,1,0:T(2,128)(2,1)S(1)}, u32[]{:S(2)}, u32[]{:S(2)}) collective-permute-start(bf16[1,72,2,1440]{3,2,1,0:T(2,128)(2,1)} %own_ref.1), channel_id=1, source_target_pairs={{4,8},{12,16},{20,24},{8,4},{16,12},{24,20},{5,9},{13,17},{21,25},... | collective-permute-start | bytes 1244168 | tf_op jit(solution)/shard_map/ppermute | solution.py:305
  17.4 5.3 %collective-permute-start.4 = (bf16[72,720]{1,0:T(8,128)(2,1)S(1)}, bf16[72,720]{1,0:T(8,128)(2,1)S(1)}, u32[]{:S(2)}, u32[]{:S(2)}) collective-permute-start(bf16[72,720]{1,0:T(8,128)(2,1)S(1)} %convert_element_type.48.refs_0_), channel_id=1, source_target_pairs={{0,2},{2,0},{1,3},{3,1},{4,6},{6,4},{5,7},{7,5},{8,10},{10,8},{9,1... | collective-permute-start | bytes 311048 | tf_op jit(solution)/shard_map/ppermute | solution.py:291
  22.7 3.6 %collective-permute-start.3 = (bf16[72,720]{1,0:T(8,128)(2,1)S(1)}, bf16[72,720]{1,0:T(8,128)(2,1)S(1)}, u32[]{:S(2)}, u32[]{:S(2)}) collective-permute-start(bf16[72,720]{1,0:T(8,128)(2,1)S(1)} %convert_element_type.48.refs_0_), channel_id=1, source_target_pairs={{0,1},{1,0},{2,3},{3,2},{4,5},{5,4},{6,7},{7,6},{8,9},{9,8},{10,11... | collective-permute-start | bytes 311048 | tf_op jit(solution)/shard_map/ppermute | solution.py:291
  22.7 3.6 %collective-permute-start.5 = (bf16[72,720]{1,0:T(8,128)(2,1)S(1)}, bf16[72,720]{1,0:T(8,128)(2,1)S(1)}, u32[]{:S(2)}, u32[]{:S(2)}) collective-permute-start(bf16[72,720]{1,0:T(8,128)(2,1)S(1)} %collective-permute-done.4.refs_2_), channel_id=1, source_target_pairs={{0,1},{1,0},{2,3},{3,2},{4,5},{5,4},{6,7},{7,6},{8,9},{9,8},{10,11... | collective-permute-start | bytes 311048 | tf_op jit(solution)/shard_map/ppermute | solution.py:291
  23.2 1.0 %copy-start = (bf16[1,72,2,1440]{3,2,1,0:T(2,128)(2,1)S(1)}, bf16[1,72,2,1440]{3,2,1,0:T(2,128)(2,1)}, u32[]{:S(2)}) copy-start(bf16[1,72,2,1440]{3,2,1,0:T(2,128)(2,1)} %x_ref.1) | copy-start | bytes 1244164
  24.2 0.7 copy-start.1
  25.3 2.4 %copy-start.2 = (bf16[1,72,2,1440]{3,2,1,0:T(2,128)(2,1)S(1)}, bf16[1,72,2,1440]{3,2,1,0:T(2,128)(2,1)}, u32[]{:S(2)}) copy-start(bf16[1,72,2,1440]{3,2,1,0:T(2,128)(2,1)} %own_ref.1) | copy-start | bytes 1244164
  35.7 34.0 %copy-start.3 = (bf16[5,5,72,72]{3,2,1,0:T(8,128)(2,1)S(1)}, bf16[5,5,72,72]{3,2,1,0:T(8,128)(2,1)}, u32[]{:S(2)}) copy-start(bf16[5,5,72,72]{3,2,1,0:T(8,128)(2,1)} %param.9) | copy-start | bytes 777604
  36.7 1.4 %collective-permute-start.10 = (bf16[192,384]{1,0:T(8,128)(2,1)S(1)}, bf16[192,384]{1,0:T(8,128)(2,1)S(1)}, u32[]{:S(2)}, u32[]{:S(2)}) collective-permute-start(bf16[192,384]{1,0:T(8,128)(2,1)S(1)} %constant_dynamic-slice_fusion.1), channel_id=1, source_target_pairs={{0,1},{1,0},{2,3},{3,2},{4,5},{5,4},{6,7},{7,6},{8,9},{9,8},{10,11... | collective-permute-start | bytes 442376 | tf_op jit(solution)/shard_map/ppermute | solution.py:291
  38.3 5.1 %collective-permute-start.11 = (bf16[96,384]{1,0:T(8,128)(2,1)S(1)}, bf16[96,384]{1,0:T(8,128)(2,1)S(1)}, u32[]{:S(2)}, u32[]{:S(2)}) collective-permute-start(bf16[96,384]{1,0:T(8,128)(2,1)S(1)} %constant_dynamic-slice_fusion), channel_id=1, source_target_pairs={{0,8},{4,12},{8,0},{12,4},{16,24},{20,28},{24,16},{28,20},{1,9},{5... | collective-permute-start | bytes 221192 | tf_op jit(solution)/shard_map/ppermute | solution.py:291
  43.4 5.5 %collective-permute-start.12 = (bf16[96,384]{1,0:T(8,128)(2,1)S(1)}, bf16[96,384]{1,0:T(8,128)(2,1)S(1)}, u32[]{:S(2)}, u32[]{:S(2)}) collective-permute-start(bf16[96,384]{1,0:T(8,128)(2,1)S(1)} %add_convert_fusion.4), channel_id=1, source_target_pairs={{0,16},{4,20},{8,24},{12,28},{16,0},{20,4},{24,8},{28,12},{1,17},{... | collective-permute-start | bytes 221192 | tf_op jit(solution)/shard_map/ppermute | solution.py:291
  46.3 11.6 %collective-permute-start.6 = (bf16[2,72,1536]{2,1,0:T(8,128)(2,1)S(1)}, bf16[2,72,1536]{2,1,0:T(8,128)(2,1)S(1)}, u32[]{:S(2)}, u32[]{:S(2)}) collective-permute-start(bf16[2,72,1536]{2,1,0:T(8,128)(2,1)S(1)} %shard_map.70.own_ref.g_ref), channel_id=1, source_target_pairs={{0,4},{4,0},{8,12},{12,8},{16,20},{20,16},{24,28},{28,24},{1,5},{5... | collective-permute-start | bytes 1327112 | tf_op jit(solution)/shard_map/ppermute | solution.py:291
  48.9 4.4 %collective-permute-start.13 = (bf16[96,384]{1,0:T(8,128)(2,1)S(1)}, bf16[96,384]{1,0:T(8,128)(2,1)S(1)}, u32[]{:S(2)}, u32[]{:S(2)}) collective-permute-start(bf16[96,384]{1,0:T(8,128)(2,1)S(1)} %add_convert_fusion.3), channel_id=1, source_target_pairs={{0,2},{2,0},{1,3},{3,1},{4,6},{6,4},{5,7},{7,5},{8,10},{10,8},{9,1... | collective-permute-start | bytes 221192 | tf_op jit(solution)/shard_map/ppermute | solution.py:291
  53.4 8.0 %collective-permute-start.14 = (bf16[96,384]{1,0:T(8,128)(2,1)S(1)}, bf16[96,384]{1,0:T(8,128)(2,1)S(1)}, u32[]{:S(2)}, u32[]{:S(2)}) collective-permute-start(bf16[96,384]{1,0:T(8,128)(2,1)S(1)} %add_convert_fusion.2), channel_id=1, source_target_pairs={{0,4},{4,0},{8,12},{12,8},{16,20},{20,16},{24,28},{28,24},{1,5},{5... | collective-permute-start | bytes 221192 | tf_op jit(solution)/shard_map/ppermute | solution.py:291
  57.8 14.3 %collective-permute-start.7 = (bf16[2,72,1536]{2,1,0:T(8,128)(2,1)S(1)}, bf16[2,72,1536]{2,1,0:T(8,128)(2,1)S(1)}, u32[]{:S(2)}, u32[]{:S(2)}) collective-permute-start(bf16[2,72,1536]{2,1,0:T(8,128)(2,1)S(1)} %collective-permute-done.6.near_ref), channel_id=1, source_target_pairs={{0,8},{8,16},{16,24},{12,4},{20,12},{28,20},{1,9},{9,17},{17,25},{... | collective-permute-start | bytes 1327112 | tf_op jit(solution)/shard_map/ppermute | solution.py:298
  61.4 8.2 %collective-permute-start.15 = (bf16[96,384]{1,0:T(8,128)(2,1)S(1)}, bf16[96,384]{1,0:T(8,128)(2,1)S(1)}, u32[]{:S(2)}, u32[]{:S(2)}) collective-permute-start(bf16[96,384]{1,0:T(8,128)(2,1)S(1)} %add_convert_fusion.1), channel_id=1, source_target_pairs={{0,8},{4,12},{8,0},{12,4},{16,24},{20,28},{24,16},{28,20},{1,9},{5... | collective-permute-start | bytes 221192 | tf_op jit(solution)/shard_map/ppermute | solution.py:291
  69.6 1.6 %collective-permute-start.16 = (bf16[192,384]{1,0:T(8,128)(2,1)S(1)}, bf16[192,384]{1,0:T(8,128)(2,1)S(1)}, u32[]{:S(2)}, u32[]{:S(2)}) collective-permute-start(bf16[192,384]{1,0:T(8,128)(2,1)S(1)} %maximum_select_fusion.x_ref), channel_id=1, source_target_pairs={{0,1},{1,0},{2,3},{3,2},{4,5},{5,4},{6,7},{7,6},{8,9},{9,8},{10,11... | collective-permute-start | bytes 442376 | tf_op jit(solution)/shard_map/ppermute | solution.py:291

commit v6 on v5

--- a/solution.py
+++ b/solution.py
@@ -101,16 +101,19 @@
     return x.reshape(x.shape[0] // 8, 8, x.shape[1])
 
 
-def pair_kernel(rows, s_ref, own_ref, *refs):
+def pair_kernel(rows, begun, s_ref, own_ref, *refs):
     *others, o_ref, mix_scr = refs
+    sum_ref = others.pop() if begun else None
     for d, other in enumerate(others):
         mix_scr[d] = mixed(other)
     for low, high in tiles(mix_scr.shape[2]):
         sq = blocks(s_ref[:, : high - low])
         own = blocks(own_ref[:, low:high].astype(F32))
-        self_inverse = 1.0 / jnp.sqrt(smoothing)
+        self_inverse = 0.0 if begun else 1.0 / jnp.sqrt(smoothing)
         total = jnp.full(own.shape[1:], self_inverse, F32)
         mixture = own * self_inverse
+        if begun:
+            mixture = mixture - blocks(sum_ref[:, low:high])
         for d in range(len(others)):
             other = blocks(mix_scr[d, :, low:high].astype(F32))
             diff = own - other
@@ -258,32 +261,42 @@
     o_ref[0] = mix_scr[...].reshape(channels, rows, width)
 
 
-def final_kernel(ksize, channels, norm, own, x_ref, *refs):
-    o_ref, scr, sem = refs[-3:]
-    n = x_ref.shape[0]
-    half = lax.axis_index("core") % 2
-    half = half if own else 1 - half
-    for h in range(2):
-
-        @pl.when(half == h)
-        def _():
-            copies = []
-            for i in range(ksize):
-                low = max(i * channels, h * n)
-                high = min((i + 1) * channels, (h + 1) * n)
-                if low >= high:
-                    continue
-                a, rows = ksize - 1 - i, slice(low - i * channels, high - i * channels)
-                for b in range(ksize):
-                    x = x_ref[low - h * n : high - h * n, b * channels : (b + 1) * channels]
-                    scr[a, b, rows] = x.astype(F32) * norm
-                at = (a, slice(None), pl.ds(rows.start, high - low))
-                copies.append(
-                    pltpu.make_async_copy(scr.at[at], o_ref.at[at], sem.at[a])
-                )
-                copies[-1].start()
-            for copy in copies:
-                copy.wait()
+def final_kernel(ksize, channels, norm, pieces, *refs):
+    xs, (o_ref, scr, sem) = refs[: len(pieces)], refs[-3:]
+    core = lax.axis_index("core")
+    end = lax.axis_index("space") // 2
+    n = xs[0].shape[0]
+    for wait in (False, True):
+        for k, (other, second) in enumerate(pieces):
+            quarter = 2 * ((core + other) % 2) + (end + second) % 2
+            for q in range(4):
+
+                @pl.when(quarter == q)
+                def _(k=k, q=q):
+                    x_ref = xs[k]
+                    slot = 0
+                    for i in range(ksize):
+                        low = max(i * channels, q * n)
+                        high = min((i + 1) * channels, (q + 1) * n)
+                        if low >= high:
+                            continue
+                        first = low - i * channels
+                        at = (ksize - 1 - i, slice(None), pl.ds(first, high - low))
+                        copy = pltpu.make_async_copy(
+                            scr.at[at], o_ref.at[at], sem.at[k, slot]
+                        )
+                        slot += 1
+                        if wait:
+                            copy.wait()
+                            continue
+                        rows = slice(first, first + high - low)
+                        for b in range(ksize):
+                            x = x_ref[
+                                low - q * n : high - q * n,
+                                b * channels : (b + 1) * channels,
+                            ]
+                            scr[ksize - 1 - i, b, rows] = x.astype(F32) * norm
+                        copy.start()
 
 
 def flip(x, axis, bit):
@@ -326,13 +339,6 @@
     keep = lax.dynamic_slice_in_dim(x, high * n, n, 0)
     give = lax.dynamic_slice_in_dim(x, (1 - high) * n, n, 0)
     return add(keep, flip(give, axis, bit))
-
-
-def join(x, axis, bit):
-    other = flip(x, axis, bit)
-    both = jnp.concatenate([x, other], axis=0)
-    swapped = jnp.concatenate([other, x], axis=0)
-    return jnp.where(own_bit(axis, bit) == 0, both, swapped)
 
 
 def reduce_all(x):
@@ -343,8 +349,10 @@
     rest += [("chip", b) for b in bits("chip")] + [("space", 1)]
     for axis in rest:
         x = add(x, flip(x, *axis))
-    x = join(x, *first)
-    return x, flip(x, *core)
+    y = flip(x, *first)
+    x_other = flip(x, *core)
+    y_other = flip(y, *core)
+    return (x, y), (x_other, y_other)
 
 
 def body(prediction_maps, truth_analysis, reciprocal_spread, deconv_inputs, filter_tensor):
@@ -383,20 +391,27 @@
         ],
         anywhere=[0, 1],
     )
-    taps = jnp.transpose(filter_tensor, (1, 2, 0, 3)).reshape(ksize * channels, ksize * channels)
+    taps = jnp.transpose(filter_tensor, (1, 2, 0, 3)).reshape(
+        ksize * channels, ksize * channels
+    )
     arrived, seen = [], []
     for i, (x, t) in enumerate(zip(fields, truths)):
         arrived += [x, core(x)] if i else [core(x)]
         seen += [t, core(t)]
 
     table = [float(v) for v in area_weights(rows_total)]
-    paired = call(
-        functools.partial(pair_kernel, rows),
-        [sds((mix, width), F32)],
-        [scale, own, *arrived],
-        [pltpu.VMEM((members - 1, mix, width), BF)],
-        spare=max(3, members) << 20,
-    )[0]
+
+    def pairs(others, so_far):
+        return call(
+            functools.partial(pair_kernel, rows, bool(so_far)),
+            [sds((mix, width), F32)],
+            [scale, own, *others, *so_far],
+            [pltpu.VMEM((len(others), mix, width), BF)],
+            spare=max(3, members) << 20,
+        )[0]
+
+    paired = pairs(arrived[:-1], ())
+    paired = pairs(arrived[-1:], (paired,))
     grad = call(
         functools.partial(energy_kernel, span, members, table),
         [slab],
@@ -429,7 +444,7 @@
         [pltpu.VMEM((3, rows * packed // LANES, mix, LANES), F32)],
         flops * 2 // 3,
     )[0]
-    own_half, other_half = reduce_all(partial)
+    early, late = reduce_all(partial)
 
     grad_hidden = call(
         functools.partial(conv_kernel, ksize),
@@ -446,19 +461,20 @@
     norm = 1.0 / float(members * rows_total * width) ** 0.5
     shape = (ksize, ksize, channels, channels)
 
-    def finish(own, *xs):
+    def finish(pieces, *xs):
+        count = len(pieces)
         return call(
-            functools.partial(final_kernel, ksize, channels, norm, own),
+            functools.partial(final_kernel, ksize, channels, norm, pieces),
             [sds(shape, F32)],
             xs,
-            [pltpu.VMEM(shape, F32), pltpu.SemaphoreType.DMA((ksize,))],
-            anywhere=[1],
+            [pltpu.VMEM(shape, F32), pltpu.SemaphoreType.DMA((count, 3))],
+            anywhere=range(count, len(xs)),
             outside=True,
-            aliases={} if own else {1: 0},
+            aliases={count: 0} if len(xs) > count else {},
         )[0]
 
-    grad_kernel = finish(True, own_half)
-    grad_kernel = finish(False, other_half, grad_kernel)
+    grad_kernel = finish([(0, 0), (0, 1)], *early)
+    grad_kernel = finish([(1, 0), (1, 1)], *late, grad_kernel)
     return (grad_hidden, grad_kernel)
 
 

time: 74.8 us -> 74.9 us (level)
    pallas_call x8 -> x9, Pallas kernels: 9.21 us -> 9.65 us  [call(): pl.pallas_call(kernel, out_shape=list(outs), in_specs=[ANY if i in anywhe...]
    ppermute x15 -> x16, waiting for transfers between devices: 39.8 us -> 39.5 us  [flip(): return lax.ppermute(x, axis, [(i, i ^ bit) for i in range(size)])]
    ppermute x15 -> x16, starting transfers between devices: 17.1 us -> 17.1 us  [flip(): return lax.ppermute(x, axis, [(i, i ^ bit) for i in range(size)])]
  transfers between devices with their start and end apart: 17 -> 18, of which waited for: 9 -> 9; matrix products, arithmetic and copies ran while one was open for 2% -> 2% of each run, Pallas kernels for 8% -> 8%
where the time goes in v6:
time: 74.9 us; the launch traced here: 74.6 us
  waiting for transfers between devices  39.5 us (53%)
  starting transfers between devices  21.3 us (28%)
  Pallas kernels  9.65 us (13%)
  local copies, waits for them, and re-layouts  2.23 us (3%)
  other arithmetic  1.09 us (1%)
  between operations  0.89 us (1%)
    ppermute x16, waiting for transfers between devices, flip(): return lax.ppermute(x, axis, [(i, i ^ bit) for i in range(size)])  39.5 us
    ppermute x16, starting transfers between devices, flip(): return lax.ppermute(x, axis, [(i, i ^ bit) for i in range(size)])  17.1 us
    pallas_call x9, Pallas kernels, call(): pl.pallas_call(kernel, out_shape=list(outs), in_specs=[ANY if i in anywhe...  9.65 us
    ppermute x1, starting transfers between devices, along(): return lax.ppermute(x, 'space', pairs)  3.5 us
    unnamed x8, local copies, waits for them, and re-layouts  1.68 us
  transfers between devices with their start and end apart: 18, of which 9 were waited for; matrix products, arithmetic and copies ran while one was open for 2% of the time, Pallas kernels for 8%

profile of v6, /device:TPU:0, one launch (start us, length us, event | category | flops | bytes accessed | tf_op | source)
XLA Modules:
  0.0 74.6 jit_solution(2806184771604137236)
XLA Ops:
  0.6 3.1 %collective-permute-start = (bf16[1,72,2,1440]{3,2,1,0:T(2,128)(2,1)}, bf16[1,72,2,1440]{3,2,1,0:T(2,128)(2,1)S(1)}, u32[]{:S(2)}, u32[]{:S(2)}) collective-permute-start(bf16[1,72,2,1440]{3,2,1,0:T(2,128)(2,1)} %x_ref.1), channel_id=1, source_target_pairs={{0,2},{2,0},{1,3},{3,1},{4,6},{6,4},{5,7},{7,5},{8,10},{10,8},{9,1... | collective-permute-start | bytes 1244168 | tf_op jit(solution)/shard_map/ppermute | solution.py:304
  3.7 0.0 collective-permute-start.2
  3.7 10.4 %collective-permute-done.refs_1_ = bf16[1,72,2,1440]{3,2,1,0:T(2,128)(2,1)S(1)} collective-permute-done((bf16[1,72,2,1440]{3,2,1,0:T(2,128)(2,1)}, bf16[1,72,2,1440]{3,2,1,0:T(2,128)(2,1)S(1)}, u32[]{:S(2)}, u32[]{:S(2)}) %collective-permute-start) | collective-permute-done | bytes 414752 | tf_op jit(solution)/shard_map/ppermute | solution.py:304
  14.1 0.0 collective-permute-start.1
  14.1 1.7 %collective-permute-start.8 = (bf16[1,72,2,1440]{3,2,1,0:T(2,128)(2,1)}, bf16[1,72,2,1440]{3,2,1,0:T(2,128)(2,1)S(1)}, u32[]{:S(2)}, u32[]{:S(2)}) collective-permute-start(bf16[1,72,2,1440]{3,2,1,0:T(2,128)(2,1)} %own_ref.1), channel_id=1, source_target_pairs={{0,4},{4,0},{8,12},{12,8},{16,20},{20,16},{24,28},{28,24},{1,5},{5... | collective-permute-start | bytes 1244168 | tf_op jit(solution)/shard_map/ppermute | solution.py:304
  15.8 0.7 collective-permute-start.9
  16.5 0.9 %convert_element_type.48.refs_0_ = bf16[72,720]{1,0:T(8,128)(2,1)S(1)} convert(f32[72,720]{1,0:T(8,128)} %param.6) | non-fusion elementwise | flops 51840 | bytes 311040 | tf_op jit(solution)/shard_map/convert_element_type | solution.py:380
  17.4 1.6 %collective-permute-start.4 = (bf16[72,720]{1,0:T(8,128)(2,1)S(1)}, bf16[72,720]{1,0:T(8,128)(2,1)S(1)}, u32[]{:S(2)}, u32[]{:S(2)}) collective-permute-start(bf16[72,720]{1,0:T(8,128)(2,1)S(1)} %convert_element_type.48.refs_0_), channel_id=1, source_target_pairs={{0,2},{2,0},{1,3},{3,1},{4,6},{6,4},{5,7},{7,5},{8,10},{10,8},{9,1... | collective-permute-start | bytes 311048 | tf_op jit(solution)/shard_map/ppermute | solution.py:304
  19.0 3.7 %collective-permute-done.4.refs_2_ = bf16[72,720]{1,0:T(8,128)(2,1)S(1)} collective-permute-done((bf16[72,720]{1,0:T(8,128)(2,1)S(1)}, bf16[72,720]{1,0:T(8,128)(2,1)S(1)}, u32[]{:S(2)}, u32[]{:S(2)}) %collective-permute-start.4) | collective-permute-done | bytes 103712 | tf_op jit(solution)/shard_map/ppermute | solution.py:304
  22.7 0.0 collective-permute-start.3
  22.7 0.0 collective-permute-done.2.refs_0_
  22.7 0.5 collective-permute-start.5
  23.2 0.0 copy-start
  23.2 1.0 %copy-done = bf16[1,72,2,1440]{3,2,1,0:T(2,128)(2,1)S(1)} copy-done((bf16[1,72,2,1440]{3,2,1,0:T(2,128)(2,1)S(1)}, bf16[1,72,2,1440]{3,2,1,0:T(2,128)(2,1)}, u32[]{:S(2)}) %copy-start) | copy-done | bytes 414744
  24.2 0.0 copy-start.1
  24.2 0.7 copy-done.1
  24.9 0.4 shard_map.68
  25.3 0.7 shard_map.69.refs_1_
  26.0 0.0 copy-start.2
  26.0 0.0 collective-permute-done.1.refs_0_
  26.0 0.5 shard_map.70.pair_ref
  26.5 0.0 collective-permute-done.3.refs_1_
  26.5 0.0 collective-permute-done.5.refs_3_
  26.6 1.4 %shard_map.71.own_ref.g_ref = bf16[2,72,1536]{2,1,0:T(8,128)(2,1)S(1)} custom-call(f32[144,128]{1,0:T(8,128)S(1)} %get-tuple-element.6.s_ref, bf16[144,1440]{1,0:T(8,128)(2,1)S(1)} %get-tuple-element.7.own_ref, f32[144,1440]{1,0:T(8,128)S(1)} %shard_map.70.pair_ref, bf16[72,720]{1,0:T(8,128)(2,1)S(1)} %convert_element_type.48.refs_0_, ...), custom_call_target="tpu_custom_call" | custom-call | bytes 2174976 | tf_op jit(solution)/shard_map/pallas_call | solution.py:39
  28.0 0.0 copy-done.2
  28.0 1.1 %shard_map.73 = (bf16[2,384,1536]{2,1,0:T(8,128)(2,1)S(1)}, f32[144,768]{1,0:T(8,128)S(1)}) custom-call(bf16[2,72,1536]{2,1,0:T(8,128)(2,1)S(1)} %shard_map.71.own_ref.g_ref, bf16[1,72,2,1440]{3,2,1,0:T(2,128)(2,1)S(1)} %copy-done.2), custom_call_target="tpu_custom_call" | custom-call | flops 265420800 | bytes 3658752 | tf_op jit(solution)/shard_map/pallas_call | solution.py:39
  29.1 6.6 %collective-permute-done.8.near_ref = bf16[1,72,2,1440]{3,2,1,0:T(2,128)(2,1)S(1)} collective-permute-done((bf16[1,72,2,1440]{3,2,1,0:T(2,128)(2,1)}, bf16[1,72,2,1440]{3,2,1,0:T(2,128)(2,1)S(1)}, u32[]{:S(2)}, u32[]{:S(2)}) %collective-permute-start.8) | collective-permute-done | bytes 414752 | tf_op jit(solution)/shard_map/ppermute | solution.py:304
  35.7 0.0 collective-permute-done.9.far_ref
  35.7 0.0 copy-start.3
  35.7 1.0 %shard_map.74 = bf16[384,384]{1,0:T(8,128)(2,1)S(1)} custom-call(bf16[2,384,1536]{2,1,0:T(8,128)(2,1)S(1)} %get-tuple-element.8.shift_ref, f32[144,768]{1,0:T(8,128)S(1)} %get-tuple-element.9.own_ref, bf16[1,72,2,1440]{3,2,1,0:T(2,128)(2,1)S(1)} %collective-permute-done.8.near_ref, bf16[1,72,2,1440]{3,2,1,0:T(2,128)(2,1)S(1)} %collective-permute-done.9.far_ref), custom_call_target="tpu_custom_call" | custom-call | flops 530841600 | bytes 3926016 | tf_op jit(solution)/shard_map/pallas_call | solution.py:39
  36.7 0.1 collective-permute-start.10
  36.8 1.3 %collective-permute-done.10 = bf16[192,384]{1,0:T(8,128)(2,1)S(1)} collective-permute-done((bf16[192,384]{1,0:T(8,128)(2,1)S(1)}, bf16[192,384]{1,0:T(8,128)(2,1)S(1)}, u32[]{:S(2)}, u32[]{:S(2)}) %collective-permute-start.10) | collective-permute-done | bytes 147488 | tf_op jit(solution)/shard_map/ppermute | solution.py:304
  38.3 2.5 %collective-permute-start.11 = (bf16[96,384]{1,0:T(8,128)(2,1)S(1)}, bf16[96,384]{1,0:T(8,128)(2,1)S(1)}, u32[]{:S(2)}, u32[]{:S(2)}) collective-permute-start(bf16[96,384]{1,0:T(8,128)(2,1)S(1)} %constant_dynamic-slice_fusion), channel_id=1, source_target_pairs={{0,8},{4,12},{8,0},{12,4},{16,24},{20,28},{24,16},{28,20},{1,9},{5... | collective-permute-start | bytes 221192 | tf_op jit(solution)/shard_map/ppermute | solution.py:304
  40.8 2.6 %collective-permute-done.11 = bf16[96,384]{1,0:T(8,128)(2,1)S(1)} collective-permute-done((bf16[96,384]{1,0:T(8,128)(2,1)S(1)}, bf16[96,384]{1,0:T(8,128)(2,1)S(1)}, u32[]{:S(2)}, u32[]{:S(2)}) %collective-permute-start.11) | collective-permute-done | bytes 73760 | tf_op jit(solution)/shard_map/ppermute | solution.py:304
  43.4 2.9 %collective-permute-start.12 = (bf16[96,384]{1,0:T(8,128)(2,1)S(1)}, bf16[96,384]{1,0:T(8,128)(2,1)S(1)}, u32[]{:S(2)}, u32[]{:S(2)}) collective-permute-start(bf16[96,384]{1,0:T(8,128)(2,1)S(1)} %add_convert_fusion.4), channel_id=1, source_target_pairs={{0,16},{4,20},{8,24},{12,28},{16,0},{20,4},{24,8},{28,12},{1,17},{... | collective-permute-start | bytes 221192 | tf_op jit(solution)/shard_map/ppermute | solution.py:304
  46.3 1.5 %collective-permute-start.6 = (bf16[2,72,1536]{2,1,0:T(8,128)(2,1)S(1)}, bf16[2,72,1536]{2,1,0:T(8,128)(2,1)S(1)}, u32[]{:S(2)}, u32[]{:S(2)}) collective-permute-start(bf16[2,72,1536]{2,1,0:T(8,128)(2,1)S(1)} %shard_map.71.own_ref.g_ref), channel_id=1, source_target_pairs={{0,4},{4,0},{8,12},{12,8},{16,20},{20,16},{24,28},{28,24},{1,5},{5... | collective-permute-start | bytes 1327112 | tf_op jit(solution)/shard_map/ppermute | solution.py:304
  47.7 1.2 %collective-permute-done.12 = bf16[96,384]{1,0:T(8,128)(2,1)S(1)} collective-permute-done((bf16[96,384]{1,0:T(8,128)(2,1)S(1)}, bf16[96,384]{1,0:T(8,128)(2,1)S(1)}, u32[]{:S(2)}, u32[]{:S(2)}) %collective-permute-start.12) | collective-permute-done | bytes 73760 | tf_op jit(solution)/shard_map/ppermute | solution.py:304
  48.9 1.6 %collective-permute-start.13 = (bf16[96,384]{1,0:T(8,128)(2,1)S(1)}, bf16[96,384]{1,0:T(8,128)(2,1)S(1)}, u32[]{:S(2)}, u32[]{:S(2)}) collective-permute-start(bf16[96,384]{1,0:T(8,128)(2,1)S(1)} %add_convert_fusion.3), channel_id=1, source_target_pairs={{0,2},{2,0},{1,3},{3,1},{4,6},{6,4},{5,7},{7,5},{8,10},{10,8},{9,1... | collective-permute-start | bytes 221192 | tf_op jit(solution)/shard_map/ppermute | solution.py:304
  50.5 2.8 %collective-permute-done.13 = bf16[96,384]{1,0:T(8,128)(2,1)S(1)} collective-permute-done((bf16[96,384]{1,0:T(8,128)(2,1)S(1)}, bf16[96,384]{1,0:T(8,128)(2,1)S(1)}, u32[]{:S(2)}, u32[]{:S(2)}) %collective-permute-start.13) | collective-permute-done | bytes 73760 | tf_op jit(solution)/shard_map/ppermute | solution.py:304
  53.4 1.6 %collective-permute-start.14 = (bf16[96,384]{1,0:T(8,128)(2,1)S(1)}, bf16[96,384]{1,0:T(8,128)(2,1)S(1)}, u32[]{:S(2)}, u32[]{:S(2)}) collective-permute-start(bf16[96,384]{1,0:T(8,128)(2,1)S(1)} %add_convert_fusion.2), channel_id=1, source_target_pairs={{0,4},{4,0},{8,12},{12,8},{16,20},{20,16},{24,28},{28,24},{1,5},{5... | collective-permute-start | bytes 221192 | tf_op jit(solution)/shard_map/ppermute | solution.py:304
  54.9 2.9 %collective-permute-done.6.near_ref = bf16[2,72,1536]{2,1,0:T(8,128)(2,1)S(1)} collective-permute-done((bf16[2,72,1536]{2,1,0:T(8,128)(2,1)S(1)}, bf16[2,72,1536]{2,1,0:T(8,128)(2,1)S(1)}, u32[]{:S(2)}, u32[]{:S(2)}) %collective-permute-start.6) | collective-permute-done | bytes 442400 | tf_op jit(solution)/shard_map/ppermute | solution.py:304
  57.8 3.5 %collective-permute-start.7 = (bf16[2,72,1536]{2,1,0:T(8,128)(2,1)S(1)}, bf16[2,72,1536]{2,1,0:T(8,128)(2,1)S(1)}, u32[]{:S(2)}, u32[]{:S(2)}) collective-permute-start(bf16[2,72,1536]{2,1,0:T(8,128)(2,1)S(1)} %collective-permute-done.6.near_ref), channel_id=1, source_target_pairs={{0,8},{8,16},{16,24},{12,4},{20,12},{28,20},{1,9},{9,17},{17,25},{... | collective-permute-start | bytes 1327112 | tf_op jit(solution)/shard_map/ppermute | solution.py:311
  61.3 0.0 collective-permute-done.14
  61.4 0.1 collective-permute-start.16
  61.5 0.1 collective-permute-start.15
  61.5 8.0 %collective-permute-done.16.refs_1_ = bf16[96,384]{1,0:T(8,128)(2,1)S(1)} collective-permute-done((bf16[96,384]{1,0:T(8,128)(2,1)S(1)}, bf16[96,384]{1,0:T(8,128)(2,1)S(1)}, u32[]{:S(2)}, u32[]{:S(2)}) %collective-permute-start.16) | collective-permute-done | bytes 73760 | tf_op jit(solution)/shard_map/ppermute | solution.py:304
  69.5 0.0 collective-permute-start.17
  69.5 0.0 copy-done.3
  69.5 0.1 copy.9
  69.7 0.4 reshape.7.w_ref
  70.1 1.0 %shard_map.75.refs_2_ = f32[5,5,72,72]{3,2,1,0:T(8,128)} custom-call(bf16[96,384]{1,0:T(8,128)(2,1)S(1)} %add_convert_fusion.1.refs_0_, bf16[96,384]{1,0:T(8,128)(2,1)S(1)} %collective-permute-done.16.refs_1_), custom_call_target="tpu_custom_call" | custom-call | bytes 665856 | tf_op jit(solution)/shard_map/pallas_call | solution.py:39
  71.1 0.0 collective-permute-done.15.refs_0_
  71.1 0.0 collective-permute-done.17.refs_1_
  71.1 1.0 %shard_map.76 = f32[5,5,72,72]{3,2,1,0:T(8,128)} custom-call(bf16[96,384]{1,0:T(8,128)(2,1)S(1)} %collective-permute-done.15.refs_0_, bf16[96,384]{1,0:T(8,128)(2,1)S(1)} %collective-permute-done.17.refs_1_, f32[5,5,72,72]{3,2,1,0:T(8,128)} %shard_map.75.refs_2_), custom_call_target="tpu_custom_call", output_to_operand_aliasing={{}: (2, {})} | custom-call | bytes 1184256 | tf_op jit(solution)/shard_map/pallas_call | solution.py:39
  72.2 0.0 collective-permute-done.7.far_ref
  72.2 2.4 %shard_map.72 = bf16[1,72,2,1440]{3,2,1,0:T(2,128)(2,1)} custom-call(bf16[360,360]{1,0:T(8,128)(2,1)S(1)} %reshape.7.w_ref, bf16[2,72,1536]{2,1,0:T(8,128)(2,1)S(1)} %shard_map.71.own_ref.g_ref, bf16[2,72,1536]{2,1,0:T(8,128)(2,1)S(1)} %collective-permute-done.6.near_ref, bf16[2,72,1536]{2,1,0:T(8,128)(2,1)S(1)} %collective-permute-done.7.far_ref), custom_call_target="tpu_custom_call" | custom-call | flops 796262400 | bytes 2001024 | tf_op jit(solution)/shard_map/pallas_call | solution.py:39
  (7 shorter events, 0.2 us)
Async XLA Ops:
  0.6 13.4 %collective-permute-start = (bf16[1,72,2,1440]{3,2,1,0:T(2,128)(2,1)}, bf16[1,72,2,1440]{3,2,1,0:T(2,128)(2,1)S(1)}, u32[]{:S(2)}, u32[]{:S(2)}) collective-permute-start(bf16[1,72,2,1440]{3,2,1,0:T(2,128)(2,1)} %x_ref.1), channel_id=1, source_target_pairs={{0,2},{2,0},{1,3},{3,1},{4,6},{6,4},{5,7},{7,5},{8,10},{10,8},{9,1... | collective-permute-start | bytes 1244168 | tf_op jit(solution)/shard_map/ppermute | solution.py:304
  3.7 19.0 %collective-permute-start.2 = (bf16[1,72,2,1440]{3,2,1,0:T(2,128)(2,1)}, bf16[1,72,2,1440]{3,2,1,0:T(2,128)(2,1)S(1)}, u32[]{:S(2)}, u32[]{:S(2)}) collective-permute-start(bf16[1,72,2,1440]{3,2,1,0:T(2,128)(2,1)} %x_ref.1), channel_id=1, source_target_pairs={{0,1},{1,0},{2,3},{3,2},{4,5},{5,4},{6,7},{7,6},{8,9},{9,8},{10,11... | collective-permute-start | bytes 1244168 | tf_op jit(solution)/shard_map/ppermute | solution.py:304
  14.1 11.9 %collective-permute-start.1 = (bf16[1,72,2,1440]{3,2,1,0:T(2,128)(2,1)S(1)}, bf16[1,72,2,1440]{3,2,1,0:T(2,128)(2,1)S(1)}, u32[]{:S(2)}, u32[]{:S(2)}) collective-permute-start(bf16[1,72,2,1440]{3,2,1,0:T(2,128)(2,1)S(1)} %collective-permute-done.refs_1_), channel_id=1, source_target_pairs={{0,1},{1,0},{2,3},{3,2},{4,5},{5,4},{6,7},{7,6},{8,9},{9,8},{10,11... | collective-permute-start | bytes 1244168 | tf_op jit(solution)/shard_map/ppermute | solution.py:304
  14.1 21.6 %collective-permute-start.8 = (bf16[1,72,2,1440]{3,2,1,0:T(2,128)(2,1)}, bf16[1,72,2,1440]{3,2,1,0:T(2,128)(2,1)S(1)}, u32[]{:S(2)}, u32[]{:S(2)}) collective-permute-start(bf16[1,72,2,1440]{3,2,1,0:T(2,128)(2,1)} %own_ref.1), channel_id=1, source_target_pairs={{0,4},{4,0},{8,12},{12,8},{16,20},{20,16},{24,28},{28,24},{1,5},{5... | collective-permute-start | bytes 1244168 | tf_op jit(solution)/shard_map/ppermute | solution.py:304
  15.8 19.9 %collective-permute-start.9 = (bf16[1,72,2,1440]{3,2,1,0:T(2,128)(2,1)}, bf16[1,72,2,1440]{3,2,1,0:T(2,128)(2,1)S(1)}, u32[]{:S(2)}, u32[]{:S(2)}) collective-permute-start(bf16[1,72,2,1440]{3,2,1,0:T(2,128)(2,1)} %own_ref.1), channel_id=1, source_target_pairs={{4,8},{12,16},{20,24},{8,4},{16,12},{24,20},{5,9},{13,17},{21,25},... | collective-permute-start | bytes 1244168 | tf_op jit(solution)/shard_map/ppermute | solution.py:318
  17.4 5.3 %collective-permute-start.4 = (bf16[72,720]{1,0:T(8,128)(2,1)S(1)}, bf16[72,720]{1,0:T(8,128)(2,1)S(1)}, u32[]{:S(2)}, u32[]{:S(2)}) collective-permute-start(bf16[72,720]{1,0:T(8,128)(2,1)S(1)} %convert_element_type.48.refs_0_), channel_id=1, source_target_pairs={{0,2},{2,0},{1,3},{3,1},{4,6},{6,4},{5,7},{7,5},{8,10},{10,8},{9,1... | collective-permute-start | bytes 311048 | tf_op jit(solution)/shard_map/ppermute | solution.py:304
  22.7 3.9 %collective-permute-start.3 = (bf16[72,720]{1,0:T(8,128)(2,1)S(1)}, bf16[72,720]{1,0:T(8,128)(2,1)S(1)}, u32[]{:S(2)}, u32[]{:S(2)}) collective-permute-start(bf16[72,720]{1,0:T(8,128)(2,1)S(1)} %convert_element_type.48.refs_0_), channel_id=1, source_target_pairs={{0,1},{1,0},{2,3},{3,2},{4,5},{5,4},{6,7},{7,6},{8,9},{9,8},{10,11... | collective-permute-start | bytes 311048 | tf_op jit(solution)/shard_map/ppermute | solution.py:304
  22.7 3.9 %collective-permute-start.5 = (bf16[72,720]{1,0:T(8,128)(2,1)S(1)}, bf16[72,720]{1,0:T(8,128)(2,1)S(1)}, u32[]{:S(2)}, u32[]{:S(2)}) collective-permute-start(bf16[72,720]{1,0:T(8,128)(2,1)S(1)} %collective-permute-done.4.refs_2_), channel_id=1, source_target_pairs={{0,1},{1,0},{2,3},{3,2},{4,5},{5,4},{6,7},{7,6},{8,9},{9,8},{10,11... | collective-permute-start | bytes 311048 | tf_op jit(solution)/shard_map/ppermute | solution.py:304
  23.2 1.0 %copy-start = (bf16[1,72,2,1440]{3,2,1,0:T(2,128)(2,1)S(1)}, bf16[1,72,2,1440]{3,2,1,0:T(2,128)(2,1)}, u32[]{:S(2)}) copy-start(bf16[1,72,2,1440]{3,2,1,0:T(2,128)(2,1)} %x_ref.1) | copy-start | bytes 1244164
  24.2 0.7 copy-start.1
  26.0 2.0 %copy-start.2 = (bf16[1,72,2,1440]{3,2,1,0:T(2,128)(2,1)S(1)}, bf16[1,72,2,1440]{3,2,1,0:T(2,128)(2,1)}, u32[]{:S(2)}) copy-start(bf16[1,72,2,1440]{3,2,1,0:T(2,128)(2,1)} %own_ref.1) | copy-start | bytes 1244164
  35.7 33.9 %copy-start.3 = (bf16[5,5,72,72]{3,2,1,0:T(8,128)(2,1)S(1)}, bf16[5,5,72,72]{3,2,1,0:T(8,128)(2,1)}, u32[]{:S(2)}) copy-start(bf16[5,5,72,72]{3,2,1,0:T(8,128)(2,1)} %param.9) | copy-start | bytes 777604
  36.7 1.4 %collective-permute-start.10 = (bf16[192,384]{1,0:T(8,128)(2,1)S(1)}, bf16[192,384]{1,0:T(8,128)(2,1)S(1)}, u32[]{:S(2)}, u32[]{:S(2)}) collective-permute-start(bf16[192,384]{1,0:T(8,128)(2,1)S(1)} %constant_dynamic-slice_fusion.1), channel_id=1, source_target_pairs={{0,1},{1,0},{2,3},{3,2},{4,5},{5,4},{6,7},{7,6},{8,9},{9,8},{10,11... | collective-permute-start | bytes 442376 | tf_op jit(solution)/shard_map/ppermute | solution.py:304
  38.3 5.1 %collective-permute-start.11 = (bf16[96,384]{1,0:T(8,128)(2,1)S(1)}, bf16[96,384]{1,0:T(8,128)(2,1)S(1)}, u32[]{:S(2)}, u32[]{:S(2)}) collective-permute-start(bf16[96,384]{1,0:T(8,128)(2,1)S(1)} %constant_dynamic-slice_fusion), channel_id=1, source_target_pairs={{0,8},{4,12},{8,0},{12,4},{16,24},{20,28},{24,16},{28,20},{1,9},{5... | collective-permute-start | bytes 221192 | tf_op jit(solution)/shard_map/ppermute | solution.py:304
  43.4 5.5 %collective-permute-start.12 = (bf16[96,384]{1,0:T(8,128)(2,1)S(1)}, bf16[96,384]{1,0:T(8,128)(2,1)S(1)}, u32[]{:S(2)}, u32[]{:S(2)}) collective-permute-start(bf16[96,384]{1,0:T(8,128)(2,1)S(1)} %add_convert_fusion.4), channel_id=1, source_target_pairs={{0,16},{4,20},{8,24},{12,28},{16,0},{20,4},{24,8},{28,12},{1,17},{... | collective-permute-start | bytes 221192 | tf_op jit(solution)/shard_map/ppermute | solution.py:304
  46.3 11.6 %collective-permute-start.6 = (bf16[2,72,1536]{2,1,0:T(8,128)(2,1)S(1)}, bf16[2,72,1536]{2,1,0:T(8,128)(2,1)S(1)}, u32[]{:S(2)}, u32[]{:S(2)}) collective-permute-start(bf16[2,72,1536]{2,1,0:T(8,128)(2,1)S(1)} %shard_map.71.own_ref.g_ref), channel_id=1, source_target_pairs={{0,4},{4,0},{8,12},{12,8},{16,20},{20,16},{24,28},{28,24},{1,5},{5... | collective-permute-start | bytes 1327112 | tf_op jit(solution)/shard_map/ppermute | solution.py:304
  48.9 4.4 %collective-permute-start.13 = (bf16[96,384]{1,0:T(8,128)(2,1)S(1)}, bf16[96,384]{1,0:T(8,128)(2,1)S(1)}, u32[]{:S(2)}, u32[]{:S(2)}) collective-permute-start(bf16[96,384]{1,0:T(8,128)(2,1)S(1)} %add_convert_fusion.3), channel_id=1, source_target_pairs={{0,2},{2,0},{1,3},{3,1},{4,6},{6,4},{5,7},{7,5},{8,10},{10,8},{9,1... | collective-permute-start | bytes 221192 | tf_op jit(solution)/shard_map/ppermute | solution.py:304
  53.4 8.0 %collective-permute-start.14 = (bf16[96,384]{1,0:T(8,128)(2,1)S(1)}, bf16[96,384]{1,0:T(8,128)(2,1)S(1)}, u32[]{:S(2)}, u32[]{:S(2)}) collective-permute-start(bf16[96,384]{1,0:T(8,128)(2,1)S(1)} %add_convert_fusion.2), channel_id=1, source_target_pairs={{0,4},{4,0},{8,12},{12,8},{16,20},{20,16},{24,28},{28,24},{1,5},{5... | collective-permute-start | bytes 221192 | tf_op jit(solution)/shard_map/ppermute | solution.py:304
  57.8 14.4 %collective-permute-start.7 = (bf16[2,72,1536]{2,1,0:T(8,128)(2,1)S(1)}, bf16[2,72,1536]{2,1,0:T(8,128)(2,1)S(1)}, u32[]{:S(2)}, u32[]{:S(2)}) collective-permute-start(bf16[2,72,1536]{2,1,0:T(8,128)(2,1)S(1)} %collective-permute-done.6.near_ref), channel_id=1, source_target_pairs={{0,8},{8,16},{16,24},{12,4},{20,12},{28,20},{1,9},{9,17},{17,25},{... | collective-permute-start | bytes 1327112 | tf_op jit(solution)/shard_map/ppermute | solution.py:311
  61.4 8.2 %collective-permute-start.16 = (bf16[96,384]{1,0:T(8,128)(2,1)S(1)}, bf16[96,384]{1,0:T(8,128)(2,1)S(1)}, u32[]{:S(2)}, u32[]{:S(2)}) collective-permute-start(bf16[96,384]{1,0:T(8,128)(2,1)S(1)} %add_convert_fusion.1.refs_0_), channel_id=1, source_target_pairs={{0,8},{4,12},{8,0},{12,4},{16,24},{20,28},{24,16},{28,20},{1,9},{5... | collective-permute-start | bytes 221192 | tf_op jit(solution)/shard_map/ppermute | solution.py:304
  61.5 9.7 %collective-permute-start.15 = (bf16[96,384]{1,0:T(8,128)(2,1)S(1)}, bf16[96,384]{1,0:T(8,128)(2,1)S(1)}, u32[]{:S(2)}, u32[]{:S(2)}) collective-permute-start(bf16[96,384]{1,0:T(8,128)(2,1)S(1)} %add_convert_fusion.1.refs_0_), channel_id=1, source_target_pairs={{0,1},{1,0},{2,3},{3,2},{4,5},{5,4},{6,7},{7,6},{8,9},{9,8},{10,11... | collective-permute-start | bytes 221192 | tf_op jit(solution)/shard_map/ppermute | solution.py:304
  69.5 1.6 %collective-permute-start.17 = (bf16[96,384]{1,0:T(8,128)(2,1)S(1)}, bf16[96,384]{1,0:T(8,128)(2,1)S(1)}, u32[]{:S(2)}, u32[]{:S(2)}) collective-permute-start(bf16[96,384]{1,0:T(8,128)(2,1)S(1)} %collective-permute-done.16.refs_1_), channel_id=1, source_target_pairs={{0,1},{1,0},{2,3},{3,2},{4,5},{5,4},{6,7},{7,6},{8,9},{9,8},{10,11... | collective-permute-start | bytes 221192 | tf_op jit(solution)/shard_map/ppermute | solution.py:304

commit v7 on v6

--- a/solution.py
+++ b/solution.py
@@ -101,19 +101,16 @@
     return x.reshape(x.shape[0] // 8, 8, x.shape[1])
 
 
-def pair_kernel(rows, begun, s_ref, own_ref, *refs):
+def pair_kernel(rows, s_ref, own_ref, *refs):
     *others, o_ref, mix_scr = refs
-    sum_ref = others.pop() if begun else None
     for d, other in enumerate(others):
         mix_scr[d] = mixed(other)
     for low, high in tiles(mix_scr.shape[2]):
         sq = blocks(s_ref[:, : high - low])
         own = blocks(own_ref[:, low:high].astype(F32))
-        self_inverse = 0.0 if begun else 1.0 / jnp.sqrt(smoothing)
+        self_inverse = 1.0 / jnp.sqrt(smoothing)
         total = jnp.full(own.shape[1:], self_inverse, F32)
         mixture = own * self_inverse
-        if begun:
-            mixture = mixture - blocks(sum_ref[:, low:high])
         for d in range(len(others)):
             other = blocks(mix_scr[d, :, low:high].astype(F32))
             diff = own - other
@@ -196,7 +193,9 @@
     o_ref[...] = over_lanes(mixed(own_ref), shift_ref)
 
 
-def kgrad_kernel(ksize, shift_ref, own_ref, near_ref, far_ref, o_ref, acc):
+def kgrad_kernel(
+    ksize, shift_ref, own_ref, near_ref, far_ref, keep_ref, give_ref, acc, total
+):
     channels, rows = near_ref.shape[1:3]
     n = shift_ref.shape[1]
     odd = lax.axis_index("space") % 2
@@ -205,6 +204,7 @@
         jnp.concatenate([mixed(near_ref), mixed(far_ref)], axis=0), shift_ref
     )
     near, far = 2 * (1 - odd), 2 * odd
+    core, half = lax.axis_index("core"), keep_ref.shape[0]
     for t in range(acc.shape[1]):
         lanes = slice(t * LANES, (t + 1) * LANES)
         acc[1, t] = own_ref[:, lanes]
@@ -219,11 +219,19 @@
                     band, r * (n // LANES) + t, pl.ds(row, channels, stride=rows), :
                 ]
                 tap = part if tap is None else tap + part
-            o_ref[
-                i * channels : (i + 1) * channels, t * LANES : (t + 1) * LANES
-            ] = tap.astype(o_ref.dtype)
-    used = ksize * channels
-    o_ref[used:] = jnp.zeros((o_ref.shape[0] - used, n), o_ref.dtype)
+            for h in range(2):
+                low, high = max(i * channels, h * half), min((i + 1) * channels, (h + 1) * half)
+                if low < high:
+                    piece = tap[low - i * channels : high - i * channels]
+                    total[
+                        (h + core) % 2,
+                        low - h * half : high - h * half,
+                        t * LANES : (t + 1) * LANES,
+                    ] = piece.astype(total.dtype)
+    used = ksize * channels - half
+    total[(1 + core) % 2, used:] = jnp.zeros((half - used, n), total.dtype)
+    keep_ref[...] = total[0]
+    give_ref[...] = total[1]
 
 
 def gather_rows(own, near, far, scr):
@@ -341,9 +349,9 @@
     return add(keep, flip(give, axis, bit))
 
 
-def reduce_all(x):
+def reduce_all(keep, give):
     core, first = ("core", 1), ("space", 2)
-    x = halve(x, *core)
+    x = add(keep, flip(give, *core))
     x = halve(x, *first)
     rest = [("space", b) for b in bits("space")[2:]]
     rest += [("chip", b) for b in bits("chip")] + [("space", 1)]
@@ -352,7 +360,7 @@
     y = flip(x, *first)
     x_other = flip(x, *core)
     y_other = flip(y, *core)
-    return (x, y), (x_other, y_other)
+    return (x, y, x_other), (y_other,)
 
 
 def body(prediction_maps, truth_analysis, reciprocal_spread, deconv_inputs, filter_tensor):
@@ -391,27 +399,20 @@
         ],
         anywhere=[0, 1],
     )
-    taps = jnp.transpose(filter_tensor, (1, 2, 0, 3)).reshape(
-        ksize * channels, ksize * channels
-    )
+    taps = jnp.transpose(filter_tensor, (1, 2, 0, 3)).reshape(ksize * channels, ksize * channels)
     arrived, seen = [], []
     for i, (x, t) in enumerate(zip(fields, truths)):
         arrived += [x, core(x)] if i else [core(x)]
         seen += [t, core(t)]
 
     table = [float(v) for v in area_weights(rows_total)]
-
-    def pairs(others, so_far):
-        return call(
-            functools.partial(pair_kernel, rows, bool(so_far)),
-            [sds((mix, width), F32)],
-            [scale, own, *others, *so_far],
-            [pltpu.VMEM((len(others), mix, width), BF)],
-            spare=max(3, members) << 20,
-        )[0]
-
-    paired = pairs(arrived[:-1], ())
-    paired = pairs(arrived[-1:], (paired,))
+    paired = call(
+        functools.partial(pair_kernel, rows),
+        [sds((mix, width), F32)],
+        [scale, own, *arrived],
+        [pltpu.VMEM((members - 1, mix, width), BF)],
+        spare=max(3, members) << 20,
+    )[0]
     grad = call(
         functools.partial(energy_kernel, span, members, table),
         [slab],
@@ -437,14 +438,17 @@
         [grad, deconv_inputs],
         flops=flops // 3,
     )
-    partial = call(
+    keep, give = call(
         functools.partial(kgrad_kernel, ksize),
-        [sds((packed, packed), BF)],
+        [sds((packed // 2, packed), BF)] * 2,
         [shifted, own_part, near, far],
-        [pltpu.VMEM((3, rows * packed // LANES, mix, LANES), F32)],
+        [
+            pltpu.VMEM((3, rows * packed // LANES, mix, LANES), F32),
+            pltpu.VMEM((2, packed // 2, packed), BF),
+        ],
         flops * 2 // 3,
-    )[0]
-    early, late = reduce_all(partial)
+    )
+    early, late = reduce_all(keep, give)
 
     grad_hidden = call(
         functools.partial(conv_kernel, ksize),
@@ -473,8 +477,8 @@
             aliases={count: 0} if len(xs) > count else {},
         )[0]
 
-    grad_kernel = finish([(0, 0), (0, 1)], *early)
-    grad_kernel = finish([(1, 0), (1, 1)], *late, grad_kernel)
+    grad_kernel = finish([(0, 0), (0, 1), (1, 0)], *early)
+    grad_kernel = finish([(1, 1)], *late, grad_kernel)
     return (grad_hidden, grad_kernel)
 
 

time: 74.9 us -> 74.9 us (level)
    pallas_call x9 -> x8, Pallas kernels: 9.65 us -> 9.48 us  [call(): pl.pallas_call(kernel, out_shape=list(outs), in_specs=[ANY if i in anywhe...]
where the time goes in v7:
time: 74.9 us; the launch traced here: 74.6 us
  waiting for transfers between devices  39.7 us (53%)
  starting transfers between devices  21.3 us (28%)
  Pallas kernels  9.48 us (13%)
  local copies, waits for them, and re-layouts  2.21 us (3%)
  other arithmetic  1.08 us (1%)
  between operations  0.86 us (1%)
    ppermute x16, waiting for transfers between devices, flip(): return lax.ppermute(x, axis, [(i, i ^ bit) for i in range(size)])  39.7 us
    ppermute x16, starting transfers between devices, flip(): return lax.ppermute(x, axis, [(i, i ^ bit) for i in range(size)])  17.1 us
    pallas_call x8, Pallas kernels, call(): pl.pallas_call(kernel, out_shape=list(outs), in_specs=[ANY if i in anywhe...  9.48 us
    ppermute x1, starting transfers between devices, along(): return lax.ppermute(x, 'space', pairs)  3.5 us
    unnamed x8, local copies, waits for them, and re-layouts  1.68 us
  transfers between devices with their start and end apart: 18, of which 9 were waited for; matrix products, arithmetic and copies ran while one was open for 2% of the time, Pallas kernels for 8%

profile of v7, /device:TPU:0, one launch (start us, length us, event | category | flops | bytes accessed | tf_op | source)
XLA Modules:
  0.0 74.6 jit_solution(10060943011880413068)
XLA Ops:
  0.6 3.1 %collective-permute-start.1 = (bf16[1,72,2,1440]{3,2,1,0:T(2,128)(2,1)}, bf16[1,72,2,1440]{3,2,1,0:T(2,128)(2,1)S(1)}, u32[]{:S(2)}, u32[]{:S(2)}) collective-permute-start(bf16[1,72,2,1440]{3,2,1,0:T(2,128)(2,1)} %x_ref.1), channel_id=1, source_target_pairs={{0,2},{2,0},{1,3},{3,1},{4,6},{6,4},{5,7},{7,5},{8,10},{10,8},{9,1... | collective-permute-start | bytes 1244168 | tf_op jit(solution)/shard_map/ppermute | solution.py:312
  3.7 0.0 collective-permute-start
  3.7 10.4 %collective-permute-done.1.refs_1_ = bf16[1,72,2,1440]{3,2,1,0:T(2,128)(2,1)S(1)} collective-permute-done((bf16[1,72,2,1440]{3,2,1,0:T(2,128)(2,1)}, bf16[1,72,2,1440]{3,2,1,0:T(2,128)(2,1)S(1)}, u32[]{:S(2)}, u32[]{:S(2)}) %collective-permute-start.1) | collective-permute-done | bytes 414752 | tf_op jit(solution)/shard_map/ppermute | solution.py:312
  14.1 0.0 collective-permute-start.2
  14.1 1.7 %collective-permute-start.8 = (bf16[1,72,2,1440]{3,2,1,0:T(2,128)(2,1)}, bf16[1,72,2,1440]{3,2,1,0:T(2,128)(2,1)S(1)}, u32[]{:S(2)}, u32[]{:S(2)}) collective-permute-start(bf16[1,72,2,1440]{3,2,1,0:T(2,128)(2,1)} %own_ref.1), channel_id=1, source_target_pairs={{0,4},{4,0},{8,12},{12,8},{16,20},{20,16},{24,28},{28,24},{1,5},{5... | collective-permute-start | bytes 1244168 | tf_op jit(solution)/shard_map/ppermute | solution.py:312
  15.8 0.7 collective-permute-start.9
  16.5 0.9 %convert_element_type.48.refs_0_ = bf16[72,720]{1,0:T(8,128)(2,1)S(1)} convert(f32[72,720]{1,0:T(8,128)} %param.6) | non-fusion elementwise | flops 51840 | bytes 311040 | tf_op jit(solution)/shard_map/convert_element_type | solution.py:388
  17.4 1.6 %collective-permute-start.4 = (bf16[72,720]{1,0:T(8,128)(2,1)S(1)}, bf16[72,720]{1,0:T(8,128)(2,1)S(1)}, u32[]{:S(2)}, u32[]{:S(2)}) collective-permute-start(bf16[72,720]{1,0:T(8,128)(2,1)S(1)} %convert_element_type.48.refs_0_), channel_id=1, source_target_pairs={{0,2},{2,0},{1,3},{3,1},{4,6},{6,4},{5,7},{7,5},{8,10},{10,8},{9,1... | collective-permute-start | bytes 311048 | tf_op jit(solution)/shard_map/ppermute | solution.py:312
  19.0 3.7 %collective-permute-done.4.refs_2_ = bf16[72,720]{1,0:T(8,128)(2,1)S(1)} collective-permute-done((bf16[72,720]{1,0:T(8,128)(2,1)S(1)}, bf16[72,720]{1,0:T(8,128)(2,1)S(1)}, u32[]{:S(2)}, u32[]{:S(2)}) %collective-permute-start.4) | collective-permute-done | bytes 103712 | tf_op jit(solution)/shard_map/ppermute | solution.py:312
  22.7 0.0 collective-permute-start.3
  22.7 0.0 collective-permute-done.refs_0_
  22.7 0.5 collective-permute-start.5
  23.2 0.0 copy-start
  23.2 1.0 %copy-done = bf16[1,72,2,1440]{3,2,1,0:T(2,128)(2,1)S(1)} copy-done((bf16[1,72,2,1440]{3,2,1,0:T(2,128)(2,1)S(1)}, bf16[1,72,2,1440]{3,2,1,0:T(2,128)(2,1)}, u32[]{:S(2)}) %copy-start) | copy-done | bytes 414744
  24.2 0.0 copy-start.1
  24.2 0.7 copy-done.1
  24.9 0.4 shard_map.68
  25.3 0.0 collective-permute-done.2.refs_2_
  25.3 0.0 copy-start.2
  25.3 1.0 %shard_map.69.pair_ref = f32[144,1440]{1,0:T(8,128)S(1)} custom-call(f32[144,128]{1,0:T(8,128)S(1)} %get-tuple-element.8.s_ref, bf16[144,1440]{1,0:T(8,128)(2,1)S(1)} %get-tuple-element.9.own_ref, bf16[1,72,2,1440]{3,2,1,0:T(2,128)(2,1)S(1)} %collective-permute-done.refs_0_, bf16[1,72,2,1440]{3,2,1,0:T(2,128)(2,1)S(1)} %collective-permute-done.1.refs_1_, ...), custom_call_target="tpu_custom_call" | custom-call | bytes 2562048 | tf_op jit(solution)/shard_map/pallas_call | solution.py:39
  26.3 0.0 collective-permute-done.3.refs_1_
  26.3 0.0 collective-permute-done.5.refs_3_
  26.3 1.4 %shard_map.70.own_ref.g_ref = bf16[2,72,1536]{2,1,0:T(8,128)(2,1)S(1)} custom-call(f32[144,128]{1,0:T(8,128)S(1)} %get-tuple-element.8.s_ref, bf16[144,1440]{1,0:T(8,128)(2,1)S(1)} %get-tuple-element.9.own_ref, f32[144,1440]{1,0:T(8,128)S(1)} %shard_map.69.pair_ref, bf16[72,720]{1,0:T(8,128)(2,1)S(1)} %convert_element_type.48.refs_0_, ...), custom_call_target="tpu_custom_call" | custom-call | bytes 2174976 | tf_op jit(solution)/shard_map/pallas_call | solution.py:39
  27.7 0.0 copy-done.2
  27.7 1.1 %shard_map.72 = (bf16[2,384,1536]{2,1,0:T(8,128)(2,1)S(1)}, f32[144,768]{1,0:T(8,128)S(1)}) custom-call(bf16[2,72,1536]{2,1,0:T(8,128)(2,1)S(1)} %shard_map.70.own_ref.g_ref, bf16[1,72,2,1440]{3,2,1,0:T(2,128)(2,1)S(1)} %copy-done.2), custom_call_target="tpu_custom_call" | custom-call | flops 265420800 | bytes 3658752 | tf_op jit(solution)/shard_map/pallas_call | solution.py:39
  28.8 6.9 %collective-permute-done.8.near_ref = bf16[1,72,2,1440]{3,2,1,0:T(2,128)(2,1)S(1)} collective-permute-done((bf16[1,72,2,1440]{3,2,1,0:T(2,128)(2,1)}, bf16[1,72,2,1440]{3,2,1,0:T(2,128)(2,1)S(1)}, u32[]{:S(2)}, u32[]{:S(2)}) %collective-permute-start.8) | collective-permute-done | bytes 414752 | tf_op jit(solution)/shard_map/ppermute | solution.py:312
  35.7 0.0 collective-permute-done.9.far_ref
  35.7 0.0 copy-start.3
  35.7 1.1 %shard_map.73 = (bf16[192,384]{1,0:T(8,128)(2,1)S(1)}, bf16[192,384]{1,0:T(8,128)(2,1)S(1)}) custom-call(bf16[2,384,1536]{2,1,0:T(8,128)(2,1)S(1)} %get-tuple-element.10.shift_ref, f32[144,768]{1,0:T(8,128)S(1)} %get-tuple-element.11.own_ref, bf16[1,72,2,1440]{3,2,1,0:T(2,128)(2,1)S(1)} %collective-permute-done.8.near_ref, ...), custom_call_target="tpu_custom_call" | custom-call | flops 530841600 | bytes 3926016 | tf_op jit(solution)/shard_map/pallas_call | solution.py:39
  36.8 0.1 collective-permute-start.10
  36.9 1.3 %collective-permute-done.10 = bf16[192,384]{1,0:T(8,128)(2,1)S(1)} collective-permute-done((bf16[192,384]{1,0:T(8,128)(2,1)S(1)}, bf16[192,384]{1,0:T(8,128)(2,1)S(1)}, u32[]{:S(2)}, u32[]{:S(2)}) %collective-permute-start.10) | collective-permute-done | bytes 147488 | tf_op jit(solution)/shard_map/ppermute | solution.py:312
  38.3 2.5 %collective-permute-start.11 = (bf16[96,384]{1,0:T(8,128)(2,1)S(1)}, bf16[96,384]{1,0:T(8,128)(2,1)S(1)}, u32[]{:S(2)}, u32[]{:S(2)}) collective-permute-start(bf16[96,384]{1,0:T(8,128)(2,1)S(1)} %constant_dynamic-slice_fusion), channel_id=1, source_target_pairs={{0,8},{4,12},{8,0},{12,4},{16,24},{20,28},{24,16},{28,20},{1,9},{5... | collective-permute-start | bytes 221192 | tf_op jit(solution)/shard_map/ppermute | solution.py:312
  40.8 2.6 %collective-permute-done.11 = bf16[96,384]{1,0:T(8,128)(2,1)S(1)} collective-permute-done((bf16[96,384]{1,0:T(8,128)(2,1)S(1)}, bf16[96,384]{1,0:T(8,128)(2,1)S(1)}, u32[]{:S(2)}, u32[]{:S(2)}) %collective-permute-start.11) | collective-permute-done | bytes 73760 | tf_op jit(solution)/shard_map/ppermute | solution.py:312
  43.4 2.9 %collective-permute-start.12 = (bf16[96,384]{1,0:T(8,128)(2,1)S(1)}, bf16[96,384]{1,0:T(8,128)(2,1)S(1)}, u32[]{:S(2)}, u32[]{:S(2)}) collective-permute-start(bf16[96,384]{1,0:T(8,128)(2,1)S(1)} %add_convert_fusion.4), channel_id=1, source_target_pairs={{0,16},{4,20},{8,24},{12,28},{16,0},{20,4},{24,8},{28,12},{1,17},{... | collective-permute-start | bytes 221192 | tf_op jit(solution)/shard_map/ppermute | solution.py:312
  46.3 1.5 %collective-permute-start.6 = (bf16[2,72,1536]{2,1,0:T(8,128)(2,1)S(1)}, bf16[2,72,1536]{2,1,0:T(8,128)(2,1)S(1)}, u32[]{:S(2)}, u32[]{:S(2)}) collective-permute-start(bf16[2,72,1536]{2,1,0:T(8,128)(2,1)S(1)} %shard_map.70.own_ref.g_ref), channel_id=1, source_target_pairs={{0,4},{4,0},{8,12},{12,8},{16,20},{20,16},{24,28},{28,24},{1,5},{5... | collective-permute-start | bytes 1327112 | tf_op jit(solution)/shard_map/ppermute | solution.py:312
  47.7 1.2 %collective-permute-done.12 = bf16[96,384]{1,0:T(8,128)(2,1)S(1)} collective-permute-done((bf16[96,384]{1,0:T(8,128)(2,1)S(1)}, bf16[96,384]{1,0:T(8,128)(2,1)S(1)}, u32[]{:S(2)}, u32[]{:S(2)}) %collective-permute-start.12) | collective-permute-done | bytes 73760 | tf_op jit(solution)/shard_map/ppermute | solution.py:312
  48.9 1.6 %collective-permute-start.13 = (bf16[96,384]{1,0:T(8,128)(2,1)S(1)}, bf16[96,384]{1,0:T(8,128)(2,1)S(1)}, u32[]{:S(2)}, u32[]{:S(2)}) collective-permute-start(bf16[96,384]{1,0:T(8,128)(2,1)S(1)} %add_convert_fusion.3), channel_id=1, source_target_pairs={{0,2},{2,0},{1,3},{3,1},{4,6},{6,4},{5,7},{7,5},{8,10},{10,8},{9,1... | collective-permute-start | bytes 221192 | tf_op jit(solution)/shard_map/ppermute | solution.py:312
  50.5 2.8 %collective-permute-done.13 = bf16[96,384]{1,0:T(8,128)(2,1)S(1)} collective-permute-done((bf16[96,384]{1,0:T(8,128)(2,1)S(1)}, bf16[96,384]{1,0:T(8,128)(2,1)S(1)}, u32[]{:S(2)}, u32[]{:S(2)}) %collective-permute-start.13) | collective-permute-done | bytes 73760 | tf_op jit(solution)/shard_map/ppermute | solution.py:312
  53.4 1.6 %collective-permute-start.14 = (bf16[96,384]{1,0:T(8,128)(2,1)S(1)}, bf16[96,384]{1,0:T(8,128)(2,1)S(1)}, u32[]{:S(2)}, u32[]{:S(2)}) collective-permute-start(bf16[96,384]{1,0:T(8,128)(2,1)S(1)} %add_convert_fusion.2), channel_id=1, source_target_pairs={{0,4},{4,0},{8,12},{12,8},{16,20},{20,16},{24,28},{28,24},{1,5},{5... | collective-permute-start | bytes 221192 | tf_op jit(solution)/shard_map/ppermute | solution.py:312
  54.9 2.9 %collective-permute-done.6.near_ref = bf16[2,72,1536]{2,1,0:T(8,128)(2,1)S(1)} collective-permute-done((bf16[2,72,1536]{2,1,0:T(8,128)(2,1)S(1)}, bf16[2,72,1536]{2,1,0:T(8,128)(2,1)S(1)}, u32[]{:S(2)}, u32[]{:S(2)}) %collective-permute-start.6) | collective-permute-done | bytes 442400 | tf_op jit(solution)/shard_map/ppermute | solution.py:312
  57.8 3.5 %collective-permute-start.7 = (bf16[2,72,1536]{2,1,0:T(8,128)(2,1)S(1)}, bf16[2,72,1536]{2,1,0:T(8,128)(2,1)S(1)}, u32[]{:S(2)}, u32[]{:S(2)}) collective-permute-start(bf16[2,72,1536]{2,1,0:T(8,128)(2,1)S(1)} %collective-permute-done.6.near_ref), channel_id=1, source_target_pairs={{0,8},{8,16},{16,24},{12,4},{20,12},{28,20},{1,9},{9,17},{17,25},{... | collective-permute-start | bytes 1327112 | tf_op jit(solution)/shard_map/ppermute | solution.py:319
  61.3 0.0 collective-permute-done.14
  61.4 0.1 collective-permute-start.15
  61.5 0.1 collective-permute-start.17
  61.5 8.0 %collective-permute-done.15.refs_1_ = bf16[96,384]{1,0:T(8,128)(2,1)S(1)} collective-permute-done((bf16[96,384]{1,0:T(8,128)(2,1)S(1)}, bf16[96,384]{1,0:T(8,128)(2,1)S(1)}, u32[]{:S(2)}, u32[]{:S(2)}) %collective-permute-start.15) | collective-permute-done | bytes 73760 | tf_op jit(solution)/shard_map/ppermute | solution.py:312
  69.5 0.0 collective-permute-start.16
  69.5 0.0 copy-done.3
  69.6 0.1 copy.9
  69.7 0.4 reshape.7.w_ref
  70.1 0.0 collective-permute-done.17.refs_2_
  70.1 1.2 %shard_map.74.refs_1_ = f32[5,5,72,72]{3,2,1,0:T(8,128)} custom-call(bf16[96,384]{1,0:T(8,128)(2,1)S(1)} %add_convert_fusion.1.refs_0_, bf16[96,384]{1,0:T(8,128)(2,1)S(1)} %collective-permute-done.15.refs_1_, bf16[96,384]{1,0:T(8,128)(2,1)S(1)} %collective-permute-done.17.refs_2_), custom_call_target="tpu_custom_call" | custom-call | bytes 739584 | tf_op jit(solution)/shard_map/pallas_call | solution.py:39
  71.3 0.0 collective-permute-done.16.refs_0_
  71.3 0.9 %shard_map.75 = f32[5,5,72,72]{3,2,1,0:T(8,128)} custom-call(bf16[96,384]{1,0:T(8,128)(2,1)S(1)} %collective-permute-done.16.refs_0_, f32[5,5,72,72]{3,2,1,0:T(8,128)} %shard_map.74.refs_1_), custom_call_target="tpu_custom_call", output_to_operand_aliasing={{}: (1, {})} | custom-call | bytes 1110528 | tf_op jit(solution)/shard_map/pallas_call | solution.py:39
  72.2 0.0 collective-permute-done.7.far_ref
  72.2 2.4 %shard_map.71 = bf16[1,72,2,1440]{3,2,1,0:T(2,128)(2,1)} custom-call(bf16[360,360]{1,0:T(8,128)(2,1)S(1)} %reshape.7.w_ref, bf16[2,72,1536]{2,1,0:T(8,128)(2,1)S(1)} %shard_map.70.own_ref.g_ref, bf16[2,72,1536]{2,1,0:T(8,128)(2,1)S(1)} %collective-permute-done.6.near_ref, bf16[2,72,1536]{2,1,0:T(8,128)(2,1)S(1)} %collective-permute-done.7.far_ref), custom_call_target="tpu_custom_call" | custom-call | flops 796262400 | bytes 2001024 | tf_op jit(solution)/shard_map/pallas_call | solution.py:39
  (6 shorter events, 0.1 us)
Async XLA Ops:
  0.6 13.4 %collective-permute-start.1 = (bf16[1,72,2,1440]{3,2,1,0:T(2,128)(2,1)}, bf16[1,72,2,1440]{3,2,1,0:T(2,128)(2,1)S(1)}, u32[]{:S(2)}, u32[]{:S(2)}) collective-permute-start(bf16[1,72,2,1440]{3,2,1,0:T(2,128)(2,1)} %x_ref.1), channel_id=1, source_target_pairs={{0,2},{2,0},{1,3},{3,1},{4,6},{6,4},{5,7},{7,5},{8,10},{10,8},{9,1... | collective-permute-start | bytes 1244168 | tf_op jit(solution)/shard_map/ppermute | solution.py:312
  3.7 19.0 %collective-permute-start = (bf16[1,72,2,1440]{3,2,1,0:T(2,128)(2,1)}, bf16[1,72,2,1440]{3,2,1,0:T(2,128)(2,1)S(1)}, u32[]{:S(2)}, u32[]{:S(2)}) collective-permute-start(bf16[1,72,2,1440]{3,2,1,0:T(2,128)(2,1)} %x_ref.1), channel_id=1, source_target_pairs={{0,1},{1,0},{2,3},{3,2},{4,5},{5,4},{6,7},{7,6},{8,9},{9,8},{10,11... | collective-permute-start | bytes 1244168 | tf_op jit(solution)/shard_map/ppermute | solution.py:312
  14.1 11.2 %collective-permute-start.2 = (bf16[1,72,2,1440]{3,2,1,0:T(2,128)(2,1)S(1)}, bf16[1,72,2,1440]{3,2,1,0:T(2,128)(2,1)S(1)}, u32[]{:S(2)}, u32[]{:S(2)}) collective-permute-start(bf16[1,72,2,1440]{3,2,1,0:T(2,128)(2,1)S(1)} %collective-permute-done.1.refs_1_), channel_id=1, source_target_pairs={{0,1},{1,0},{2,3},{3,2},{4,5},{5,4},{6,7},{7,6},{8,9},{9,8},{10,11... | collective-permute-start | bytes 1244168 | tf_op jit(solution)/shard_map/ppermute | solution.py:312
  14.1 21.6 %collective-permute-start.8 = (bf16[1,72,2,1440]{3,2,1,0:T(2,128)(2,1)}, bf16[1,72,2,1440]{3,2,1,0:T(2,128)(2,1)S(1)}, u32[]{:S(2)}, u32[]{:S(2)}) collective-permute-start(bf16[1,72,2,1440]{3,2,1,0:T(2,128)(2,1)} %own_ref.1), channel_id=1, source_target_pairs={{0,4},{4,0},{8,12},{12,8},{16,20},{20,16},{24,28},{28,24},{1,5},{5... | collective-permute-start | bytes 1244168 | tf_op jit(solution)/shard_map/ppermute | solution.py:312
  15.8 19.9 %collective-permute-start.9 = (bf16[1,72,2,1440]{3,2,1,0:T(2,128)(2,1)}, bf16[1,72,2,1440]{3,2,1,0:T(2,128)(2,1)S(1)}, u32[]{:S(2)}, u32[]{:S(2)}) collective-permute-start(bf16[1,72,2,1440]{3,2,1,0:T(2,128)(2,1)} %own_ref.1), channel_id=1, source_target_pairs={{4,8},{12,16},{20,24},{8,4},{16,12},{24,20},{5,9},{13,17},{21,25},... | collective-permute-start | bytes 1244168 | tf_op jit(solution)/shard_map/ppermute | solution.py:326
  17.4 5.3 %collective-permute-start.4 = (bf16[72,720]{1,0:T(8,128)(2,1)S(1)}, bf16[72,720]{1,0:T(8,128)(2,1)S(1)}, u32[]{:S(2)}, u32[]{:S(2)}) collective-permute-start(bf16[72,720]{1,0:T(8,128)(2,1)S(1)} %convert_element_type.48.refs_0_), channel_id=1, source_target_pairs={{0,2},{2,0},{1,3},{3,1},{4,6},{6,4},{5,7},{7,5},{8,10},{10,8},{9,1... | collective-permute-start | bytes 311048 | tf_op jit(solution)/shard_map/ppermute | solution.py:312
  22.7 3.6 %collective-permute-start.3 = (bf16[72,720]{1,0:T(8,128)(2,1)S(1)}, bf16[72,720]{1,0:T(8,128)(2,1)S(1)}, u32[]{:S(2)}, u32[]{:S(2)}) collective-permute-start(bf16[72,720]{1,0:T(8,128)(2,1)S(1)} %convert_element_type.48.refs_0_), channel_id=1, source_target_pairs={{0,1},{1,0},{2,3},{3,2},{4,5},{5,4},{6,7},{7,6},{8,9},{9,8},{10,11... | collective-permute-start | bytes 311048 | tf_op jit(solution)/shard_map/ppermute | solution.py:312
  22.7 3.6 %collective-permute-start.5 = (bf16[72,720]{1,0:T(8,128)(2,1)S(1)}, bf16[72,720]{1,0:T(8,128)(2,1)S(1)}, u32[]{:S(2)}, u32[]{:S(2)}) collective-permute-start(bf16[72,720]{1,0:T(8,128)(2,1)S(1)} %collective-permute-done.4.refs_2_), channel_id=1, source_target_pairs={{0,1},{1,0},{2,3},{3,2},{4,5},{5,4},{6,7},{7,6},{8,9},{9,8},{10,11... | collective-permute-start | bytes 311048 | tf_op jit(solution)/shard_map/ppermute | solution.py:312
  23.2 1.0 %copy-start = (bf16[1,72,2,1440]{3,2,1,0:T(2,128)(2,1)S(1)}, bf16[1,72,2,1440]{3,2,1,0:T(2,128)(2,1)}, u32[]{:S(2)}) copy-start(bf16[1,72,2,1440]{3,2,1,0:T(2,128)(2,1)} %x_ref.1) | copy-start | bytes 1244164
  24.2 0.7 copy-start.1
  25.3 2.4 %copy-start.2 = (bf16[1,72,2,1440]{3,2,1,0:T(2,128)(2,1)S(1)}, bf16[1,72,2,1440]{3,2,1,0:T(2,128)(2,1)}, u32[]{:S(2)}) copy-start(bf16[1,72,2,1440]{3,2,1,0:T(2,128)(2,1)} %own_ref.1) | copy-start | bytes 1244164
  35.7 33.9 %copy-start.3 = (bf16[5,5,72,72]{3,2,1,0:T(8,128)(2,1)S(1)}, bf16[5,5,72,72]{3,2,1,0:T(8,128)(2,1)}, u32[]{:S(2)}) copy-start(bf16[5,5,72,72]{3,2,1,0:T(8,128)(2,1)} %param.9) | copy-start | bytes 777604
  36.8 1.4 %collective-permute-start.10 = (bf16[192,384]{1,0:T(8,128)(2,1)S(1)}, bf16[192,384]{1,0:T(8,128)(2,1)S(1)}, u32[]{:S(2)}, u32[]{:S(2)}) collective-permute-start(bf16[192,384]{1,0:T(8,128)(2,1)S(1)} %get-tuple-element.13), channel_id=1, source_target_pairs={{0,1},{1,0},{2,3},{3,2},{4,5},{5,4},{6,7},{7,6},{8,9},{9,8},{10,11... | collective-permute-start | bytes 442376 | tf_op jit(solution)/shard_map/ppermute | solution.py:312
  38.3 5.1 %collective-permute-start.11 = (bf16[96,384]{1,0:T(8,128)(2,1)S(1)}, bf16[96,384]{1,0:T(8,128)(2,1)S(1)}, u32[]{:S(2)}, u32[]{:S(2)}) collective-permute-start(bf16[96,384]{1,0:T(8,128)(2,1)S(1)} %constant_dynamic-slice_fusion), channel_id=1, source_target_pairs={{0,8},{4,12},{8,0},{12,4},{16,24},{20,28},{24,16},{28,20},{1,9},{5... | collective-permute-start | bytes 221192 | tf_op jit(solution)/shard_map/ppermute | solution.py:312
  43.4 5.5 %collective-permute-start.12 = (bf16[96,384]{1,0:T(8,128)(2,1)S(1)}, bf16[96,384]{1,0:T(8,128)(2,1)S(1)}, u32[]{:S(2)}, u32[]{:S(2)}) collective-permute-start(bf16[96,384]{1,0:T(8,128)(2,1)S(1)} %add_convert_fusion.4), channel_id=1, source_target_pairs={{0,16},{4,20},{8,24},{12,28},{16,0},{20,4},{24,8},{28,12},{1,17},{... | collective-permute-start | bytes 221192 | tf_op jit(solution)/shard_map/ppermute | solution.py:312
  46.3 11.6 %collective-permute-start.6 = (bf16[2,72,1536]{2,1,0:T(8,128)(2,1)S(1)}, bf16[2,72,1536]{2,1,0:T(8,128)(2,1)S(1)}, u32[]{:S(2)}, u32[]{:S(2)}) collective-permute-start(bf16[2,72,1536]{2,1,0:T(8,128)(2,1)S(1)} %shard_map.70.own_ref.g_ref), channel_id=1, source_target_pairs={{0,4},{4,0},{8,12},{12,8},{16,20},{20,16},{24,28},{28,24},{1,5},{5... | collective-permute-start | bytes 1327112 | tf_op jit(solution)/shard_map/ppermute | solution.py:312
  48.9 4.4 %collective-permute-start.13 = (bf16[96,384]{1,0:T(8,128)(2,1)S(1)}, bf16[96,384]{1,0:T(8,128)(2,1)S(1)}, u32[]{:S(2)}, u32[]{:S(2)}) collective-permute-start(bf16[96,384]{1,0:T(8,128)(2,1)S(1)} %add_convert_fusion.3), channel_id=1, source_target_pairs={{0,2},{2,0},{1,3},{3,1},{4,6},{6,4},{5,7},{7,5},{8,10},{10,8},{9,1... | collective-permute-start | bytes 221192 | tf_op jit(solution)/shard_map/ppermute | solution.py:312
  53.4 8.0 %collective-permute-start.14 = (bf16[96,384]{1,0:T(8,128)(2,1)S(1)}, bf16[96,384]{1,0:T(8,128)(2,1)S(1)}, u32[]{:S(2)}, u32[]{:S(2)}) collective-permute-start(bf16[96,384]{1,0:T(8,128)(2,1)S(1)} %add_convert_fusion.2), channel_id=1, source_target_pairs={{0,4},{4,0},{8,12},{12,8},{16,20},{20,16},{24,28},{28,24},{1,5},{5... | collective-permute-start | bytes 221192 | tf_op jit(solution)/shard_map/ppermute | solution.py:312
  57.8 14.4 %collective-permute-start.7 = (bf16[2,72,1536]{2,1,0:T(8,128)(2,1)S(1)}, bf16[2,72,1536]{2,1,0:T(8,128)(2,1)S(1)}, u32[]{:S(2)}, u32[]{:S(2)}) collective-permute-start(bf16[2,72,1536]{2,1,0:T(8,128)(2,1)S(1)} %collective-permute-done.6.near_ref), channel_id=1, source_target_pairs={{0,8},{8,16},{16,24},{12,4},{20,12},{28,20},{1,9},{9,17},{17,25},{... | collective-permute-start | bytes 1327112 | tf_op jit(solution)/shard_map/ppermute | solution.py:319
  61.4 8.2 %collective-permute-start.15 = (bf16[96,384]{1,0:T(8,128)(2,1)S(1)}, bf16[96,384]{1,0:T(8,128)(2,1)S(1)}, u32[]{:S(2)}, u32[]{:S(2)}) collective-permute-start(bf16[96,384]{1,0:T(8,128)(2,1)S(1)} %add_convert_fusion.1.refs_0_), channel_id=1, source_target_pairs={{0,8},{4,12},{8,0},{12,4},{16,24},{20,28},{24,16},{28,20},{1,9},{5... | collective-permute-start | bytes 221192 | tf_op jit(solution)/shard_map/ppermute | solution.py:312
  61.5 8.6 %collective-permute-start.17 = (bf16[96,384]{1,0:T(8,128)(2,1)S(1)}, bf16[96,384]{1,0:T(8,128)(2,1)S(1)}, u32[]{:S(2)}, u32[]{:S(2)}) collective-permute-start(bf16[96,384]{1,0:T(8,128)(2,1)S(1)} %add_convert_fusion.1.refs_0_), channel_id=1, source_target_pairs={{0,1},{1,0},{2,3},{3,2},{4,5},{5,4},{6,7},{7,6},{8,9},{9,8},{10,11... | collective-permute-start | bytes 221192 | tf_op jit(solution)/shard_map/ppermute | solution.py:312
  69.5 1.8 %collective-permute-start.16 = (bf16[96,384]{1,0:T(8,128)(2,1)S(1)}, bf16[96,384]{1,0:T(8,128)(2,1)S(1)}, u32[]{:S(2)}, u32[]{:S(2)}) collective-permute-start(bf16[96,384]{1,0:T(8,128)(2,1)S(1)} %collective-permute-done.15.refs_1_), channel_id=1, source_target_pairs={{0,1},{1,0},{2,3},{3,2},{4,5},{5,4},{6,7},{7,6},{8,9},{9,8},{10,11... | collective-permute-start | bytes 221192 | tf_op jit(solution)/shard_map/ppermute | solution.py:312

commit v8 on v6

--- a/solution.py
+++ b/solution.py
@@ -101,19 +101,16 @@
     return x.reshape(x.shape[0] // 8, 8, x.shape[1])
 
 
-def pair_kernel(rows, begun, s_ref, own_ref, *refs):
+def pair_kernel(rows, s_ref, own_ref, *refs):
     *others, o_ref, mix_scr = refs
-    sum_ref = others.pop() if begun else None
     for d, other in enumerate(others):
         mix_scr[d] = mixed(other)
     for low, high in tiles(mix_scr.shape[2]):
         sq = blocks(s_ref[:, : high - low])
         own = blocks(own_ref[:, low:high].astype(F32))
-        self_inverse = 0.0 if begun else 1.0 / jnp.sqrt(smoothing)
+        self_inverse = 1.0 / jnp.sqrt(smoothing)
         total = jnp.full(own.shape[1:], self_inverse, F32)
         mixture = own * self_inverse
-        if begun:
-            mixture = mixture - blocks(sum_ref[:, low:high])
         for d in range(len(others)):
             other = blocks(mix_scr[d, :, low:high].astype(F32))
             diff = own - other
@@ -346,13 +343,13 @@
     x = halve(x, *core)
     x = halve(x, *first)
     rest = [("space", b) for b in bits("space")[2:]]
-    rest += [("chip", b) for b in bits("chip")] + [("space", 1)]
+    rest += [("space", 1)] + [("chip", b) for b in bits("chip")]
     for axis in rest:
         x = add(x, flip(x, *axis))
     y = flip(x, *first)
     x_other = flip(x, *core)
     y_other = flip(y, *core)
-    return (x, y), (x_other, y_other)
+    return (x, y, x_other), (y_other,)
 
 
 def body(prediction_maps, truth_analysis, reciprocal_spread, deconv_inputs, filter_tensor):
@@ -391,27 +388,20 @@
         ],
         anywhere=[0, 1],
     )
-    taps = jnp.transpose(filter_tensor, (1, 2, 0, 3)).reshape(
-        ksize * channels, ksize * channels
-    )
+    taps = jnp.transpose(filter_tensor, (1, 2, 0, 3)).reshape(ksize * channels, ksize * channels)
     arrived, seen = [], []
     for i, (x, t) in enumerate(zip(fields, truths)):
         arrived += [x, core(x)] if i else [core(x)]
         seen += [t, core(t)]
 
     table = [float(v) for v in area_weights(rows_total)]
-
-    def pairs(others, so_far):
-        return call(
-            functools.partial(pair_kernel, rows, bool(so_far)),
-            [sds((mix, width), F32)],
-            [scale, own, *others, *so_far],
-            [pltpu.VMEM((len(others), mix, width), BF)],
-            spare=max(3, members) << 20,
-        )[0]
-
-    paired = pairs(arrived[:-1], ())
-    paired = pairs(arrived[-1:], (paired,))
+    paired = call(
+        functools.partial(pair_kernel, rows),
+        [sds((mix, width), F32)],
+        [scale, own, *arrived],
+        [pltpu.VMEM((members - 1, mix, width), BF)],
+        spare=max(3, members) << 20,
+    )[0]
     grad = call(
         functools.partial(energy_kernel, span, members, table),
         [slab],
@@ -473,8 +463,8 @@
             aliases={count: 0} if len(xs) > count else {},
         )[0]
 
-    grad_kernel = finish([(0, 0), (0, 1)], *early)
-    grad_kernel = finish([(1, 0), (1, 1)], *late, grad_kernel)
+    grad_kernel = finish([(0, 0), (0, 1), (1, 0)], *early)
+    grad_kernel = finish([(1, 1)], *late, grad_kernel)
     return (grad_hidden, grad_kernel)
 
 

time: 74.9 us -> 77.8 us (1.039)
  waiting for transfers between devices: 39.5 us -> 41.8 us
  starting transfers between devices: 21.3 us -> 22.1 us
    ppermute x16, waiting for transfers between devices: 39.5 us -> 41.8 us  [flip(): return lax.ppermute(x, axis, [(i, i ^ bit) for i in range(size)])]
    ppermute x16, starting transfers between devices: 17.1 us -> 17.9 us  [flip(): return lax.ppermute(x, axis, [(i, i ^ bit) for i in range(size)])]
    pallas_call x9 -> x8, Pallas kernels: 9.65 us -> 9.44 us  [call(): pl.pallas_call(kernel, out_shape=list(outs), in_specs=[ANY if i in anywhe...]
  transfers between devices with their start and end apart: 18 -> 18, of which waited for: 9 -> 8; matrix products, arithmetic and copies ran while one was open for 2% -> 2% of each run, Pallas kernels for 8% -> 8%
where the time goes in v8:
time: 77.8 us; the launch traced here: 77.6 us
  waiting for transfers between devices  41.8 us (54%)
  starting transfers between devices  22.1 us (28%)
  Pallas kernels  9.44 us (12%)
  local copies, waits for them, and re-layouts  2.23 us (3%)
  other arithmetic  1.09 us (1%)
  between operations  0.87 us (1%)
    ppermute x16, waiting for transfers between devices, flip(): return lax.ppermute(x, axis, [(i, i ^ bit) for i in range(size)])  41.8 us
    ppermute x16, starting transfers between devices, flip(): return lax.ppermute(x, axis, [(i, i ^ bit) for i in range(size)])  17.9 us
    pallas_call x8, Pallas kernels, call(): pl.pallas_call(kernel, out_shape=list(outs), in_specs=[ANY if i in anywhe...  9.44 us
    ppermute x1, starting transfers between devices, along(): return lax.ppermute(x, 'space', pairs)  3.5 us
    unnamed x8, local copies, waits for them, and re-layouts  1.68 us
  transfers between devices with their start and end apart: 18, of which 8 were waited for; matrix products, arithmetic and copies ran while one was open for 2% of the time, Pallas kernels for 8%

profile of v8, /device:TPU:0, one launch (start us, length us, event | category | flops | bytes accessed | tf_op | source)
XLA Modules:
  0.0 77.6 jit_solution(14320997938206781427)
XLA Ops:
  0.6 3.1 %collective-permute-start.1 = (bf16[1,72,2,1440]{3,2,1,0:T(2,128)(2,1)}, bf16[1,72,2,1440]{3,2,1,0:T(2,128)(2,1)S(1)}, u32[]{:S(2)}, u32[]{:S(2)}) collective-permute-start(bf16[1,72,2,1440]{3,2,1,0:T(2,128)(2,1)} %x_ref.1), channel_id=1, source_target_pairs={{0,2},{2,0},{1,3},{3,1},{4,6},{6,4},{5,7},{7,5},{8,10},{10,8},{9,1... | collective-permute-start | bytes 1244168 | tf_op jit(solution)/shard_map/ppermute | solution.py:301
  3.7 0.0 collective-permute-start
  3.7 10.4 %collective-permute-done.1.refs_1_ = bf16[1,72,2,1440]{3,2,1,0:T(2,128)(2,1)S(1)} collective-permute-done((bf16[1,72,2,1440]{3,2,1,0:T(2,128)(2,1)}, bf16[1,72,2,1440]{3,2,1,0:T(2,128)(2,1)S(1)}, u32[]{:S(2)}, u32[]{:S(2)}) %collective-permute-start.1) | collective-permute-done | bytes 414752 | tf_op jit(solution)/shard_map/ppermute | solution.py:301
  14.1 0.0 collective-permute-start.2
  14.1 1.7 %collective-permute-start.8 = (bf16[1,72,2,1440]{3,2,1,0:T(2,128)(2,1)}, bf16[1,72,2,1440]{3,2,1,0:T(2,128)(2,1)S(1)}, u32[]{:S(2)}, u32[]{:S(2)}) collective-permute-start(bf16[1,72,2,1440]{3,2,1,0:T(2,128)(2,1)} %own_ref.1), channel_id=1, source_target_pairs={{0,4},{4,0},{8,12},{12,8},{16,20},{20,16},{24,28},{28,24},{1,5},{5... | collective-permute-start | bytes 1244168 | tf_op jit(solution)/shard_map/ppermute | solution.py:301
  15.8 0.7 collective-permute-start.9
  16.5 0.9 %convert_element_type.48.refs_0_ = bf16[72,720]{1,0:T(8,128)(2,1)S(1)} convert(f32[72,720]{1,0:T(8,128)} %param.6) | non-fusion elementwise | flops 51840 | bytes 311040 | tf_op jit(solution)/shard_map/convert_element_type | solution.py:377
  17.4 1.6 %collective-permute-start.4 = (bf16[72,720]{1,0:T(8,128)(2,1)S(1)}, bf16[72,720]{1,0:T(8,128)(2,1)S(1)}, u32[]{:S(2)}, u32[]{:S(2)}) collective-permute-start(bf16[72,720]{1,0:T(8,128)(2,1)S(1)} %convert_element_type.48.refs_0_), channel_id=1, source_target_pairs={{0,2},{2,0},{1,3},{3,1},{4,6},{6,4},{5,7},{7,5},{8,10},{10,8},{9,1... | collective-permute-start | bytes 311048 | tf_op jit(solution)/shard_map/ppermute | solution.py:301
  19.0 3.7 %collective-permute-done.4.refs_2_ = bf16[72,720]{1,0:T(8,128)(2,1)S(1)} collective-permute-done((bf16[72,720]{1,0:T(8,128)(2,1)S(1)}, bf16[72,720]{1,0:T(8,128)(2,1)S(1)}, u32[]{:S(2)}, u32[]{:S(2)}) %collective-permute-start.4) | collective-permute-done | bytes 103712 | tf_op jit(solution)/shard_map/ppermute | solution.py:301
  22.7 0.0 collective-permute-start.3
  22.7 0.0 collective-permute-done.refs_0_
  22.7 0.5 collective-permute-start.5
  23.2 0.0 copy-start
  23.2 1.0 %copy-done = bf16[1,72,2,1440]{3,2,1,0:T(2,128)(2,1)S(1)} copy-done((bf16[1,72,2,1440]{3,2,1,0:T(2,128)(2,1)S(1)}, bf16[1,72,2,1440]{3,2,1,0:T(2,128)(2,1)}, u32[]{:S(2)}) %copy-start) | copy-done | bytes 414744
  24.2 0.0 copy-start.1
  24.2 0.7 copy-done.1
  24.9 0.4 shard_map.68
  25.3 0.0 collective-permute-done.2.refs_2_
  25.3 0.0 copy-start.2
  25.3 1.0 %shard_map.69.pair_ref = f32[144,1440]{1,0:T(8,128)S(1)} custom-call(f32[144,128]{1,0:T(8,128)S(1)} %get-tuple-element.6.s_ref, bf16[144,1440]{1,0:T(8,128)(2,1)S(1)} %get-tuple-element.7.own_ref, bf16[1,72,2,1440]{3,2,1,0:T(2,128)(2,1)S(1)} %collective-permute-done.refs_0_, bf16[1,72,2,1440]{3,2,1,0:T(2,128)(2,1)S(1)} %collective-permute-done.1.refs_1_, ...), custom_call_target="tpu_custom_call" | custom-call | bytes 2562048 | tf_op jit(solution)/shard_map/pallas_call | solution.py:39
  26.3 0.0 collective-permute-done.3.refs_1_
  26.3 0.0 collective-permute-done.5.refs_3_
  26.3 1.4 %shard_map.70.own_ref.g_ref = bf16[2,72,1536]{2,1,0:T(8,128)(2,1)S(1)} custom-call(f32[144,128]{1,0:T(8,128)S(1)} %get-tuple-element.6.s_ref, bf16[144,1440]{1,0:T(8,128)(2,1)S(1)} %get-tuple-element.7.own_ref, f32[144,1440]{1,0:T(8,128)S(1)} %shard_map.69.pair_ref, bf16[72,720]{1,0:T(8,128)(2,1)S(1)} %convert_element_type.48.refs_0_, ...), custom_call_target="tpu_custom_call" | custom-call | bytes 2174976 | tf_op jit(solution)/shard_map/pallas_call | solution.py:39
  27.7 0.0 copy-done.2
  27.7 1.1 %shard_map.72 = (bf16[2,384,1536]{2,1,0:T(8,128)(2,1)S(1)}, f32[144,768]{1,0:T(8,128)S(1)}) custom-call(bf16[2,72,1536]{2,1,0:T(8,128)(2,1)S(1)} %shard_map.70.own_ref.g_ref, bf16[1,72,2,1440]{3,2,1,0:T(2,128)(2,1)S(1)} %copy-done.2), custom_call_target="tpu_custom_call" | custom-call | flops 265420800 | bytes 3658752 | tf_op jit(solution)/shard_map/pallas_call | solution.py:39
  28.8 6.8 %collective-permute-done.8.near_ref = bf16[1,72,2,1440]{3,2,1,0:T(2,128)(2,1)S(1)} collective-permute-done((bf16[1,72,2,1440]{3,2,1,0:T(2,128)(2,1)}, bf16[1,72,2,1440]{3,2,1,0:T(2,128)(2,1)S(1)}, u32[]{:S(2)}, u32[]{:S(2)}) %collective-permute-start.8) | collective-permute-done | bytes 414752 | tf_op jit(solution)/shard_map/ppermute | solution.py:301
  35.7 0.0 collective-permute-done.9.far_ref
  35.7 0.0 copy-start.3
  35.7 1.0 %shard_map.73 = bf16[384,384]{1,0:T(8,128)(2,1)S(1)} custom-call(bf16[2,384,1536]{2,1,0:T(8,128)(2,1)S(1)} %get-tuple-element.8.shift_ref, f32[144,768]{1,0:T(8,128)S(1)} %get-tuple-element.9.own_ref, bf16[1,72,2,1440]{3,2,1,0:T(2,128)(2,1)S(1)} %collective-permute-done.8.near_ref, bf16[1,72,2,1440]{3,2,1,0:T(2,128)(2,1)S(1)} %collective-permute-done.9.far_ref), custom_call_target="tpu_custom_call" | custom-call | flops 530841600 | bytes 3926016 | tf_op jit(solution)/shard_map/pallas_call | solution.py:39
  36.7 0.1 collective-permute-start.10
  36.8 1.3 %collective-permute-done.10 = bf16[192,384]{1,0:T(8,128)(2,1)S(1)} collective-permute-done((bf16[192,384]{1,0:T(8,128)(2,1)S(1)}, bf16[192,384]{1,0:T(8,128)(2,1)S(1)}, u32[]{:S(2)}, u32[]{:S(2)}) %collective-permute-start.10) | collective-permute-done | bytes 147488 | tf_op jit(solution)/shard_map/ppermute | solution.py:301
  38.2 0.1 add_convert_fusion
  38.3 2.5 %collective-permute-start.11 = (bf16[96,384]{1,0:T(8,128)(2,1)S(1)}, bf16[96,384]{1,0:T(8,128)(2,1)S(1)}, u32[]{:S(2)}, u32[]{:S(2)}) collective-permute-start(bf16[96,384]{1,0:T(8,128)(2,1)S(1)} %constant_dynamic-slice_fusion), channel_id=1, source_target_pairs={{0,8},{4,12},{8,0},{12,4},{16,24},{20,28},{24,16},{28,20},{1,9},{5... | collective-permute-start | bytes 221192 | tf_op jit(solution)/shard_map/ppermute | solution.py:301
  40.8 2.6 %collective-permute-done.11 = bf16[96,384]{1,0:T(8,128)(2,1)S(1)} collective-permute-done((bf16[96,384]{1,0:T(8,128)(2,1)S(1)}, bf16[96,384]{1,0:T(8,128)(2,1)S(1)}, u32[]{:S(2)}, u32[]{:S(2)}) %collective-permute-start.11) | collective-permute-done | bytes 73760 | tf_op jit(solution)/shard_map/ppermute | solution.py:301
  43.4 2.9 %collective-permute-start.12 = (bf16[96,384]{1,0:T(8,128)(2,1)S(1)}, bf16[96,384]{1,0:T(8,128)(2,1)S(1)}, u32[]{:S(2)}, u32[]{:S(2)}) collective-permute-start(bf16[96,384]{1,0:T(8,128)(2,1)S(1)} %add_convert_fusion.4), channel_id=1, source_target_pairs={{0,16},{4,20},{8,24},{12,28},{16,0},{20,4},{24,8},{28,12},{1,17},{... | collective-permute-start | bytes 221192 | tf_op jit(solution)/shard_map/ppermute | solution.py:301
  46.3 1.5 %collective-permute-start.6 = (bf16[2,72,1536]{2,1,0:T(8,128)(2,1)S(1)}, bf16[2,72,1536]{2,1,0:T(8,128)(2,1)S(1)}, u32[]{:S(2)}, u32[]{:S(2)}) collective-permute-start(bf16[2,72,1536]{2,1,0:T(8,128)(2,1)S(1)} %shard_map.70.own_ref.g_ref), channel_id=1, source_target_pairs={{0,4},{4,0},{8,12},{12,8},{16,20},{20,16},{24,28},{28,24},{1,5},{5... | collective-permute-start | bytes 1327112 | tf_op jit(solution)/shard_map/ppermute | solution.py:301
  47.7 1.2 %collective-permute-done.12 = bf16[96,384]{1,0:T(8,128)(2,1)S(1)} collective-permute-done((bf16[96,384]{1,0:T(8,128)(2,1)S(1)}, bf16[96,384]{1,0:T(8,128)(2,1)S(1)}, u32[]{:S(2)}, u32[]{:S(2)}) %collective-permute-start.12) | collective-permute-done | bytes 73760 | tf_op jit(solution)/shard_map/ppermute | solution.py:301
  48.9 1.6 %collective-permute-start.13 = (bf16[96,384]{1,0:T(8,128)(2,1)S(1)}, bf16[96,384]{1,0:T(8,128)(2,1)S(1)}, u32[]{:S(2)}, u32[]{:S(2)}) collective-permute-start(bf16[96,384]{1,0:T(8,128)(2,1)S(1)} %add_convert_fusion.3), channel_id=1, source_target_pairs={{0,4},{4,0},{8,12},{12,8},{16,20},{20,16},{24,28},{28,24},{1,5},{5... | collective-permute-start | bytes 221192 | tf_op jit(solution)/shard_map/ppermute | solution.py:301
  50.5 8.1 %collective-permute-done.13 = bf16[96,384]{1,0:T(8,128)(2,1)S(1)} collective-permute-done((bf16[96,384]{1,0:T(8,128)(2,1)S(1)}, bf16[96,384]{1,0:T(8,128)(2,1)S(1)}, u32[]{:S(2)}, u32[]{:S(2)}) %collective-permute-start.13) | collective-permute-done | bytes 73760 | tf_op jit(solution)/shard_map/ppermute | solution.py:301
  58.6 1.6 %collective-permute-start.14 = (bf16[96,384]{1,0:T(8,128)(2,1)S(1)}, bf16[96,384]{1,0:T(8,128)(2,1)S(1)}, u32[]{:S(2)}, u32[]{:S(2)}) collective-permute-start(bf16[96,384]{1,0:T(8,128)(2,1)S(1)} %add_convert_fusion.2), channel_id=1, source_target_pairs={{0,2},{2,0},{1,3},{3,1},{4,6},{6,4},{5,7},{7,5},{8,10},{10,8},{9,1... | collective-permute-start | bytes 221192 | tf_op jit(solution)/shard_map/ppermute | solution.py:301
  60.2 0.0 collective-permute-done.6.near_ref
  60.2 3.5 %collective-permute-start.7 = (bf16[2,72,1536]{2,1,0:T(8,128)(2,1)S(1)}, bf16[2,72,1536]{2,1,0:T(8,128)(2,1)S(1)}, u32[]{:S(2)}, u32[]{:S(2)}) collective-permute-start(bf16[2,72,1536]{2,1,0:T(8,128)(2,1)S(1)} %collective-permute-done.6.near_ref), channel_id=1, source_target_pairs={{0,8},{8,16},{16,24},{12,4},{20,12},{28,20},{1,9},{9,17},{17,25},{... | collective-permute-start | bytes 1327112 | tf_op jit(solution)/shard_map/ppermute | solution.py:308
  63.7 0.0 collective-permute-done.14
  63.8 1.0 %collective-permute-start.15 = (bf16[96,384]{1,0:T(8,128)(2,1)S(1)}, bf16[96,384]{1,0:T(8,128)(2,1)S(1)}, u32[]{:S(2)}, u32[]{:S(2)}) collective-permute-start(bf16[96,384]{1,0:T(8,128)(2,1)S(1)} %add_convert_fusion.1.refs_0_), channel_id=1, source_target_pairs={{0,8},{4,12},{8,0},{12,4},{16,24},{20,28},{24,16},{28,20},{1,9},{5... | collective-permute-start | bytes 221192 | tf_op jit(solution)/shard_map/ppermute | solution.py:301
  64.7 0.0 collective-permute-start.17
  64.7 7.7 %collective-permute-done.15.refs_1_ = bf16[96,384]{1,0:T(8,128)(2,1)S(1)} collective-permute-done((bf16[96,384]{1,0:T(8,128)(2,1)S(1)}, bf16[96,384]{1,0:T(8,128)(2,1)S(1)}, u32[]{:S(2)}, u32[]{:S(2)}) %collective-permute-start.15) | collective-permute-done | bytes 73760 | tf_op jit(solution)/shard_map/ppermute | solution.py:301
  72.4 0.0 collective-permute-start.16
  72.5 0.0 copy-done.3
  72.5 0.1 copy.9
  72.6 0.4 reshape.7.w_ref
  73.0 0.0 collective-permute-done.17.refs_2_
  73.0 1.2 %shard_map.74.refs_1_ = f32[5,5,72,72]{3,2,1,0:T(8,128)} custom-call(bf16[96,384]{1,0:T(8,128)(2,1)S(1)} %add_convert_fusion.1.refs_0_, bf16[96,384]{1,0:T(8,128)(2,1)S(1)} %collective-permute-done.15.refs_1_, bf16[96,384]{1,0:T(8,128)(2,1)S(1)} %collective-permute-done.17.refs_2_), custom_call_target="tpu_custom_call" | custom-call | bytes 739584 | tf_op jit(solution)/shard_map/pallas_call | solution.py:39
  74.2 0.0 collective-permute-done.16.refs_0_
  74.3 0.9 %shard_map.75 = f32[5,5,72,72]{3,2,1,0:T(8,128)} custom-call(bf16[96,384]{1,0:T(8,128)(2,1)S(1)} %collective-permute-done.16.refs_0_, f32[5,5,72,72]{3,2,1,0:T(8,128)} %shard_map.74.refs_1_), custom_call_target="tpu_custom_call", output_to_operand_aliasing={{}: (1, {})} | custom-call | bytes 1110528 | tf_op jit(solution)/shard_map/pallas_call | solution.py:39
  75.1 0.0 collective-permute-done.7.far_ref
  75.1 2.4 %shard_map.71 = bf16[1,72,2,1440]{3,2,1,0:T(2,128)(2,1)} custom-call(bf16[360,360]{1,0:T(8,128)(2,1)S(1)} %reshape.7.w_ref, bf16[2,72,1536]{2,1,0:T(8,128)(2,1)S(1)} %shard_map.70.own_ref.g_ref, bf16[2,72,1536]{2,1,0:T(8,128)(2,1)S(1)} %collective-permute-done.6.near_ref, bf16[2,72,1536]{2,1,0:T(8,128)(2,1)S(1)} %collective-permute-done.7.far_ref), custom_call_target="tpu_custom_call" | custom-call | flops 796262400 | bytes 2001024 | tf_op jit(solution)/shard_map/pallas_call | solution.py:39
  (6 shorter events, 0.1 us)
Async XLA Ops:
  0.6 13.4 %collective-permute-start.1 = (bf16[1,72,2,1440]{3,2,1,0:T(2,128)(2,1)}, bf16[1,72,2,1440]{3,2,1,0:T(2,128)(2,1)S(1)}, u32[]{:S(2)}, u32[]{:S(2)}) collective-permute-start(bf16[1,72,2,1440]{3,2,1,0:T(2,128)(2,1)} %x_ref.1), channel_id=1, source_target_pairs={{0,2},{2,0},{1,3},{3,1},{4,6},{6,4},{5,7},{7,5},{8,10},{10,8},{9,1... | collective-permute-start | bytes 1244168 | tf_op jit(solution)/shard_map/ppermute | solution.py:301
  3.7 19.0 %collective-permute-start = (bf16[1,72,2,1440]{3,2,1,0:T(2,128)(2,1)}, bf16[1,72,2,1440]{3,2,1,0:T(2,128)(2,1)S(1)}, u32[]{:S(2)}, u32[]{:S(2)}) collective-permute-start(bf16[1,72,2,1440]{3,2,1,0:T(2,128)(2,1)} %x_ref.1), channel_id=1, source_target_pairs={{0,1},{1,0},{2,3},{3,2},{4,5},{5,4},{6,7},{7,6},{8,9},{9,8},{10,11... | collective-permute-start | bytes 1244168 | tf_op jit(solution)/shard_map/ppermute | solution.py:301
  14.1 11.2 %collective-permute-start.2 = (bf16[1,72,2,1440]{3,2,1,0:T(2,128)(2,1)S(1)}, bf16[1,72,2,1440]{3,2,1,0:T(2,128)(2,1)S(1)}, u32[]{:S(2)}, u32[]{:S(2)}) collective-permute-start(bf16[1,72,2,1440]{3,2,1,0:T(2,128)(2,1)S(1)} %collective-permute-done.1.refs_1_), channel_id=1, source_target_pairs={{0,1},{1,0},{2,3},{3,2},{4,5},{5,4},{6,7},{7,6},{8,9},{9,8},{10,11... | collective-permute-start | bytes 1244168 | tf_op jit(solution)/shard_map/ppermute | solution.py:301
  14.1 21.6 %collective-permute-start.8 = (bf16[1,72,2,1440]{3,2,1,0:T(2,128)(2,1)}, bf16[1,72,2,1440]{3,2,1,0:T(2,128)(2,1)S(1)}, u32[]{:S(2)}, u32[]{:S(2)}) collective-permute-start(bf16[1,72,2,1440]{3,2,1,0:T(2,128)(2,1)} %own_ref.1), channel_id=1, source_target_pairs={{0,4},{4,0},{8,12},{12,8},{16,20},{20,16},{24,28},{28,24},{1,5},{5... | collective-permute-start | bytes 1244168 | tf_op jit(solution)/shard_map/ppermute | solution.py:301
  15.8 19.9 %collective-permute-start.9 = (bf16[1,72,2,1440]{3,2,1,0:T(2,128)(2,1)}, bf16[1,72,2,1440]{3,2,1,0:T(2,128)(2,1)S(1)}, u32[]{:S(2)}, u32[]{:S(2)}) collective-permute-start(bf16[1,72,2,1440]{3,2,1,0:T(2,128)(2,1)} %own_ref.1), channel_id=1, source_target_pairs={{4,8},{12,16},{20,24},{8,4},{16,12},{24,20},{5,9},{13,17},{21,25},... | collective-permute-start | bytes 1244168 | tf_op jit(solution)/shard_map/ppermute | solution.py:315
  17.4 5.3 %collective-permute-start.4 = (bf16[72,720]{1,0:T(8,128)(2,1)S(1)}, bf16[72,720]{1,0:T(8,128)(2,1)S(1)}, u32[]{:S(2)}, u32[]{:S(2)}) collective-permute-start(bf16[72,720]{1,0:T(8,128)(2,1)S(1)} %convert_element_type.48.refs_0_), channel_id=1, source_target_pairs={{0,2},{2,0},{1,3},{3,1},{4,6},{6,4},{5,7},{7,5},{8,10},{10,8},{9,1... | collective-permute-start | bytes 311048 | tf_op jit(solution)/shard_map/ppermute | solution.py:301
  22.7 3.6 %collective-permute-start.3 = (bf16[72,720]{1,0:T(8,128)(2,1)S(1)}, bf16[72,720]{1,0:T(8,128)(2,1)S(1)}, u32[]{:S(2)}, u32[]{:S(2)}) collective-permute-start(bf16[72,720]{1,0:T(8,128)(2,1)S(1)} %convert_element_type.48.refs_0_), channel_id=1, source_target_pairs={{0,1},{1,0},{2,3},{3,2},{4,5},{5,4},{6,7},{7,6},{8,9},{9,8},{10,11... | collective-permute-start | bytes 311048 | tf_op jit(solution)/shard_map/ppermute | solution.py:301
  22.7 3.6 %collective-permute-start.5 = (bf16[72,720]{1,0:T(8,128)(2,1)S(1)}, bf16[72,720]{1,0:T(8,128)(2,1)S(1)}, u32[]{:S(2)}, u32[]{:S(2)}) collective-permute-start(bf16[72,720]{1,0:T(8,128)(2,1)S(1)} %collective-permute-done.4.refs_2_), channel_id=1, source_target_pairs={{0,1},{1,0},{2,3},{3,2},{4,5},{5,4},{6,7},{7,6},{8,9},{9,8},{10,11... | collective-permute-start | bytes 311048 | tf_op jit(solution)/shard_map/ppermute | solution.py:301
  23.2 1.0 %copy-start = (bf16[1,72,2,1440]{3,2,1,0:T(2,128)(2,1)S(1)}, bf16[1,72,2,1440]{3,2,1,0:T(2,128)(2,1)}, u32[]{:S(2)}) copy-start(bf16[1,72,2,1440]{3,2,1,0:T(2,128)(2,1)} %x_ref.1) | copy-start | bytes 1244164
  24.2 0.7 copy-start.1
  25.3 2.4 %copy-start.2 = (bf16[1,72,2,1440]{3,2,1,0:T(2,128)(2,1)S(1)}, bf16[1,72,2,1440]{3,2,1,0:T(2,128)(2,1)}, u32[]{:S(2)}) copy-start(bf16[1,72,2,1440]{3,2,1,0:T(2,128)(2,1)} %own_ref.1) | copy-start | bytes 1244164
  35.7 36.8 %copy-start.3 = (bf16[5,5,72,72]{3,2,1,0:T(8,128)(2,1)S(1)}, bf16[5,5,72,72]{3,2,1,0:T(8,128)(2,1)}, u32[]{:S(2)}) copy-start(bf16[5,5,72,72]{3,2,1,0:T(8,128)(2,1)} %param.9) | copy-start | bytes 777604
  36.7 1.4 %collective-permute-start.10 = (bf16[192,384]{1,0:T(8,128)(2,1)S(1)}, bf16[192,384]{1,0:T(8,128)(2,1)S(1)}, u32[]{:S(2)}, u32[]{:S(2)}) collective-permute-start(bf16[192,384]{1,0:T(8,128)(2,1)S(1)} %constant_dynamic-slice_fusion.1), channel_id=1, source_target_pairs={{0,1},{1,0},{2,3},{3,2},{4,5},{5,4},{6,7},{7,6},{8,9},{9,8},{10,11... | collective-permute-start | bytes 442376 | tf_op jit(solution)/shard_map/ppermute | solution.py:301
  38.3 5.1 %collective-permute-start.11 = (bf16[96,384]{1,0:T(8,128)(2,1)S(1)}, bf16[96,384]{1,0:T(8,128)(2,1)S(1)}, u32[]{:S(2)}, u32[]{:S(2)}) collective-permute-start(bf16[96,384]{1,0:T(8,128)(2,1)S(1)} %constant_dynamic-slice_fusion), channel_id=1, source_target_pairs={{0,8},{4,12},{8,0},{12,4},{16,24},{20,28},{24,16},{28,20},{1,9},{5... | collective-permute-start | bytes 221192 | tf_op jit(solution)/shard_map/ppermute | solution.py:301
  43.4 5.5 %collective-permute-start.12 = (bf16[96,384]{1,0:T(8,128)(2,1)S(1)}, bf16[96,384]{1,0:T(8,128)(2,1)S(1)}, u32[]{:S(2)}, u32[]{:S(2)}) collective-permute-start(bf16[96,384]{1,0:T(8,128)(2,1)S(1)} %add_convert_fusion.4), channel_id=1, source_target_pairs={{0,16},{4,20},{8,24},{12,28},{16,0},{20,4},{24,8},{28,12},{1,17},{... | collective-permute-start | bytes 221192 | tf_op jit(solution)/shard_map/ppermute | solution.py:301
  46.3 14.0 %collective-permute-start.6 = (bf16[2,72,1536]{2,1,0:T(8,128)(2,1)S(1)}, bf16[2,72,1536]{2,1,0:T(8,128)(2,1)S(1)}, u32[]{:S(2)}, u32[]{:S(2)}) collective-permute-start(bf16[2,72,1536]{2,1,0:T(8,128)(2,1)S(1)} %shard_map.70.own_ref.g_ref), channel_id=1, source_target_pairs={{0,4},{4,0},{8,12},{12,8},{16,20},{20,16},{24,28},{28,24},{1,5},{5... | collective-permute-start | bytes 1327112 | tf_op jit(solution)/shard_map/ppermute | solution.py:301
  48.9 9.7 %collective-permute-start.13 = (bf16[96,384]{1,0:T(8,128)(2,1)S(1)}, bf16[96,384]{1,0:T(8,128)(2,1)S(1)}, u32[]{:S(2)}, u32[]{:S(2)}) collective-permute-start(bf16[96,384]{1,0:T(8,128)(2,1)S(1)} %add_convert_fusion.3), channel_id=1, source_target_pairs={{0,4},{4,0},{8,12},{12,8},{16,20},{20,16},{24,28},{28,24},{1,5},{5... | collective-permute-start | bytes 221192 | tf_op jit(solution)/shard_map/ppermute | solution.py:301
  58.6 5.1 %collective-permute-start.14 = (bf16[96,384]{1,0:T(8,128)(2,1)S(1)}, bf16[96,384]{1,0:T(8,128)(2,1)S(1)}, u32[]{:S(2)}, u32[]{:S(2)}) collective-permute-start(bf16[96,384]{1,0:T(8,128)(2,1)S(1)} %add_convert_fusion.2), channel_id=1, source_target_pairs={{0,2},{2,0},{1,3},{3,1},{4,6},{6,4},{5,7},{7,5},{8,10},{10,8},{9,1... | collective-permute-start | bytes 221192 | tf_op jit(solution)/shard_map/ppermute | solution.py:301
  60.2 14.9 %collective-permute-start.7 = (bf16[2,72,1536]{2,1,0:T(8,128)(2,1)S(1)}, bf16[2,72,1536]{2,1,0:T(8,128)(2,1)S(1)}, u32[]{:S(2)}, u32[]{:S(2)}) collective-permute-start(bf16[2,72,1536]{2,1,0:T(8,128)(2,1)S(1)} %collective-permute-done.6.near_ref), channel_id=1, source_target_pairs={{0,8},{8,16},{16,24},{12,4},{20,12},{28,20},{1,9},{9,17},{17,25},{... | collective-permute-start | bytes 1327112 | tf_op jit(solution)/shard_map/ppermute | solution.py:308
  63.8 8.7 %collective-permute-start.15 = (bf16[96,384]{1,0:T(8,128)(2,1)S(1)}, bf16[96,384]{1,0:T(8,128)(2,1)S(1)}, u32[]{:S(2)}, u32[]{:S(2)}) collective-permute-start(bf16[96,384]{1,0:T(8,128)(2,1)S(1)} %add_convert_fusion.1.refs_0_), channel_id=1, source_target_pairs={{0,8},{4,12},{8,0},{12,4},{16,24},{20,28},{24,16},{28,20},{1,9},{5... | collective-permute-start | bytes 221192 | tf_op jit(solution)/shard_map/ppermute | solution.py:301
  64.7 8.2 %collective-permute-start.17 = (bf16[96,384]{1,0:T(8,128)(2,1)S(1)}, bf16[96,384]{1,0:T(8,128)(2,1)S(1)}, u32[]{:S(2)}, u32[]{:S(2)}) collective-permute-start(bf16[96,384]{1,0:T(8,128)(2,1)S(1)} %add_convert_fusion.1.refs_0_), channel_id=1, source_target_pairs={{0,1},{1,0},{2,3},{3,2},{4,5},{5,4},{6,7},{7,6},{8,9},{9,8},{10,11... | collective-permute-start | bytes 221192 | tf_op jit(solution)/shard_map/ppermute | solution.py:301
  72.4 1.8 %collective-permute-start.16 = (bf16[96,384]{1,0:T(8,128)(2,1)S(1)}, bf16[96,384]{1,0:T(8,128)(2,1)S(1)}, u32[]{:S(2)}, u32[]{:S(2)}) collective-permute-start(bf16[96,384]{1,0:T(8,128)(2,1)S(1)} %collective-permute-done.15.refs_1_), channel_id=1, source_target_pairs={{0,1},{1,0},{2,3},{3,2},{4,5},{5,4},{6,7},{7,6},{8,9},{9,8},{10,11... | collective-permute-start | bytes 221192 | tf_op jit(solution)/shard_map/ppermute | solution.py:301
